TPU v7x, 32 devices: a whole 2x2x4 slice. The times are simulated.
32 devices in a mesh: member: 2 (over y), tile: 4 (over z), chan: 2 (over x), sub: 2 (over core).
Axes of the slice: x: 2, y: 2, z: 4, core: 2. Of those that a mesh axis runs over, the one named last changes fastest.
Arguments:
- obs_values: bfloat16 [131072, 64], P(('member', 'tile', 'chan', 'sub')), parts along dimension 0, may hold values from -6 to 6
- obs_weight: bfloat16 [131072], P(('member', 'tile', 'chan', 'sub')), parts along dimension 0, may hold values from 0.25 to 4
- obs_tile: int32 [131072], P(('member', 'tile', 'chan', 'sub')), parts along dimension 0, may hold values from 0 to 7, as said below
- obs_cell: int32 [131072], P(('member', 'tile', 'chan', 'sub')), parts along dimension 0, may hold values from 0 to 3071
- conv_one: bfloat16 [3, 3, 256, 64], P(None, None, 'chan'), may hold values from -0.25 to 0.25
- conv_two: bfloat16 [3, 3, 256, 256], P(None, None, 'chan'), may hold values from -0.125 to 0.125
- density_gain: float32 [256], P('chan'), may hold values from -2 to 2
- cotangent: bfloat16 [512, 32, 768], P(('member', 'chan'), 'tile', 'sub'), parts along dimension 0, may hold values from -6 to 6
Outputs:
- encoded: bfloat16 [512, 32, 768], P(('member', 'chan'), 'tile', 'sub'), parts along dimension 0
- grad_conv_one: float32 [6, 3, 256, 64], P('member', None, 'chan'), parts along dimension 0
- grad_conv_two: float32 [6, 3, 256, 256], P('member', None, 'chan'), parts along dimension 0
- grad_gain: float32 [512], P(('member', 'chan')), parts along dimension 0
There are 2 independent parts, one for each index of `member`. A program takes and returns all parts, laid end to end along the dimension named above; an argument that names none is the same for every part. Nothing has to cross between parts.
Inputs may be any that keep to these rules, and one draw needn't show every extreme that they name: `obs_tile`: among the rows of one device no tile is named by more than 1024 rows, and one tile, the same for every device of a member, is named by exactly 1024 of them.
All inputs are finite; a program needn't handle non-finite values.
Results may differ from a plain program's by a relative error of at most 0.0055.
Values may be sent and summed in bfloat16 or wider, within the bound.
No kernel may reach another device: no remote copies, remote signals or barrier semaphores. Data moves between devices by JAX's collectives and lax.ppermute only.
A program may use at most 64 MiB of HBM per device.

v0:
```python
import math

import jax
import jax.numpy as jnp
from jax import lax
from jax.sharding import PartitionSpec as P


def padded_2(block, sides, width):
    for axis, dim in sides:
        count = lax.axis_size(axis)
        forward = [(i, i + 1) for i in range(count - 1)]
        backward = [(target, source) for source, target in forward]
        low = lax.ppermute(
            lax.slice_in_dim(block, block.shape[dim] - width, None, axis=dim), axis, forward
        )
        high = lax.ppermute(lax.slice_in_dim(block, 0, width, axis=dim), axis, backward)
        block = jnp.concatenate([low, block, high], axis=dim)
    return block


def conv_apply(padded, kernel):
    n_rows = padded.shape[1] - 2
    n_cols = padded.shape[2] - 2
    summed = None
    for row_off in range(3):
        for col_off in range(3):
            window = padded[:, row_off : row_off + n_rows, col_off : col_off + n_cols]
            product_term = jnp.einsum(
                "oc,chw->ohw", kernel[row_off, col_off], window, preferred_element_type=jnp.float32
            )
            summed = product_term if summed is None else summed + product_term
    return summed


def kernel_grad(out_grad, padded):
    n_rows = out_grad.shape[1]
    n_cols = out_grad.shape[2]
    blocks = []
    for row_off in range(3):
        row_terms = []
        for col_off in range(3):
            window = padded[:, row_off : row_off + n_rows, col_off : col_off + n_cols]
            row_terms.append(
                jnp.einsum("ohw,chw->oc", out_grad, window, preferred_element_type=jnp.float32)
            )
        blocks.append(jnp.stack(row_terms))
    return jnp.stack(blocks)


def back_apply(padded_grad, kernel_cols):
    n_rows = padded_grad.shape[1] - 2
    n_cols = padded_grad.shape[2] - 2
    summed = None
    for row_off in range(3):
        for col_off in range(3):
            window = padded_grad[
                :, 2 - row_off : 2 - row_off + n_rows, 2 - col_off : 2 - col_off + n_cols
            ]
            product_term = jnp.einsum(
                "oc,ohw->chw",
                kernel_cols[row_off, col_off],
                window,
                preferred_element_type=jnp.float32,
            )
            summed = product_term if summed is None else summed + product_term
    return summed


def grid_local(flat_values, flat_weight, cell_flat, n_cells):
    n_recv = flat_values.shape[0]
    obs_chans = flat_values.shape[1]
    block_rows = math.gcd(n_recv, 1024)
    n_blocks = n_recv // block_rows
    cell_ids = jnp.arange(n_cells, dtype=jnp.int32)
    ones_col = jnp.ones((block_rows,), jnp.bfloat16)

    def add_block(carry, pieces):
        data_acc, dens_acc = carry
        block_vals, block_weight, block_cell = pieces
        placing = jnp.where(
            block_cell[None, :] == cell_ids[:, None],
            block_weight[None, :],
            jnp.zeros((), jnp.bfloat16),
        )
        data_acc = data_acc + jnp.einsum(
            "ij,ci->jc", block_vals, placing, preferred_element_type=jnp.float32
        )
        dens_acc = dens_acc + jnp.dot(placing, ones_col, preferred_element_type=jnp.float32)
        return ((data_acc, dens_acc), None)

    start = (jnp.zeros((obs_chans, n_cells), jnp.float32), jnp.zeros((n_cells,), jnp.float32))
    (data_acc, dens_acc), unused = lax.scan(
        add_block,
        start,
        (
            flat_values.reshape(n_blocks, block_rows, obs_chans),
            flat_weight.reshape(n_blocks, block_rows),
            cell_flat.reshape(n_blocks, block_rows),
        ),
    )
    return (data_acc, dens_acc)


def body(obs_values, obs_weight, obs_tile, obs_cell, conv_one, conv_two, density_gain, cotangent):
    n_rows = cotangent.shape[1]
    n_cols = cotangent.shape[2]
    n_cells = n_rows * n_cols
    n_tiles = lax.axis_size("tile") * lax.axis_size("sub")
    n_obs = obs_values.shape[0]
    obs_chans = obs_values.shape[1]
    capacity = 2 * n_obs // n_tiles
    onehot = (obs_tile[:, None] == jnp.arange(n_tiles, dtype=jnp.int32)[None, :]).astype(jnp.int32)
    slots = jnp.sum(jnp.cumsum(onehot, axis=0) * onehot, axis=1) - 1
    dest_slot = obs_tile * capacity + slots
    source = (
        jnp.full((n_tiles * capacity,), n_obs, jnp.int32)
        .at[dest_slot]
        .set(jnp.arange(n_obs, dtype=jnp.int32))
    )
    filled = source < n_obs
    pick = jnp.minimum(source, n_obs - 1)
    send_values = jnp.where(
        filled[:, None], jnp.take(obs_values, pick, axis=0), jnp.zeros((), jnp.bfloat16)
    )
    send_values = send_values.reshape(n_tiles, capacity * obs_chans)
    send_weight = jnp.where(
        filled, jnp.take(obs_weight, pick), jnp.zeros((), jnp.bfloat16)
    ).reshape(n_tiles, capacity)
    send_cell = jnp.where(filled, jnp.take(obs_cell, pick), 0).reshape(n_tiles, capacity)
    got_values, got_weight, got_cell = (
        lax.all_to_all(send_values, ("tile", "sub"), split_axis=0, concat_axis=0, tiled=True),
        lax.all_to_all(send_weight, ("tile", "sub"), split_axis=0, concat_axis=0, tiled=True),
        lax.all_to_all(send_cell, ("tile", "sub"), split_axis=0, concat_axis=0, tiled=True),
    )
    flat_values = got_values.reshape(-1, obs_chans)
    flat_weight = got_weight.reshape(-1)
    cell_flat = got_cell.reshape(-1)
    data_grid, dens_grid = grid_local(flat_values, flat_weight, cell_flat, n_cells)
    data_part = data_grid.reshape(obs_chans, n_rows, n_cols)
    dens_part = dens_grid.reshape(n_rows, n_cols)
    data_sum, density = lax.psum((data_part, dens_part), "chan")
    features = (data_sum / (1.0 + density)[None]).astype(jnp.bfloat16)
    log_density = jnp.log1p(density)
    feats_pad = padded_2(features, (("tile", 1), ("sub", 2)), 1)
    pre_one = conv_apply(feats_pad, conv_one) + density_gain[:, None, None] * log_density[None]
    hidden = jax.nn.silu(pre_one).astype(jnp.bfloat16)
    hidden_own = padded_2(hidden, (("tile", 1), ("sub", 2)), 1)
    hidden_pad = lax.all_gather(hidden_own, "chan", axis=0, tiled=True)
    encoded = conv_apply(hidden_pad, conv_two).astype(jnp.bfloat16)
    cot_pad = padded_2(cotangent, (("tile", 1), ("sub", 2)), 1)
    grad_two = kernel_grad(cotangent, hidden_pad)
    cot_full = lax.all_gather(cot_pad, "chan", axis=0, tiled=True)
    kernel_cols = lax.all_to_all(conv_two, "chan", split_axis=3, concat_axis=2, tiled=True)
    grad_hidden = back_apply(cot_full, kernel_cols)
    sigma = jax.nn.sigmoid(pre_one)
    grad_pre = (grad_hidden * sigma * (1.0 + pre_one * (1.0 - sigma))).astype(jnp.bfloat16)
    grad_one = kernel_grad(grad_pre, feats_pad)
    grad_gain = jnp.sum(grad_pre.astype(jnp.float32) * log_density[None], axis=(1, 2))
    summed_one, summed_two, summed_gain = lax.psum((grad_one, grad_two, grad_gain), ("tile", "sub"))
    scale_factor = 1.0 / math.sqrt(n_tiles * n_cells)
    return (
        encoded,
        summed_one * scale_factor,
        summed_two * scale_factor,
        summed_gain * scale_factor,
    )


def solution(mesh):
    placed = (
        P(("member", "tile", "chan", "sub"), None),
        P(("member", "tile", "chan", "sub")),
        P(("member", "tile", "chan", "sub")),
        P(("member", "tile", "chan", "sub")),
        P(None, None, "chan", None),
        P(None, None, "chan", None),
        P("chan"),
        P(("member", "chan"), "tile", "sub"),
    )
    return jax.shard_map(
        body,
        mesh=mesh,
        in_specs=placed,
        out_specs=(
            P(("member", "chan"), "tile", "sub"),
            P("member", None, "chan", None),
            P("member", None, "chan", None),
            P(("member", "chan")),
        ),
        check_vma=False,
    )
```

profile of v0, /device:TPU:0, one launch (start us, length us, event | category | flops | bytes accessed | tf_op | source)
XLA Modules:
  0.0 490.8 jit_solution(184157803824915240)
XLA Ops:
  12.4 15.5 %scatter_custom_fusion = s32[8192]{0:T(1024)S(1)} fusion(s32[4096]{0:T(1024)S(1)} %compare_select_fusion.1, s32[4096]{0:T(1024)S(1)} %iota.14, s32[]{:T(128)} %constant.46.clone.1), kind=kCustom, calls=%fused_computation.211 | custom fusion | bytes 32772 | tf_op jit(solution)/shard_map/scatter | solution.py:119
  28.0 50.7 %gather_fusion.2 = bf16[8192]{0:T(1024)(128)(2,1)S(1)} fusion(bf16[4096]{0:T(1024)(128)(2,1)S(1)} %copy-done.2, s32[8192]{0:T(1024)S(1)} %fusion.153), kind=kCustom, calls=%fused_computation.2 | custom fusion | bytes 65536 | tf_op jit(solution)/shard_map/jit(_take)/gather | solution.py:128
  80.7 6.3 %all-to-all-start.2 = ((bf16[8,2,512]{2,1,0:T(2,128)(2,1)}), bf16[8,2,512]{2,1,0:T(2,128)(2,1)S(1)}, u32[]{:S(2)}, u32[]{:S(2)}) async-start(bf16[8,2,512]{2,1,0:T(2,128)(2,1)} %reshape.179), calls=%async_computation.2 | async-start | bytes 32768 | tf_op jit(solution)/shard_map/all_to_all | solution.py:133
  87.0 45.5 %gather_fusion.1 = s32[8192]{0:T(1024)S(1)} fusion(s32[4096]{0:T(1024)S(1)} %copy-done, s32[8192]{0:T(1024)S(1)} %fusion.153), kind=kCustom, calls=%fused_computation.1 | custom fusion | bytes 98304 | tf_op jit(solution)/shard_map/jit(_take)/gather | solution.py:130
  133.2 5.1 %all-to-all-start.1 = ((s32[8,1,1024]{2,1,0:T(1,128)}), s32[8,1,1024]{2,1,0:T(1,128)S(1)}, u32[]{:S(2)}, u32[]{:S(2)}) async-start(s32[8,1,1024]{2,1,0:T(1,128)} %bitcast.2), calls=%async_computation.1 | async-start | bytes 65536 | tf_op jit(solution)/shard_map/all_to_all | solution.py:134
  149.3 24.0 %gather_fusion = bf16[8192,64]{1,0:T(8,128)(2,1)S(1)} fusion(bf16[4096,64]{1,0:T(8,128)(2,1)S(1)} %copy.118, s32[8192]{0:T(1024)S(1)} %fusion.153), kind=kCustom, calls=%fused_computation | custom fusion | bytes 2129920 | tf_op jit(solution)/shard_map/jit(_take)/gather | solution.py:124
  174.9 4.4 all-to-all-start.3
  182.9 8.3 %all-to-all-done.3 = bf16[3,3,128,256]{2,1,0,3:T(4,128)(2,1)} async-done(((bf16[3,3,128,256]{2,1,0,3:T(4,128)(2,1)}), bf16[3,3,128,256]{2,1,0,3:T(4,128)(2,1)}, u32[]{:S(2)}, u32[]{:S(2)}) %all-to-all-start.3) | async-done | bytes 589856 | tf_op jit(solution)/shard_map/all_to_all | solution.py:154
  191.2 4.7 all-to-all-start
  196.6 3.9 collective-permute-start.8
  202.0 14.0 %collective-permute-done.8 = bf16[128,1,384]{0,2,1:T(8,128)(2,1)S(1)} collective-permute-done((bf16[128,1,384]{0,2,1:T(8,128)(2,1)S(1)}, bf16[128,1,384]{0,2,1:T(8,128)(2,1)S(1)}, u32[]{:S(2)}, u32[]{:S(2)}) %collective-permute-start.8) | collective-permute-done | bytes 98336 | tf_op jit(solution)/shard_map/ppermute | solution.py:14
  225.5 6.4 %reduce.2 = bf16[8,65536]{1,0:T(8,128)(2,1)S(1)} reduce(bf16[8,1,65536]{2,1,0:T(2,128)(2,1)S(1)} %reshape.178, bf16[]{:T(256)} %constant.88), dimensions={1}, to_apply=%all_to_all.33.reduce_sub_computation | reduce | bytes 2097154 | tf_op jit(solution)/shard_map/all_to_all | solution.py:132
  234.1 38.9 %while.13 = (s32[]{:T(128)}, f32[64,3072]{1,0:T(8,128)}, f32[3072]{0:T(1024)S(1)}, bf16[8,1024,64]{2,1,0:T(8,128)(2,1)S(1)}, s32[8,1024]{1,0:T(8,128)S(1)}, /*in...) while((s32[]{:T(128)}, f32[64,3072]{1,0:T(8,128)}, f32[3072]{0:T(1024)S(1)}, ...), condition=%wide.region_5.6_spmd.clone, body=%wide.region_4.5_spmd.clone.sunk | while | flops 421926912 | bytes 8200364 | solution.py:93
  275.1 6.9 %psum.36 = f32[8,384]{1,0:T(8,128)S(1)} all-reduce(f32[8,384]{1,0:T(8,128)S(1)} %reshape.88), channel_id=1, replica_groups=mesh['member'=2,'tile'=4,'chan'=2,'sub'=2] {'chan'}, use_global_device_ids=true, to_apply=%region_7.8 | all-reduce | flops 3072 | bytes 24576 | tf_op jit(solution)/shard_map/psum | solution.py:142
  282.5 3.3 fusion.25
  298.2 25.3 %all-reduce.4.cloned.1.call-done = f32[64,8,384]{2,0,1:T(8,128)} async-done(((f32[64,8,384]{2,0,1:T(8,128)}), f32[64,8,384]{2,0,1:T(8,128)}) %all-reduce.4.cloned.1.call-update) | async-done | bytes 786448 | tf_op jit(solution)/shard_map/psum | solution.py:142
  324.7 3.4 collective-permute-start
  329.9 4.3 collective-permute-done.1
  335.5 3.0 collective-permute-start.2
  350.4 3.4 collective-permute-start.4
  356.4 4.1 collective-permute-done.5
  363.1 14.7 %psum.39 = f32[128]{0:T(128)S(1)} all-reduce(f32[128]{0:T(128)S(1)} %get-tuple-element.118), channel_id=1, replica_groups=mesh['member'=2,'tile'=4,'chan'=2,'sub'=2] {'tile','sub'}, use_global_device_ids=true, to_apply=%region_11.12 | all-reduce | flops 128 | bytes 1024 | tf_op jit(solution)/shard_map/psum | solution.py:160
  383.8 25.9 %all-gather.3.cloned.1.call-done = bf16[256,10,386]{0,2,1:T(8,128)(2,1)} async-done(((bf16[128,10,386]{0,2,1:T(8,128)(2,1)}), bf16[256,10,386]{0,2,1:T(8,128)(2,1)}) %all-gather.3.cloned.1.call-update) | async-done | bytes 1976336 | tf_op jit(solution)/shard_map/all_gather | solution.py:149
  425.5 54.1 %all-reduce.6.cloned.1.call-done = (f32[3,3,128,64]{2,3,1,0:T(8,128)}, f32[3,3,128,256]{2,3,1,0:T(8,128)}) async-done(((f32[3,3,128,64]{2,3,1,0:T(8,128)}, f32[3,3,128,256]{2,3,1,0:T(8,128)}), (f32[3,3,128,64]{2,3,1,0:T(8,128)}, f32[3,3,128,256]{2,3,1,0:T(8,128)})) %all-reduce.6.cloned.1.call-update) | async-done | bytes 1474576 | tf_op jit(solution)/shard_map/psum | solution.py:160
  (263 shorter events, 138.2 us)
Async XLA Ops:
  7.2 79.8 %copy-start = (s32[4096]{0:T(1024)S(1)}, s32[4096]{0:T(1024)}, u32[]{:S(2)}) copy-start(s32[4096]{0:T(1024)} %param.13) | copy-start | bytes 49156
  80.7 52.5 %all-to-all-start.2 = ((bf16[8,2,512]{2,1,0:T(2,128)(2,1)}), bf16[8,2,512]{2,1,0:T(2,128)(2,1)S(1)}, u32[]{:S(2)}, u32[]{:S(2)}) async-start(bf16[8,2,512]{2,1,0:T(2,128)(2,1)} %reshape.179), calls=%async_computation.2 | async-start | bytes 32768 | tf_op jit(solution)/shard_map/all_to_all | solution.py:133
  87.0 51.3 %copy-start.19 = (bf16[3,3,128,256]{3,2,1,0:T(8,128)(2,1)S(1)}, bf16[3,3,128,256]{3,2,1,0:T(8,128)(2,1)}, u32[]{:S(2)}) copy-start(bf16[3,3,128,256]{3,2,1,0:T(8,128)(2,1)} %param.15) | copy-start | bytes 1769476
  133.2 41.7 %all-to-all-start.1 = ((s32[8,1,1024]{2,1,0:T(1,128)}), s32[8,1,1024]{2,1,0:T(1,128)S(1)}, u32[]{:S(2)}, u32[]{:S(2)}) async-start(s32[8,1,1024]{2,1,0:T(1,128)} %bitcast.2), calls=%async_computation.1 | async-start | bytes 65536 | tf_op jit(solution)/shard_map/all_to_all | solution.py:134
  174.9 16.3 %all-to-all-start.3 = ((bf16[3,3,128,256]{2,1,0,3:T(4,128)(2,1)}), bf16[3,3,128,256]{2,1,0,3:T(4,128)(2,1)}, u32[]{:S(2)}, u32[]{:S(2)}) async-start(bf16[3,3,128,256]{2,1,0,3:T(4,128)(2,1)} %copy.125), calls=%async_computation.3 | async-start | bytes 1572864 | tf_op jit(solution)/shard_map/all_to_all | solution.py:154
  191.2 33.3 %all-to-all-start = ((bf16[8,2,32768]{2,1,0:T(2,128)(2,1)}), bf16[8,2,32768]{2,1,0:T(2,128)(2,1)S(1)}, u32[]{:S(2)}, u32[]{:S(2)}) async-start(bf16[8,2,32768]{2,1,0:T(2,128)(2,1)} %reshape.177), calls=%async_computation | async-start | bytes 2097152 | tf_op jit(solution)/shard_map/all_to_all | solution.py:132
  195.9 86.6 %all-gather.5.cloned.1.call-start = ((), (), s32[]{:S(2)}) async-start(), calls=%async_computation.6 | async-start | bytes 3010560 | tf_op jit(solution)/shard_map/all_gather | solution.py:153
  196.6 19.5 %collective-permute-start.8 = (bf16[128,1,384]{0,2,1:T(8,128)(2,1)S(1)}, bf16[128,1,384]{0,2,1:T(8,128)(2,1)S(1)}, u32[]{:S(2)}, u32[]{:S(2)}) collective-permute-start(bf16[128,1,384]{0,2,1:T(8,128)(2,1)S(1)} %get-tuple-element.104), channel_id=1, source_target_pairs={{0,4},{4,8},{8,12},{1,5},{5,9},{9,13},{2,6},{6,10},{10,14},{3,7},{... | collective-permute-start | bytes 294920 | tf_op jit(solution)/shard_map/ppermute | solution.py:14
  200.4 15.6 %collective-permute-start.9 = (bf16[128,1,384]{0,2,1:T(8,128)(2,1)S(1)}, bf16[128,1,384]{0,2,1:T(8,128)(2,1)S(1)}, u32[]{:S(2)}, u32[]{:S(2)}) collective-permute-start(bf16[128,1,384]{0,2,1:T(8,128)(2,1)S(1)} %get-tuple-element.105), channel_id=1, source_target_pairs={{4,0},{8,4},{12,8},{5,1},{9,5},{13,9},{6,2},{10,6},{14,10},{7,3},{... | collective-permute-start | bytes 294920 | tf_op jit(solution)/shard_map/ppermute | solution.py:17
  216.0 3.2 collective-permute-start.10
  217.9 3.1 collective-permute-start.11
  222.2 101.3 %all-reduce.4.cloned.1.call-start = ((), (), s32[]{:S(2)}) async-start(), calls=%async_computation.4 | async-start | bytes 1572864 | tf_op jit(solution)/shard_map/psum | solution.py:142
  282.0 127.7 %all-gather.3.cloned.1.call-start = ((), (), s32[]{:S(2)}) async-start(), calls=%async_computation.5 | async-start | bytes 3010560 | tf_op jit(solution)/shard_map/all_gather | solution.py:149
  296.4 33.0 %copy-start.29 = (bf16[3,3,128,64]{2,3,1,0:T(8,128)(2,1)S(1)}, bf16[3,3,128,64]{2,3,1,0:T(8,128)(2,1)}, u32[]{:S(2)}) copy-start(bf16[3,3,128,64]{2,3,1,0:T(8,128)(2,1)} %param.14) | copy-start | bytes 442372
  324.7 5.1 %collective-permute-start = (bf16[64,1,384]{2,0,1:T(8,128)(2,1)S(1)}, bf16[64,1,384]{2,0,1:T(8,128)(2,1)S(1)}, u32[]{:S(2)}, u32[]{:S(2)}) collective-permute-start(bf16[64,1,384]{2,0,1:T(8,128)(2,1)S(1)} %get-tuple-element.112), channel_id=1, source_target_pairs={{0,4},{4,8},{8,12},{1,5},{5,9},{9,13},{2,6},{6,10},{10,14},{3,7},{... | collective-permute-start | bytes 147464 | tf_op jit(solution)/shard_map/ppermute | solution.py:14
  328.1 6.0 %collective-permute-start.1 = (bf16[64,1,384]{2,0,1:T(8,128)(2,1)S(1)}, bf16[64,1,384]{2,0,1:T(8,128)(2,1)S(1)}, u32[]{:S(2)}, u32[]{:S(2)}) collective-permute-start(bf16[64,1,384]{2,0,1:T(8,128)(2,1)S(1)} %get-tuple-element.113), channel_id=1, source_target_pairs={{4,0},{8,4},{12,8},{5,1},{9,5},{13,9},{6,2},{10,6},{14,10},{7,3},{... | collective-permute-start | bytes 147464 | tf_op jit(solution)/shard_map/ppermute | solution.py:17
  334.2 5.2 %collective-permute-start.3 = (bf16[64,10,1]{2,0,1:T(8,128)(2,1)S(1)}, bf16[64,10,1]{2,0,1:T(8,128)(2,1)S(1)}, u32[]{:S(2)}, u32[]{:S(2)}) collective-permute-start(bf16[64,10,1]{2,0,1:T(8,128)(2,1)S(1)} %get-tuple-element.110), channel_id=1, source_target_pairs={{1,0},{3,2},{5,4},{7,6},{9,8},{11,10},{13,12},{15,14},{17,16},{19,... | collective-permute-start | bytes 3848 | tf_op jit(solution)/shard_map/ppermute | solution.py:17
  335.5 4.1 collective-permute-start.2
  350.4 6.0 %collective-permute-start.4 = (bf16[128,1,384]{0,2,1:T(8,128)(2,1)S(1)}, bf16[128,1,384]{0,2,1:T(8,128)(2,1)S(1)}, u32[]{:S(2)}, u32[]{:S(2)}) collective-permute-start(bf16[128,1,384]{0,2,1:T(8,128)(2,1)S(1)} %get-tuple-element.106), channel_id=1, source_target_pairs={{0,4},{4,8},{8,12},{1,5},{5,9},{9,13},{2,6},{6,10},{10,14},{3,7},{... | collective-permute-start | bytes 294920 | tf_op jit(solution)/shard_map/ppermute | solution.py:14
  353.8 6.7 %collective-permute-start.5 = (bf16[128,1,384]{0,2,1:T(8,128)(2,1)S(1)}, bf16[128,1,384]{0,2,1:T(8,128)(2,1)S(1)}, u32[]{:S(2)}, u32[]{:S(2)}) collective-permute-start(bf16[128,1,384]{0,2,1:T(8,128)(2,1)S(1)} %get-tuple-element.107), channel_id=1, source_target_pairs={{4,0},{8,4},{12,8},{5,1},{9,5},{13,9},{6,2},{10,6},{14,10},{7,3},{... | collective-permute-start | bytes 294920 | tf_op jit(solution)/shard_map/ppermute | solution.py:17
  360.5 17.3 %collective-permute-start.6 = (bf16[128,10,1]{0,2,1:T(2,128)(2,1)S(1)}, bf16[128,10,1]{0,2,1:T(2,128)(2,1)S(1)}, u32[]{:S(2)}, u32[]{:S(2)}) collective-permute-start(bf16[128,10,1]{0,2,1:T(2,128)(2,1)S(1)} %get-tuple-element.102), channel_id=1, source_target_pairs={{0,1},{2,3},{4,5},{6,7},{8,9},{10,11},{12,13},{14,15},{16,17},{18,... | collective-permute-start | bytes 7688 | tf_op jit(solution)/shard_map/ppermute | solution.py:14
  361.8 16.0 %collective-permute-start.7 = (bf16[128,10,1]{0,2,1:T(2,128)(2,1)S(1)}, bf16[128,10,1]{0,2,1:T(2,128)(2,1)S(1)}, u32[]{:S(2)}, u32[]{:S(2)}) collective-permute-start(bf16[128,10,1]{0,2,1:T(2,128)(2,1)S(1)} %get-tuple-element.103), channel_id=1, source_target_pairs={{1,0},{3,2},{5,4},{7,6},{9,8},{11,10},{13,12},{15,14},{17,16},{19,... | collective-permute-start | bytes 7688 | tf_op jit(solution)/shard_map/ppermute | solution.py:17
  380.3 99.4 %all-reduce.6.cloned.1.call-start = ((), (), s32[]{:S(2)}) async-start(), calls=%async_computation.7 | async-start | bytes 2949120 | tf_op jit(solution)/shard_map/psum | solution.py:160
  383.3 28.8 %copy-start.11 = (bf16[128,8,384]{0,2,1:T(8,128)(2,1)S(1)}, bf16[128,8,384]{0,2,1:T(8,128)(2,1)}, u32[]{:S(2)}) copy-start(bf16[128,8,384]{0,2,1:T(8,128)(2,1)} %copy-done.10) | copy-start | bytes 2359300
  (41 other events, 178.8 us)
Sparse Core Ops, SparseCore 0:
  222.3 37.8 all-gather.4
  282.2 41.2 all-reduce.3
  380.4 29.3 all-gather.2
  418.6 61.0 all-reduce.5
where the time goes:
time: 500 us; the launch traced here: 491 us
  local copies, waits for them, and re-layouts  174 us (35%)
  waiting for transfers between devices  139 us (28%)
  matrix products  70 us (14%)
  starting transfers between devices  46.1 us (9%)
  other arithmetic  25.3 us (5%)
  blocking collectives  21.6 us (4%)
  between operations  14.9 us (3%)
    psum x1, waiting for transfers between devices, body(): lax.psum((grad_one, grad_two, grad_gain), ('tile', 'sub'))  54.1 us
    gather x1, local copies, waits for them, and re-layouts, body(): jnp.take(obs_weight, pick)  50.7 us
    gather x1, local copies, waits for them, and re-layouts, body(): jnp.take(obs_cell, pick)  45.5 us
    all_gather x1, waiting for transfers between devices, body(): hidden_pad = lax.all_gather(hidden_own, 'chan', axis=0, tiled=True)  25.9 us
    gather x2, local copies, waits for them, and re-layouts, body(): jnp.take(obs_values, pick, axis=0)  25.6 us
    psum x1, waiting for transfers between devices, body(): data_sum, density = lax.psum((data_part, dens_part), 'chan')  25.3 us
    dot_general x9, matrix products, back_apply(): jnp.einsum('oc,ohw->chw', kernel_cols[row_off, col_off], window, preferre...  18.1 us
    dot_general x8, matrix products, add_block(): jnp.einsum('ij,ci->jc', block_vals, placing, preferred_element_type=jnp.f...  17.4 us
  transfers between devices with their start and end apart: 20, of which 10 were waited for; matrix products, arithmetic and copies ran while one was open for 33% of the time, Pallas kernels for 0%

commit v1 on v0

v1 whole, which is shorter than its diff:
```python
import functools
import math

import jax
import jax.numpy as jnp
from jax import lax
from jax.experimental import pallas as pl
from jax.experimental.pallas import tpu as pltpu
from jax.sharding import PartitionSpec as P

BF16 = jnp.bfloat16
F32 = jnp.float32
LANES = 128
BLOCK = 256
META = 8
VMEM_BYTES = 56 * 1024 * 1024


def dot_nt(a, b):
    return lax.dot_general(a, b, (((1,), (1,)), ((), ())), preferred_element_type=F32)


def dot_nn(a, b):
    return lax.dot_general(a, b, (((1,), (0,)), ((), ())), preferred_element_type=F32)


def iota(shape, dim, dtype=jnp.int32):
    return lax.broadcasted_iota(jnp.int32, shape, dim).astype(dtype)


def vmem_spec():
    return pl.BlockSpec(memory_space=pltpu.VMEM)


def smem_spec():
    return pl.BlockSpec(memory_space=pltpu.SMEM)


def call(kernel, out_shape, in_specs, scratch, flops, moved, name):
    n_out = len(out_shape) if isinstance(out_shape, (tuple, list)) else None
    out_specs = vmem_spec() if n_out is None else [vmem_spec() for _ in range(n_out)]
    return pl.pallas_call(
        kernel,
        out_shape=out_shape,
        in_specs=in_specs,
        out_specs=out_specs,
        scratch_shapes=scratch,
        compiler_params=pltpu.CompilerParams(vmem_limit_bytes=VMEM_BYTES),
        cost_estimate=pl.CostEstimate(flops=flops, bytes_accessed=moved, transcendentals=0),
        name=name,
    )


def route_kernel(
    n_tiles, cap, tile_ref, weight_ref, cell_ref, values_ref, out_ref,
    onehot_ref, slot_ref, info_ref, info_smem, sem,
):
    n_blocks = tile_ref.shape[0]
    n_obs_chans = values_ref.shape[1]
    pairs = n_tiles * n_blocks
    tiles = tile_ref[...]
    for t in range(n_tiles):
        onehot_ref[t * n_blocks : (t + 1) * n_blocks, :] = jnp.where(tiles == t, 1.0, 0.0).astype(BF16)
    onehot = onehot_ref[...]
    upper = jnp.where(
        iota((BLOCK, BLOCK), 0) <= iota((BLOCK, BLOCK), 1), 1.0, 0.0
    ).astype(BF16)
    cum = dot_nn(onehot, upper)
    totals = dot_nn(onehot, jnp.ones((BLOCK, BLOCK), BF16))
    here = iota((pairs, pairs), 0)
    there = iota((pairs, pairs), 1)
    earlier = jnp.where(
        (here // n_blocks == there // n_blocks) & (there < here), 1.0, 0.0
    ).astype(BF16)
    offset = dot_nn(earlier, totals.astype(BF16))
    place = cum + offset - 1.0
    slots = jnp.zeros(tiles.shape, F32)
    for t in range(n_tiles):
        slots = jnp.where(tiles == t, place[t * n_blocks : (t + 1) * n_blocks, :], slots)
    slot_ref[...] = slots
    total_row = dot_nt(jnp.ones((8, BLOCK), BF16), onehot)
    offset_row = dot_nt(total_row.astype(BF16), earlier)
    base_row = jnp.minimum(jnp.floor(offset_row * (1.0 / LANES)) * LANES, float(cap - BLOCK))
    spill = jnp.where(offset_row + total_row > base_row + BLOCK, 1.0, 0.0)
    any_spill = jnp.max(spill, axis=1, keepdims=True)
    info_ref[...] = jnp.where(
        iota((8, pairs), 0) == 0, base_row, any_spill
    ).astype(jnp.int32)
    copy = pltpu.make_async_copy(info_ref, info_smem, sem)
    copy.start()
    out_ref[...] = jnp.zeros(out_ref.shape, BF16)
    eye = jnp.where(
        iota((n_obs_chans, n_obs_chans), 0) == iota((n_obs_chans, n_obs_chans), 1), 1.0, 0.0
    ).astype(BF16)
    meta_row = iota((16, BLOCK), 0)
    window = iota((BLOCK, BLOCK), 0, F32)
    copy.wait()

    def columns(b):
        rows = values_ref[pl.ds(pl.multiple_of(b * BLOCK, BLOCK), BLOCK), :]
        turned = dot_nt(eye, rows).astype(BF16)
        cell = cell_ref[pl.ds(b, 1), :]
        weight = weight_ref[pl.ds(b, 1), :]
        high = (cell // LANES).astype(F32)
        low = (cell % LANES).astype(F32)
        meta = jnp.where(
            meta_row == 0,
            weight,
            jnp.where(meta_row == 1, high, jnp.where(meta_row == 2, low, 0.0)),
        ).astype(BF16)
        return jnp.concatenate([turned, meta], axis=0)

    def add(t, base, wide, key):
        chosen = jnp.where(window == key, 1.0, 0.0).astype(BF16)
        part = dot_nt(wide, chosen)[: n_obs_chans + META].astype(BF16)
        where = pl.ds(pl.multiple_of(base, LANES), BLOCK)
        out_ref[t, :, where] = out_ref[t, :, where] + part

    def first(b, carry):
        wide = columns(b)
        tile = tile_ref[pl.ds(b, 1), :]
        slot = slot_ref[pl.ds(b, 1), :]
        for t in range(n_tiles):
            base = info_smem[0, t * n_blocks + b]
            key = jnp.where(tile == t, slot - base.astype(F32), -1.0)
            add(t, base, wide, key)
        return carry

    lax.fori_loop(0, n_blocks, first, 0)

    if cap > BLOCK:

        @pl.when(info_smem[1, 0] > 0)
        def _():
            def second(b, carry):
                wide = columns(b)
                tile = tile_ref[pl.ds(b, 1), :]
                slot = slot_ref[pl.ds(b, 1), :]
                for t in range(n_tiles):
                    start = info_smem[0, t * n_blocks + b]
                    base = jnp.minimum(start + BLOCK, cap - BLOCK)
                    far = (tile == t) & (slot >= (start + BLOCK).astype(F32))
                    key = jnp.where(far, slot - base.astype(F32), -1.0)
                    add(t, base, wide, key)
                return carry

            lax.fori_loop(0, n_blocks, second, 0)


def route(obs_values, obs_weight, obs_tile, obs_cell, n_tiles, cap):
    n_obs, chans = obs_values.shape
    n_blocks = n_obs // BLOCK
    rows = chans + META
    return call(
        functools.partial(route_kernel, n_tiles, cap),
        jax.ShapeDtypeStruct((n_tiles, rows, cap), BF16),
        [vmem_spec()] * 4,
        [
            pltpu.VMEM((n_tiles * n_blocks, BLOCK), BF16),
            pltpu.VMEM((n_blocks, BLOCK), F32),
            pltpu.VMEM((8, n_tiles * n_blocks), jnp.int32),
            pltpu.SMEM((8, n_tiles * n_blocks), jnp.int32),
            pltpu.SemaphoreType.DMA,
        ],
        2 * n_obs * n_tiles * BLOCK * 80,
        n_tiles * rows * cap * 2,
        "route",
    )(
        obs_tile.reshape(n_blocks, BLOCK),
        obs_weight.astype(F32).reshape(n_blocks, BLOCK),
        obs_cell.reshape(n_blocks, BLOCK),
        obs_values,
    )


def grid_kernel(n_rows, n_cols, got_ref, own_ref, send_ref, left_ref):
    n_send, rows, cap = got_ref.shape
    chans = rows - META
    per_row = n_cols // LANES
    data_rows = n_rows * chans
    own_ref[...] = jnp.zeros(own_ref.shape, F32)
    columns = iota((n_cols, cap), 0, F32)
    row_ids = iota((n_rows, cap), 0, F32)

    def one(s, carry):
        values = got_ref[s, 0:chans, :]
        meta = got_ref[s, chans:rows, :].astype(F32)
        weight = meta[0:1]
        high = meta[1:2]
        row = jnp.floor((high + 0.5) * (1.0 / per_row))
        column = (high - row * per_row) * LANES + meta[2:3]
        placed = jnp.where(columns == column, weight, 0.0).astype(BF16)
        in_row = jnp.where(row_ids == row, 1.0, 0.0)
        for r in range(n_rows):
            left_ref[r * chans : (r + 1) * chans, :] = values * in_row[r : r + 1].astype(BF16)
        left_ref[data_rows : data_rows + n_rows, :] = in_row.astype(BF16)
        own_ref[...] += dot_nt(left_ref[...], placed)
        return carry

    left_ref[data_rows:, :] = jnp.zeros((left_ref.shape[0] - data_rows, cap), BF16)
    lax.fori_loop(0, n_send, one, 0)
    send_ref[0:data_rows, :] = own_ref[0:data_rows, :].astype(BF16)
    density = own_ref[data_rows : data_rows + n_rows, :]
    high = density.astype(BF16)
    low = (density - high.astype(F32)).astype(BF16)
    send_ref[data_rows : data_rows + 2 * n_rows, :] = jnp.concatenate(
        [high.astype(F32), low.astype(F32)], axis=0
    ).astype(BF16)


def grid(got, n_rows, n_cols):
    n_send, rows, cap = got.shape
    chans = rows - META
    total = n_rows * chans + 2 * n_rows
    return call(
        functools.partial(grid_kernel, n_rows, n_cols),
        [
            jax.ShapeDtypeStruct((total, n_cols), F32),
            jax.ShapeDtypeStruct((total, n_cols), BF16),
        ],
        [vmem_spec()],
        [pltpu.VMEM((total, cap), BF16)],
        2 * n_send * cap * total * n_cols,
        n_send * rows * cap * 2,
        "grid",
    )(got)


def lane_mask(shape, n_cols, sub, depth):
    lane = iota(shape, 1)
    width = n_cols + LANES
    keep_right = (lane >= n_cols) & (lane < n_cols + depth) & (sub == 0)
    keep_left = (lane >= width - depth) & (sub == 1)
    return (lane < n_cols) | keep_right | keep_left


def back_kernel(n_cols, index_ref, kernel_ref, own_ref, peer_ref, halo_ref, out_ref, wide_ref, acc_ref):
    n_ext = halo_ref.shape[0]
    n_rows = n_ext - 2
    n_out = out_ref.shape[1]
    own_chans = own_ref.shape[1]
    all_chans = halo_ref.shape[1]
    width = n_cols + LANES
    keep = lane_mask((all_chans, width), n_cols, index_ref[2], 1)
    acc_ref[...] = jnp.zeros(acc_ref.shape, F32)

    def one(h, carry):
        if peer_ref is None:
            mid = own_ref[h]
        else:
            mid = jnp.concatenate([own_ref[h], peer_ref[h]], axis=0)
        ext = jnp.concatenate([mid, halo_ref[h]], axis=1).astype(F32)
        ext = jnp.where(keep, ext, 0.0)
        wide_ref[0:all_chans, :] = pltpu.roll(ext, width - 1, 1)[:, :n_cols].astype(BF16)
        wide_ref[all_chans : 2 * all_chans, :] = mid
        wide_ref[2 * all_chans :, :] = pltpu.roll(ext, 1, 1)[:, :n_cols].astype(BF16)
        part = dot_nn(kernel_ref[...], wide_ref[...])
        for a in range(3):
            acc_ref[h + a] += part[a * n_out : (a + 1) * n_out]
        return carry

    lax.fori_loop(0, n_ext, one, 0)
    out_ref[...] = acc_ref[2 : 2 + n_rows]


def back(index, kernel, own, peer, halo, n_cols):
    n_ext, all_chans = halo.shape[0], halo.shape[1]
    n_out = kernel.shape[0] // 3
    body = functools.partial(back_kernel, n_cols)
    pieces = [own] if peer is None else [own, peer]
    if peer is None:
        body = lambda i, k, o, *rest: back_kernel(n_cols, i, k, o, None, *rest)
    return call(
        body,
        jax.ShapeDtypeStruct((n_ext - 2, n_out, n_cols), F32),
        [smem_spec()] + [vmem_spec()] * (2 + len(pieces)),
        [
            pltpu.VMEM((3 * all_chans, n_cols), BF16),
            pltpu.VMEM((n_ext + 2, n_out, n_cols), F32),
        ],
        2 * n_ext * 9 * all_chans * n_out * n_cols,
        n_ext * all_chans * n_cols * 2,
        "back",
    )(index, kernel, *pieces, halo)


def grads_kernel(
    index_ref, kernel_ref, gain_ref, feats_ref, halo_ref, cot_ref, back_ref,
    hidden_ref, grads_ref,
    taps_ref, logs_ref, pre_ref, wide_ref, out_grad_ref, pre_grad_ref, gain_acc_ref, acc_ref,
):
    n_feat_rows, _, n_cols = feats_ref.shape
    n_rows = n_feat_rows - 4
    n_hidden = kernel_ref.shape[0]
    chans = kernel_ref.shape[1] // 9
    own = cot_ref.shape[1]
    width = n_cols + LANES
    tile, chan, sub, n_tile = index_ref[0], index_ref[1], index_ref[2], index_ref[3]
    keep_two = lane_mask((chans, width), n_cols, sub, 2)

    def taps(i, carry):
        ext = jnp.concatenate([feats_ref[i], halo_ref[i]], axis=1).astype(F32)
        feats = jnp.where(keep_two, ext[0:chans], 0.0)
        logs_ref[i] = jnp.log(1.0 + (ext[chans : chans + 1] + ext[chans + 1 : chans + 2]))
        taps_ref[i, 0:chans, :] = pltpu.roll(feats, 1, 1).astype(BF16)
        taps_ref[i, chans : 2 * chans, :] = feats.astype(BF16)
        taps_ref[i, 2 * chans : 3 * chans, :] = pltpu.roll(feats, width - 1, 1).astype(BF16)
        return carry

    lax.fori_loop(0, n_feat_rows, taps, 0)
    gain = gain_ref[...]
    keep_one = lane_mask((n_hidden, width), n_cols, sub, 1)
    acc_ref[...] = jnp.zeros(acc_ref.shape, F32)
    for e in (0, 1, n_rows + 2, n_rows + 3):
        out_grad_ref[e] = jnp.zeros((own, n_cols), BF16)
        pre_grad_ref[e] = jnp.zeros((own, n_cols), BF16)
    for r in range(n_rows):
        out_grad_ref[r + 2] = cot_ref[r]

    def hide(h, carry):
        columns = taps_ref[pl.ds(h, 3)].reshape(9 * chans, width)
        pre = dot_nn(kernel_ref[...], columns) + gain * logs_ref[h + 1]
        pre_ref[...] = pre[:, :n_cols]
        hidden = pre / (1.0 + jnp.exp(-pre))
        inside = ((h > 0) | (tile > 0)) & ((h < n_rows + 1) | (tile < n_tile - 1))
        hidden = jnp.where(keep_one & inside, hidden, 0.0)
        hidden_ref[h, 0:n_hidden, :] = pltpu.roll(hidden, 1, 1)[:, :n_cols].astype(BF16)
        hidden_ref[h, n_hidden : 2 * n_hidden, :] = hidden[:, :n_cols].astype(BF16)
        hidden_ref[h, 2 * n_hidden :, :] = pltpu.roll(hidden, width - 1, 1)[:, :n_cols].astype(BF16)
        left = out_grad_ref[pl.ds(h, 3)].reshape(3 * own, n_cols)
        acc_ref[:, 0 : 3 * n_hidden] += dot_nt(left, hidden_ref[h])

        @pl.when((h > 0) & (h < n_rows + 1))
        def _():
            mine = pre_ref[pl.ds(pl.multiple_of(chan * own, own), own), :]
            s = 1.0 / (1.0 + jnp.exp(-mine))
            grad = (back_ref[h - 1] * s * (1.0 + mine * (1.0 - s))).astype(BF16)
            pre_grad_ref[h + 1] = grad
            gain_acc_ref[...] += grad.astype(F32) * logs_ref[h + 1][:, :n_cols]

        return carry

    gain_acc_ref[...] = jnp.zeros(gain_acc_ref.shape, F32)
    lax.fori_loop(0, n_rows + 2, hide, 0)
    one_at = 3 * n_hidden

    def first_grad(f, carry):
        left = pre_grad_ref[pl.ds(f, 3)].reshape(3 * own, n_cols)
        acc_ref[:, one_at : one_at + 3 * chans] += dot_nt(left, taps_ref[f + 1][:, :n_cols])
        return carry

    lax.fori_loop(0, n_rows + 2, first_grad, 0)
    gain_at = one_at + 3 * chans
    gain_grad = jnp.sum(gain_acc_ref[...], axis=1, keepdims=True)
    grads_ref[:, 0:gain_at] = acc_ref[:, 0:gain_at].astype(BF16)
    tail = grads_ref.shape[1] - gain_at
    high = gain_grad.astype(BF16).astype(F32)
    low = gain_grad - high
    spread = jnp.where(iota((own, tail), 1) == 0, high, low).astype(BF16)
    grads_ref[0:own, gain_at:] = spread
    grads_ref[own:, gain_at:] = jnp.zeros((2 * own, tail), BF16)


def grads(index, kernel, gain, feats, halo, cot, back_out):
    n_rows, own, n_cols = cot.shape
    n_hidden = kernel.shape[0]
    chans = kernel.shape[1] // 9
    width = n_cols + LANES
    lanes = -(-(3 * n_hidden + 3 * chans + 2) // LANES) * LANES
    return call(
        grads_kernel,
        [
            jax.ShapeDtypeStruct((n_rows + 2, 3 * n_hidden, n_cols), BF16),
            jax.ShapeDtypeStruct((3 * own, lanes), BF16),
        ],
        [smem_spec()] + [vmem_spec()] * 6,
        [
            pltpu.VMEM((n_rows + 4, 3 * chans, width), BF16),
            pltpu.VMEM((n_rows + 4, 1, width), F32),
            pltpu.VMEM((n_hidden, n_cols), F32),
            pltpu.VMEM((8, LANES), BF16),
            pltpu.VMEM((n_rows + 4, own, n_cols), BF16),
            pltpu.VMEM((n_rows + 4, own, n_cols), BF16),
            pltpu.VMEM((own, n_cols), F32),
            pltpu.VMEM((3 * own, lanes), F32),
        ],
        2 * (n_rows + 2) * 9 * n_cols * n_hidden * (own + chans),
        (n_rows + 2) * 3 * n_hidden * n_cols * 2,
        "grads",
    )(index, kernel, gain, feats, halo, cot, back_out)


def encode_kernel(kernel_ref, hidden_ref, out_ref, acc_ref):
    n_ext = hidden_ref.shape[0]
    n_rows = n_ext - 2
    own = out_ref.shape[1]
    acc_ref[...] = jnp.zeros(acc_ref.shape, F32)

    def one(h, carry):
        part = dot_nn(kernel_ref[...], hidden_ref[h])
        for a in range(3):
            acc_ref[h - a + 2] += part[a * own : (a + 1) * own]
        return carry

    lax.fori_loop(0, n_ext, one, 0)
    out_ref[...] = acc_ref[2 : 2 + n_rows].astype(BF16)


def encode(kernel, hidden):
    n_ext, _, n_cols = hidden.shape
    own = kernel.shape[0] // 3
    return call(
        encode_kernel,
        jax.ShapeDtypeStruct((n_ext - 2, own, n_cols), BF16),
        [vmem_spec()] * 2,
        [pltpu.VMEM((n_ext + 2, own, n_cols), F32)],
        2 * n_ext * kernel.shape[0] * kernel.shape[1] * n_cols,
        hidden.size * 2,
        "encode",
    )(kernel, hidden)


def step_perm(count, by):
    return [(i, i + by) for i in range(count) if 0 <= i + by < count]


def swap_sub(x):
    return lax.ppermute(x, "sub", [(0, 1), (1, 0)])


def swap_chan(x):
    return lax.ppermute(x, "chan", [(0, 1), (1, 0)])


def with_rows(block, depth, n_tile):
    low = lax.ppermute(block[-depth:], "tile", step_perm(n_tile, 1))
    high = lax.ppermute(block[:depth], "tile", step_perm(n_tile, -1))
    return jnp.concatenate([low, block, high], axis=0)


def side_halo(block, sub):
    n_cols = block.shape[-1]
    near = jnp.where(sub == 0, block[..., n_cols - LANES :], block[..., :LANES])
    return swap_sub(near)


def body(obs_values, obs_weight, obs_tile, obs_cell, conv_one, conv_two, density_gain, cotangent):
    own, n_rows, n_cols = cotangent.shape
    n_tile = lax.axis_size("tile")
    n_sub = lax.axis_size("sub")
    n_chan = lax.axis_size("chan")
    n_tiles = n_tile * n_sub
    chans = obs_values.shape[1]
    n_hidden = own * n_chan
    cap = 2 * obs_values.shape[0] // n_tiles
    tile, chan, sub = lax.axis_index("tile"), lax.axis_index("chan"), lax.axis_index("sub")
    index = jnp.stack([tile, chan, sub, jnp.int32(n_tile)]).astype(jnp.int32)

    cot = cotangent.transpose(1, 0, 2)
    cot_ext = with_rows(cot, 1, n_tile)
    if n_chan == 2:
        cot_peer = swap_chan(cot_ext)
        cot_pair = jnp.concatenate([cot_ext, cot_peer], axis=1)
    else:
        cot_peer = None
        cot_ext = lax.all_gather(cot_ext, "chan", axis=1, tiled=True)
        cot_pair = cot_ext
    cot_halo = side_halo(cot_pair, sub)

    columns = lax.all_to_all(conv_two, "chan", split_axis=3, concat_axis=2, tiled=True)
    if n_chan == 2:
        columns = jnp.where(chan == 0, columns, jnp.roll(columns, own, axis=2))
    back_weights = columns.transpose(0, 3, 1, 2).reshape(3 * own, 3 * n_hidden)
    code_weights = conv_two.transpose(0, 2, 1, 3).reshape(3 * own, 3 * n_hidden)
    one_full = lax.all_gather(conv_one, "chan", axis=2, tiled=True)
    one_weights = one_full.transpose(2, 0, 1, 3).reshape(n_hidden, 9 * chans)
    gain = lax.all_gather(density_gain, "chan", axis=0, tiled=True)[:, None]

    sent = route(obs_values, obs_weight, obs_tile, obs_cell, n_tiles, cap)
    got = lax.all_to_all(sent, ("tile", "sub"), split_axis=0, concat_axis=0, tiled=True)
    back_out = back(index, back_weights, cot_ext, cot_peer, cot_halo, n_cols)
    part, message = grid(got, n_rows, n_cols)
    data_rows = n_rows * chans
    data = part[:data_rows]
    density = part[data_rows : data_rows + n_rows]
    if n_chan == 2:
        other = swap_chan(message).astype(F32)
        data = data + other[:data_rows]
        density = density + (
            other[data_rows : data_rows + n_rows] + other[data_rows + n_rows :]
        )
    else:
        data, density = lax.psum((data, density), "chan")
    features = data.reshape(n_rows, chans, n_cols) / (1.0 + density)[:, None]
    high = density.astype(BF16)
    low = (density - high.astype(F32)).astype(BF16)
    packed = jnp.concatenate(
        [
            features.astype(BF16),
            high[:, None],
            low[:, None],
            jnp.zeros((n_rows, META - 2, n_cols), BF16),
        ],
        axis=1,
    )
    feats = with_rows(packed, 2, n_tile)
    feats_halo = side_halo(feats, sub)

    hidden, partial = grads(index, one_weights, gain, feats, feats_halo, cot, back_out)

    half = partial.shape[0] // 2
    keep = jnp.where(sub == 0, partial[:half], partial[half:])
    give = jnp.where(sub == 0, partial[half:], partial[:half])
    mine = (keep.astype(F32) + swap_sub(give).astype(F32)).astype(BF16)
    lanes = mine.shape[1]
    spread = lax.all_to_all(
        mine.reshape(n_tile, half // n_tile, lanes), "tile", 0, 0, tiled=True
    )
    mine = jnp.sum(spread.astype(F32), axis=0).astype(BF16)
    mine = lax.all_to_all(
        jnp.broadcast_to(mine[None], (n_tile,) + mine.shape), "tile", 0, 0, tiled=True
    ).reshape(half, lanes)
    other = swap_sub(mine)
    first = jnp.where(sub == 0, mine, other)
    second = jnp.where(sub == 0, other, mine)
    total = jnp.concatenate([first, second], axis=0).astype(F32)

    encoded = encode(code_weights, hidden).transpose(1, 0, 2)

    scale = 1.0 / math.sqrt(n_tiles * n_rows * n_cols)
    total = total * scale
    one_at = 3 * n_hidden
    gain_at = one_at + 3 * chans
    grad_two = total[:, :one_at].reshape(3, own, 3, n_hidden).transpose(0, 2, 1, 3)[::-1]
    grad_one = total[:, one_at:gain_at].reshape(3, own, 3, chans).transpose(0, 2, 1, 3)[::-1]
    grad_gain = total[:own, gain_at] + total[:own, gain_at + 1]
    return encoded, grad_one, grad_two, grad_gain


def solution(mesh):
    placed = (
        P(("member", "tile", "chan", "sub"), None),
        P(("member", "tile", "chan", "sub")),
        P(("member", "tile", "chan", "sub")),
        P(("member", "tile", "chan", "sub")),
        P(None, None, "chan", None),
        P(None, None, "chan", None),
        P("chan"),
        P(("member", "chan"), "tile", "sub"),
    )
    return jax.shard_map(
        body,
        mesh=mesh,
        in_specs=placed,
        out_specs=(
            P(("member", "chan"), "tile", "sub"),
            P("member", None, "chan", None),
            P("member", None, "chan", None),
            P(("member", "chan")),
        ),
        check_vma=False,
    )
```

time: 500 us -> 203 us (0.41); the launches traced: 491 us -> 203 us
  local copies, waits for them, and re-layouts: 174 us -> 19.7 us
  waiting for transfers between devices: 139 us -> 27.5 us
  matrix products: 70 us -> 0 us
  Pallas kernels: 0 us -> 58.8 us
  blocking collectives: 21.6 us -> 55.7 us
  other arithmetic: 25.3 us -> 7.73 us
  starting transfers between devices: 46.1 us -> 32.2 us
  between operations: 14.9 us -> 1.03 us
    gather x4 -> x0, local copies, waits for them, and re-layouts: 122 us -> none  [the longest x1 50.7 us: body(): jnp.take(obs_weight, pick)]
    psum x2 -> x0, waiting for transfers between devices: 79.4 us -> none  [the longest x1 54.1 us: body(): lax.psum((grad_one, grad_two, grad_gain), ('tile', 'sub'))]
    dot_general x61 -> x0, matrix products: 70 us -> none  [the longest x9 18.1 us: back_apply(): jnp.einsum('oc,ohw->chw', kernel_cols[row_off, col_off], window, preferre...]
    pallas_call x0 -> x5, Pallas kernels: none -> 58.8 us  [the longest x1 20 us: grads(): call(grads_kernel, [jax.ShapeDtypeStruct((n_rows + 2, 3 * n_hidden, n_col...]
    all_to_all x0 -> x2, blocking collectives: none -> 29.1 us  [the longest x1 14.9 us: body(): lax.all_to_all(mine.reshape(n_tile, half // n_tile, lanes), 'tile', 0, 0,...]
    all_gather x0 -> x2, blocking collectives: none -> 26.6 us  [the longest x1 22.4 us: body(): one_full = lax.all_gather(conv_one, 'chan', axis=2, tiled=True)]
    all_gather x2 -> x0, waiting for transfers between devices: 25.9 us -> none  [the longest x1 25.9 us: body(): hidden_pad = lax.all_gather(hidden_own, 'chan', axis=0, tiled=True)]
    psum x2 -> x0, blocking collectives: 21.6 us -> none  [the longest x1 14.7 us: body(): lax.psum((grad_one, grad_two, grad_gain), ('tile', 'sub'))]
  transfers between devices with their start and end apart: 20 -> 12, of which waited for: 10 -> 5; matrix products, arithmetic and copies ran while one was open for 33% -> 7% of each run, Pallas kernels for 0% -> 13%
where the time goes in v1:
time: 203 us
  Pallas kernels  58.8 us (29%)
  blocking collectives  55.7 us (27%)
  starting transfers between devices  32.2 us (16%)
  waiting for transfers between devices  27.5 us (14%)
  local copies, waits for them, and re-layouts  19.7 us (10%)
  other arithmetic  7.73 us (4%)
    all_gather x1, blocking collectives, body(): one_full = lax.all_gather(conv_one, 'chan', axis=2, tiled=True)  22.4 us
    pallas_call x1, Pallas kernels, grads(): call(grads_kernel, [jax.ShapeDtypeStruct((n_rows + 2, 3 * n_hidden, n_col...  20 us
    ppermute x2, waiting for transfers between devices, with_rows(): low = lax.ppermute(block[-depth:], 'tile', step_perm(n_tile, 1))  18.3 us
    ppermute x2, starting transfers between devices, with_rows(): low = lax.ppermute(block[-depth:], 'tile', step_perm(n_tile, 1))  15.5 us
    all_to_all x1, blocking collectives, body(): lax.all_to_all(mine.reshape(n_tile, half // n_tile, lanes), 'tile', 0, 0,...  14.9 us
    all_to_all x1, blocking collectives, body(): lax.all_to_all(jnp.broadcast_to(mine[None], (n_tile,) + mine.shape), 'til...  14.2 us
    unnamed x34, local copies, waits for them, and re-layouts  12.2 us
    pallas_call x1, Pallas kernels, route(): call(functools.partial(route_kernel, n_tiles, cap), jax.ShapeDtypeStruct(...  12 us
  transfers between devices with their start and end apart: 12, of which 5 were waited for; matrix products, arithmetic and copies ran while one was open for 7% of the time, Pallas kernels for 13%

profile of v1, /device:TPU:0, one launch (start us, length us, event | category | flops | bytes accessed | tf_op | source)
XLA Modules:
  0.0 202.7 jit_solution(1834482754920417145)
XLA Ops:
  0.7 2.4 %copy.47.values_ref = bf16[4096,64]{1,0:T(8,128)(2,1)} copy(bf16[4096,64]{0,1:T(8,128)(2,1)} %param.8) | data formatting | bytes 1048576 | tf_op args[0]
  4.9 12.0 %route.1 = bf16[8,72,1024]{2,1,0:T(8,128)(2,1)} custom-call(s32[16,256]{1,0:T(8,128)} %reshape.48.tile_ref, f32[16,256]{1,0:T(8,128)} %reshape.59.weight_ref, s32[16,256]{1,0:T(8,128)} %reshape.51.cell_ref, bf16[4096,64]{1,0:T(8,128)(2,1)} %copy.47.values_ref), custom_call_target="tpu_custom_call" | custom-call | flops 1342177280 | bytes 1179648 | tf_op jit(solution)/shard_map/route/pallas_call | solution.py:154
  16.9 6.5 %all-to-all-start = ((bf16[8,72,1024]{2,1,0:T(8,128)(2,1)}), bf16[8,72,1024]{2,1,0:T(8,128)(2,1)S(1)}, u32[]{:S(2)}, u32[]{:S(2)}) async-start(bf16[8,72,1024]{2,1,0:T(8,128)(2,1)} %route.1), calls=%async_computation | async-start | bytes 2359296 | tf_op jit(solution)/shard_map/all_to_all | solution.py:480
  23.5 4.1 %collective-permute-start.4 = (bf16[1,128,384]{2,1,0:T(8,128)(2,1)S(1)}, bf16[1,128,384]{2,1,0:T(8,128)(2,1)S(1)}, u32[]{:S(2)}, u32[]{:S(2)}) collective-permute-start(bf16[1,128,384]{2,1,0:T(8,128)(2,1)S(1)} %get-tuple-element.32), channel_id=1, source_target_pairs={{0,4},{4,8},{8,12},{1,5},{5,9},{9,13},{2,6},{6,10},{10,14},{3,7},{... | collective-permute-start | bytes 294920 | tf_op jit(solution)/shard_map/ppermute | solution.py:436
  27.6 1.3 collective-permute-start.5
  28.9 16.7 %collective-permute-done.4 = bf16[1,128,384]{2,1,0:T(8,128)(2,1)S(1)} collective-permute-done((bf16[1,128,384]{2,1,0:T(8,128)(2,1)S(1)}, bf16[1,128,384]{2,1,0:T(8,128)(2,1)S(1)}, u32[]{:S(2)}, u32[]{:S(2)}) %collective-permute-start.4) | collective-permute-done | bytes 98336 | tf_op jit(solution)/shard_map/ppermute | solution.py:436
  46.7 1.5 collective-permute-start.6
  49.5 3.8 %all-to-all-done.got_ref = bf16[8,72,1024]{2,1,0:T(8,128)(2,1)S(1)} async-done(((bf16[8,72,1024]{2,1,0:T(8,128)(2,1)}), bf16[8,72,1024]{2,1,0:T(8,128)(2,1)S(1)}, u32[]{:S(2)}, u32[]{:S(2)}) %all-to-all-start) | async-done | bytes 1179680 | tf_op jit(solution)/shard_map/all_to_all | solution.py:480
  54.2 3.5 %all-to-all-start.1 = ((bf16[3,3,128,256]{2,1,0,3:T(4,128)(2,1)}), bf16[3,3,128,256]{2,1,0,3:T(4,128)(2,1)S(1)}, u32[]{:S(2)}, u32[]{:S(2)}) async-start(bf16[3,3,128,256]{2,1,0,3:T(4,128)(2,1)} %copy.51), calls=%async_computation.1 | async-start | bytes 1572864 | tf_op jit(solution)/shard_map/all_to_all | solution.py:470
  57.8 8.6 %grid.1 = (f32[528,384]{1,0:T(8,128)}, bf16[528,384]{1,0:T(8,128)(2,1)}) custom-call(bf16[8,72,1024]{2,1,0:T(8,128)(2,1)} %copy-done.5), custom_call_target="tpu_custom_call" | custom-call | flops 3321888768 | bytes 1179648 | tf_op jit(solution)/shard_map/grid/pallas_call | solution.py:215
  66.4 2.0 collective-permute-start
  68.4 22.4 %all_gather.6 = bf16[3,3,256,64]{2,3,1,0:T(8,128)(2,1)S(1)} all-gather(bf16[3,3,128,64]{2,3,1,0:T(8,128)(2,1)S(1)} %copy-done.8), channel_id=1, replica_groups=mesh['member'=2,'tile'=4,'chan'=2,'sub'=2] {'chan'}, dimensions={2}, use_global_device_ids=true | all-gather | bytes 442368 | tf_op jit(solution)/shard_map/all_gather | solution.py:475
  91.7 4.2 %all-gather = f32[2,1,128]{2,1,0:T(1,128)S(1)} all-gather(f32[1,1,128]{2,1,0:T(1,128)S(1)} %bitcast.58), channel_id=1, replica_groups=mesh['member'=2,'tile'=4,'chan'=2,'sub'=2] {'chan'}, dimensions={0}, use_global_device_ids=true | all-gather | bytes 1536 | tf_op jit(solution)/shard_map/all_gather | solution.py:477
  97.8 2.2 %fusion = bf16[10,256,128]{2,1,0:T(8,128)(2,1)} fusion(bf16[10,128,384]{2,1,0:T(8,128)(2,1)} %collective-permute-done.6.peer_ref, bf16[1,128,384]{2,1,0:T(8,128)(2,1)S(1)} %collective-permute-done.5, bf16[8,128,384]{2,1,0:T(8,128)(2,1)S(1)} %bitcast.41, bf16[1,128,384]{2,1,0:T(8,128)(2,1)S(1)} %collective-permute-done.4, pred[]{:T(512)S(6)} %eq.4), kind=kLoop, calls=%fused_computation.8 | loop fusion | flops 5570560 | bytes 2621441 | tf_op jit(solution)/shard_map/jit(_where)/select_n | solution.py:443
  100.4 11.5 %collective-permute-start.1 = (bf16[2,72,384]{2,1,0:T(8,128)(2,1)S(1)}, bf16[2,72,384]{2,1,0:T(8,128)(2,1)S(1)}, u32[]{:S(2)}, u32[]{:S(2)}) collective-permute-start(bf16[2,72,384]{2,1,0:T(8,128)(2,1)S(1)} %get-tuple-element.36), channel_id=1, source_target_pairs={{0,4},{4,8},{8,12},{1,5},{5,9},{9,13},{2,6},{6,10},{10,14},{3,7},{... | collective-permute-start | bytes 331784 | tf_op jit(solution)/shard_map/ppermute | solution.py:436
  113.2 1.6 collective-permute-done.1
  114.8 4.1 %collective-permute-done.2 = bf16[2,72,384]{2,1,0:T(8,128)(2,1)S(1)} collective-permute-done((bf16[2,72,384]{2,1,0:T(8,128)(2,1)S(1)}, bf16[2,72,384]{2,1,0:T(8,128)(2,1)S(1)}, u32[]{:S(2)}, u32[]{:S(2)}) %collective-permute-start.2) | collective-permute-done | bytes 110624 | tf_op jit(solution)/shard_map/ppermute | solution.py:437
  121.6 9.5 %back.1.back_ref = f32[8,128,384]{2,1,0:T(8,128)} custom-call(s32[4]{0:T(128)} %pad_add_fusion.index_ref, bf16[384,768]{1,0:T(8,128)(2,1)} %bitcast.55, bf16[10,128,384]{2,1,0:T(8,128)(2,1)} %pad_maximum_fusion.own_ref, bf16[10,128,384]{2,1,0:T(8,128)(2,1)} %collective-permute-done.6.peer_ref, bf16[10,256,128]{2,1,0:T(8,128)(2,1)} %collective-permute-done.7.halo_ref), custom_call_target="tpu_custom_call" | custom-call | flops 2264924160 | bytes 1966080 | tf_op jit(solution)/shard_map/back/pallas_call | solution.py:273
  131.1 20.0 %grads.1 = (bf16[10,768,384]{2,1,0:T(8,128)(2,1)}, bf16[384,1024]{1,0:T(8,128)(2,1)}) custom-call(s32[4]{0:T(128)} %pad_add_fusion.index_ref, bf16[256,576]{1,0:T(8,128)(2,1)} %copy.55.kernel_ref, f32[256,1]{1,0:T(8,128)} %copy.56.gain_ref, bf16[12,72,384]{2,1,0:T(8,128)(2,1)} %copy-done.4, bf16[12,72,128]{2,1,0:T(8,128)(2,1)} %collective-permute-done.3.halo_ref, ...), custom_call_target="tpu_custom_call" | custom-call | flops 3397386240 | bytes 5898240 | tf_op jit(solution)/shard_map/grads/pallas_call | solution.py:370
  153.0 1.3 collective-permute-done.8
  154.5 14.9 %all_to_all.33 = bf16[4,48,1024]{2,1,0:T(8,128)(2,1)S(1)} all-to-all(bf16[4,48,1024]{2,1,0:T(8,128)(2,1)S(1)} %bitcast.51), channel_id=1, replica_groups=mesh['member'=2,'tile'=4,'chan'=2,'sub'=2] {'tile'}, dimensions={0} | all-to-all | bytes 786432 | tf_op jit(solution)/shard_map/all_to_all | solution.py:516
  169.5 14.2 %all_to_all.34 = bf16[4,48,1024]{2,1,0:T(8,128)(2,1)S(1)} all-to-all(bf16[4,48,1024]{2,1,0:T(8,128)(2,1)S(1)} %broadcast_in_dim.23), channel_id=1, replica_groups=mesh['member'=2,'tile'=4,'chan'=2,'sub'=2] {'tile'}, dimensions={0} | all-to-all | bytes 786432 | tf_op jit(solution)/shard_map/all_to_all | solution.py:520
  185.1 8.8 %encode.1 = bf16[8,128,384]{2,1,0:T(8,128)(2,1)} custom-call(bf16[384,768]{1,0:T(8,128)(2,1)} %bitcast.56, bf16[10,768,384]{2,1,0:T(8,128)(2,1)} %get-tuple-element.10.hidden_ref), custom_call_target="tpu_custom_call" | custom-call | flops 2264924160 | bytes 5898240 | tf_op jit(solution)/shard_map/encode/pallas_call | solution.py:412
  193.9 2.5 %copy.58 = bf16[128,8,384]{2,1,0:T(8,128)(2,1)} copy(bf16[128,8,384]{2,0,1:T(8,128)(2,1)} %bitcast.54) | data formatting | bytes 1572864
  (84 shorter events, 22.3 us)
Async XLA Ops:
  0.6 2.4 %copy-start.9 = (s32[4096]{0:T(1024)S(1)}, s32[4096]{0:T(1024)}, u32[]{:S(2)}) copy-start(s32[4096]{0:T(1024)} %param.10) | copy-start | bytes 49156
  0.6 3.0 %copy-start.10 = (s32[4096]{0:T(1024)S(1)}, s32[4096]{0:T(1024)}, u32[]{:S(2)}) copy-start(s32[4096]{0:T(1024)} %param.11) | copy-start | bytes 49156
  0.7 3.6 %copy-start.11 = (bf16[4096]{0:T(1024)(128)(2,1)S(1)}, bf16[4096]{0:T(1024)(128)(2,1)}, u32[]{:S(2)}) copy-start(bf16[4096]{0:T(1024)(128)(2,1)} %param.9) | copy-start | bytes 24580
  16.9 6.5 %copy-start.7 = (bf16[128,8,384]{2,1,0:T(8,128)(2,1)S(1)}, bf16[128,8,384]{2,1,0:T(8,128)(2,1)}, u32[]{:S(2)}) copy-start(bf16[128,8,384]{2,1,0:T(8,128)(2,1)} %param.15) | copy-start | bytes 2359300
  16.9 36.3 %all-to-all-start = ((bf16[8,72,1024]{2,1,0:T(8,128)(2,1)}), bf16[8,72,1024]{2,1,0:T(8,128)(2,1)S(1)}, u32[]{:S(2)}, u32[]{:S(2)}) async-start(bf16[8,72,1024]{2,1,0:T(8,128)(2,1)} %route.1), calls=%async_computation | async-start | bytes 2359296 | tf_op jit(solution)/shard_map/all_to_all | solution.py:480
  23.5 74.3 %copy-start = (bf16[128,8,384]{2,0,1:T(8,128)(2,1)}, bf16[128,8,384]{2,0,1:T(8,128)(2,1)S(1)}, u32[]{:S(2)}) copy-start(bf16[128,8,384]{2,0,1:T(8,128)(2,1)S(1)} %copy.64) | copy-start | bytes 2359300
  23.5 24.7 %copy-start.3 = (bf16[3,3,128,256]{3,2,1,0:T(8,128)(2,1)S(1)}, bf16[3,3,128,256]{3,2,1,0:T(8,128)(2,1)}, u32[]{:S(2)}) copy-start(bf16[3,3,128,256]{3,2,1,0:T(8,128)(2,1)} %param.13) | copy-start | bytes 1769476
  23.5 22.0 %collective-permute-start.4 = (bf16[1,128,384]{2,1,0:T(8,128)(2,1)S(1)}, bf16[1,128,384]{2,1,0:T(8,128)(2,1)S(1)}, u32[]{:S(2)}, u32[]{:S(2)}) collective-permute-start(bf16[1,128,384]{2,1,0:T(8,128)(2,1)S(1)} %get-tuple-element.32), channel_id=1, source_target_pairs={{0,4},{4,8},{8,12},{1,5},{5,9},{9,13},{2,6},{6,10},{10,14},{3,7},{... | collective-permute-start | bytes 294920 | tf_op jit(solution)/shard_map/ppermute | solution.py:436
  27.6 18.0 %collective-permute-start.5 = (bf16[1,128,384]{2,1,0:T(8,128)(2,1)S(1)}, bf16[1,128,384]{2,1,0:T(8,128)(2,1)S(1)}, u32[]{:S(2)}, u32[]{:S(2)}) collective-permute-start(bf16[1,128,384]{2,1,0:T(8,128)(2,1)S(1)} %get-tuple-element.33), channel_id=1, source_target_pairs={{4,0},{8,4},{12,8},{5,1},{9,5},{13,9},{6,2},{10,6},{14,10},{7,3},{... | collective-permute-start | bytes 294920 | tf_op jit(solution)/shard_map/ppermute | solution.py:437
  46.7 51.1 %collective-permute-start.6 = (bf16[10,128,384]{2,1,0:T(8,128)(2,1)}, bf16[10,128,384]{2,1,0:T(8,128)(2,1)}, u32[]{:S(2)}, u32[]{:S(2)}) collective-permute-start(bf16[10,128,384]{2,1,0:T(8,128)(2,1)} %pad_maximum_fusion.own_ref), channel_id=1, source_target_pairs={{0,2},{2,0},{1,3},{3,1},{4,6},{6,4},{5,7},{7,5},{8,10},{10,8},{9,1... | collective-permute-start | bytes 2949128 | tf_op jit(solution)/shard_map/ppermute | solution.py:432
  54.2 43.1 %all-to-all-start.1 = ((bf16[3,3,128,256]{2,1,0,3:T(4,128)(2,1)}), bf16[3,3,128,256]{2,1,0,3:T(4,128)(2,1)S(1)}, u32[]{:S(2)}, u32[]{:S(2)}) async-start(bf16[3,3,128,256]{2,1,0,3:T(4,128)(2,1)} %copy.51), calls=%async_computation.1 | async-start | bytes 1572864 | tf_op jit(solution)/shard_map/all_to_all | solution.py:470
  57.8 10.6 %copy-start.8 = (bf16[3,3,128,64]{2,3,1,0:T(8,128)(2,1)S(1)}, bf16[3,3,128,64]{2,3,1,0:T(8,128)(2,1)}, u32[]{:S(2)}) copy-start(bf16[3,3,128,64]{2,3,1,0:T(8,128)(2,1)} %param.12) | copy-start | bytes 442372
  57.8 33.9 %copy-start.12 = (f32[128]{0:T(128)S(1)}, f32[128]{0:T(128)}, u32[]{:S(2)}) copy-start(f32[128]{0:T(128)} %param.14) | copy-start | bytes 1540
  66.4 33.6 %collective-permute-start = (bf16[528,384]{1,0:T(8,128)(2,1)}, bf16[528,384]{1,0:T(8,128)(2,1)S(1)}, u32[]{:S(2)}, u32[]{:S(2)}) collective-permute-start(bf16[528,384]{1,0:T(8,128)(2,1)} %get-tuple-element.9), channel_id=1, source_target_pairs={{0,2},{2,0},{1,3},{3,1},{4,6},{6,4},{5,7},{7,5},{8,10},{10,8},{9,1... | collective-permute-start | bytes 1216520 | tf_op jit(solution)/shard_map/ppermute | solution.py:432
  97.8 2.3 %copy-start.6 = (f32[528,384]{1,0:T(8,128)S(1)}, f32[528,384]{1,0:T(8,128)}, u32[]{:S(2)}) copy-start(f32[528,384]{1,0:T(8,128)} %get-tuple-element.8) | copy-start | bytes 2433028
  100.0 21.7 %collective-permute-start.7 = (bf16[10,256,128]{2,1,0:T(8,128)(2,1)}, bf16[10,256,128]{2,1,0:T(8,128)(2,1)}, u32[]{:S(2)}, u32[]{:S(2)}) collective-permute-start(bf16[10,256,128]{2,1,0:T(8,128)(2,1)} %fusion), channel_id=1, source_target_pairs={{0,1},{1,0},{2,3},{3,2},{4,5},{5,4},{6,7},{7,6},{8,9},{9,8},{10,11... | collective-permute-start | bytes 1966088 | tf_op jit(solution)/shard_map/ppermute | solution.py:428
  100.4 14.4 %collective-permute-start.1 = (bf16[2,72,384]{2,1,0:T(8,128)(2,1)S(1)}, bf16[2,72,384]{2,1,0:T(8,128)(2,1)S(1)}, u32[]{:S(2)}, u32[]{:S(2)}) collective-permute-start(bf16[2,72,384]{2,1,0:T(8,128)(2,1)S(1)} %get-tuple-element.36), channel_id=1, source_target_pairs={{0,4},{4,8},{8,12},{1,5},{5,9},{9,13},{2,6},{6,10},{10,14},{3,7},{... | collective-permute-start | bytes 331784 | tf_op jit(solution)/shard_map/ppermute | solution.py:436
  111.8 7.1 %collective-permute-start.2 = (bf16[2,72,384]{2,1,0:T(8,128)(2,1)S(1)}, bf16[2,72,384]{2,1,0:T(8,128)(2,1)S(1)}, u32[]{:S(2)}, u32[]{:S(2)}) collective-permute-start(bf16[2,72,384]{2,1,0:T(8,128)(2,1)S(1)} %get-tuple-element.37), channel_id=1, source_target_pairs={{4,0},{8,4},{12,8},{5,1},{9,5},{13,9},{6,2},{10,6},{14,10},{7,3},{... | collective-permute-start | bytes 331784 | tf_op jit(solution)/shard_map/ppermute | solution.py:437
  119.0 1.7 copy-start.4
  119.8 11.3 %collective-permute-start.3 = (bf16[12,72,128]{2,1,0:T(8,128)(2,1)}, bf16[12,72,128]{2,1,0:T(8,128)(2,1)}, u32[]{:S(2)}, u32[]{:S(2)}) collective-permute-start(bf16[12,72,128]{2,1,0:T(8,128)(2,1)} %slice_select_fusion), channel_id=1, source_target_pairs={{0,1},{1,0},{2,3},{3,2},{4,5},{5,4},{6,7},{7,6},{8,9},{9,8},{10,11... | collective-permute-start | bytes 663560 | tf_op jit(solution)/shard_map/ppermute | solution.py:428
  151.2 3.2 %copy-start.2 = (bf16[384,1024]{1,0:T(8,128)(2,1)S(1)}, bf16[384,1024]{1,0:T(8,128)(2,1)}, u32[]{:S(2)}) copy-start(bf16[384,1024]{1,0:T(8,128)(2,1)} %get-tuple-element.11) | copy-start | bytes 2359300
  152.4 1.9 collective-permute-start.8
  183.7 12.7 %collective-permute-start.9 = (bf16[192,1024]{1,0:T(8,128)(2,1)S(1)}, bf16[192,1024]{1,0:T(8,128)(2,1)S(1)}, u32[]{:S(2)}, u32[]{:S(2)}) collective-permute-start(bf16[192,1024]{1,0:T(8,128)(2,1)S(1)} %bitcast.50), channel_id=1, source_target_pairs={{0,1},{1,0},{2,3},{3,2},{4,5},{5,4},{6,7},{7,6},{8,9},{9,8},{10,11... | collective-permute-start | bytes 1179656 | tf_op jit(solution)/shard_map/ppermute | solution.py:428
  199.5 1.2 slice-start
  (2 other events, 2.2 us)

commit v2 on v1

v2 whole, which is shorter than its diff:
```python
import functools
import math

import jax
import jax.numpy as jnp
from jax import lax
from jax.experimental import pallas as pl
from jax.experimental.pallas import tpu as pltpu
from jax.sharding import PartitionSpec as P

BF16 = jnp.bfloat16
F32 = jnp.float32
LANES = 128
BLOCK = 256
META = 8
MIB = 1024 * 1024


def dot_nt(a, b):
    return lax.dot_general(a, b, (((1,), (1,)), ((), ())), preferred_element_type=F32)


def dot_nn(a, b):
    return lax.dot_general(a, b, (((1,), (0,)), ((), ())), preferred_element_type=F32)


def iota(shape, dim, dtype=jnp.int32):
    return lax.broadcasted_iota(jnp.int32, shape, dim).astype(dtype)


def vmem_spec():
    return pl.BlockSpec(memory_space=pltpu.VMEM)


def smem_spec():
    return pl.BlockSpec(memory_space=pltpu.SMEM)


def call(kernel, out_shape, in_specs, scratch, flops, moved, name, vmem=48):
    n_out = len(out_shape) if isinstance(out_shape, (tuple, list)) else None
    out_specs = vmem_spec() if n_out is None else [vmem_spec() for _ in range(n_out)]
    return pl.pallas_call(
        kernel,
        out_shape=out_shape,
        in_specs=in_specs,
        out_specs=out_specs,
        scratch_shapes=scratch,
        compiler_params=pltpu.CompilerParams(vmem_limit_bytes=vmem * MIB),
        cost_estimate=pl.CostEstimate(flops=flops, bytes_accessed=moved, transcendentals=0),
        name=name,
    )


def route_kernel(n_tiles, cap, n_parts, tile_ref, weight_ref, cell_ref, values_ref, *rest):
    outs = rest[:n_parts]
    onehot_ref, slot_ref, weight32_ref, all_ref, info_ref, info_smem, sem = rest[n_parts:]
    n_lines = tile_ref.shape[0]
    n_blocks = n_lines // 2
    n_obs_chans = values_ref.shape[0]
    pairs = n_tiles * n_lines
    tiles = tile_ref[...]
    for t in range(n_tiles):
        onehot_ref[t * n_lines : (t + 1) * n_lines, :] = jnp.where(tiles == t, 1.0, 0.0).astype(BF16)
    onehot = onehot_ref[...]
    upper = jnp.where(
        iota((LANES, LANES), 0) <= iota((LANES, LANES), 1), 1.0, 0.0
    ).astype(BF16)
    here = iota((pairs, pairs), 0)
    there = iota((pairs, pairs), 1)
    earlier = jnp.where(
        (here // n_lines == there // n_lines) & (there < here), 1.0, 0.0
    ).astype(BF16)
    total_row = dot_nt(jnp.ones((8, LANES), BF16), onehot)
    offset_row = dot_nt(total_row.astype(BF16), earlier)
    base_row = jnp.minimum(jnp.floor(offset_row * (1.0 / LANES)) * LANES, float(cap - BLOCK))
    even = iota((8, pairs), 1) % 2 == 0
    base_pair = jnp.where(even, base_row, pltpu.roll(base_row, 1, 1))
    spill = jnp.where(offset_row + total_row > base_pair + BLOCK, 1.0, 0.0)
    any_spill = jnp.max(spill, axis=1, keepdims=True)
    info_ref[...] = jnp.where(
        iota((8, pairs), 0) == 0, base_row, any_spill
    ).astype(jnp.int32)
    copy = pltpu.make_async_copy(info_ref, info_smem, sem)
    copy.start()
    cum = dot_nn(onehot, upper)
    totals = dot_nn(onehot, jnp.ones((LANES, LANES), BF16))
    offset = dot_nn(earlier, totals.astype(BF16))
    place = cum + offset - 1.0
    slots = jnp.zeros(tiles.shape, F32)
    for t in range(n_tiles):
        slots = jnp.where(tiles == t, place[t * n_lines : (t + 1) * n_lines, :], slots)
    slot_ref[...] = slots
    weight32_ref[...] = weight_ref[...].astype(F32)
    all_ref[...] = jnp.zeros(all_ref.shape, BF16)
    meta_row = iota((16, BLOCK), 0)
    window = iota((BLOCK, BLOCK), 0, F32)
    copy.wait()

    def line(ref, b):
        return jnp.concatenate([ref[pl.ds(2 * b, 1), :], ref[pl.ds(2 * b + 1, 1), :]], axis=1)

    def columns(b):
        values = values_ref[:, pl.ds(pl.multiple_of(b * BLOCK, BLOCK), BLOCK)]
        cell = line(cell_ref, b)
        weight = line(weight32_ref, b)
        high = (cell // LANES).astype(F32)
        low = (cell % LANES).astype(F32)
        meta = jnp.where(
            meta_row == 0,
            weight,
            jnp.where(meta_row == 1, high, jnp.where(meta_row == 2, low, 0.0)),
        ).astype(BF16)
        return jnp.concatenate([values, meta], axis=0)

    def add(t, base, wide, key):
        chosen = jnp.where(window == key, 1.0, 0.0).astype(BF16)
        part = dot_nt(wide, chosen)[: n_obs_chans + META].astype(BF16)
        where = pl.ds(pl.multiple_of(base, LANES), BLOCK)
        all_ref[t, :, where] = all_ref[t, :, where] + part

    def first(b):
        wide = columns(b)
        tile = line(tile_ref, b)
        slot = line(slot_ref, b)
        for t in range(n_tiles):
            base = info_smem[0, t * n_lines + 2 * b]
            key = jnp.where(tile == t, slot - base.astype(F32), -1.0)
            add(t, base, wide, key)

    def first_two(i, carry):
        first(2 * i)
        first(2 * i + 1)
        return carry

    lax.fori_loop(0, n_blocks // 2, first_two, 0)

    if cap > BLOCK:

        @pl.when(info_smem[1, 0] > 0)
        def _():
            def second(b, carry):
                wide = columns(b)
                tile = line(tile_ref, b)
                slot = line(slot_ref, b)
                for t in range(n_tiles):
                    start = info_smem[0, t * n_lines + 2 * b]
                    base = jnp.minimum(start + BLOCK, cap - BLOCK)
                    far = (tile == t) & (slot >= (start + BLOCK).astype(F32))
                    key = jnp.where(far, slot - base.astype(F32), -1.0)
                    add(t, base, wide, key)
                return carry

            lax.fori_loop(0, n_blocks, second, 0)

    part = cap // n_parts
    for p in range(n_parts):
        outs[p][...] = all_ref[:, :, p * part : (p + 1) * part]


def route(obs_values, obs_weight, obs_tile, obs_cell, n_tiles, cap, n_parts):
    n_obs, chans = obs_values.shape
    n_lines = n_obs // LANES
    rows = chans + META
    return call(
        functools.partial(route_kernel, n_tiles, cap, n_parts),
        [jax.ShapeDtypeStruct((n_tiles, rows, cap // n_parts), BF16)] * n_parts,
        [vmem_spec()] * 4,
        [
            pltpu.VMEM((n_tiles * n_lines, LANES), BF16),
            pltpu.VMEM((n_lines, LANES), F32),
            pltpu.VMEM((n_lines, LANES), F32),
            pltpu.VMEM((n_tiles, rows, cap), BF16),
            pltpu.VMEM((8, n_tiles * n_lines), jnp.int32),
            pltpu.SMEM((8, n_tiles * n_lines), jnp.int32),
            pltpu.SemaphoreType.DMA,
        ],
        2 * n_obs * n_tiles * BLOCK * 80,
        n_tiles * rows * cap * 2,
        "route",
        24,
    )(
        obs_tile.reshape(n_lines, LANES),
        obs_weight.reshape(n_lines, LANES),
        obs_cell.reshape(n_lines, LANES),
        obs_values.T,
    )


def grid_kernel(n_rows, n_cols, group, first, last, got_ref, *rest):
    rest = list(rest)
    before_ref = None if first else rest.pop(0)
    own_ref = rest.pop(0)
    send_ref = rest.pop(0) if last else None
    left_ref, right_ref = rest
    n_send, rows, cap = got_ref.shape
    chans = rows - META
    per_row = n_cols // LANES
    columns = iota((n_cols, cap), 0, F32)
    row_ids = iota((META, cap), 0)
    total = None
    for g in range(n_send // group):
        slot = g % 2
        for i in range(group):
            s = g * group + i
            at = slice(i * cap, (i + 1) * cap)
            values = got_ref[s, 0:chans, :]
            meta = got_ref[s, chans:rows, :].astype(F32)
            weight = meta[0:1]
            high = meta[1:2]
            row = jnp.floor((high + 0.5) * (1.0 / per_row))
            column = (high - row * per_row) * LANES + meta[2:3]
            right_ref[slot, :, at] = jnp.where(columns == column, weight, 0.0).astype(BF16)
            for r in range(n_rows):
                mask = jnp.where(row == r, 1.0, 0.0)
                left_ref[slot, r * rows : r * rows + chans, at] = values * mask.astype(BF16)
                left_ref[slot, r * rows + chans : (r + 1) * rows, at] = jnp.where(
                    row_ids == 0, mask, 0.0
                ).astype(BF16)
        part = dot_nt(left_ref[slot], right_ref[slot])
        total = part if total is None else total + part
    if before_ref is not None:
        total = total + before_ref[...]
    own_ref[...] = total
    if last:
        line = iota((META, n_cols), 0)
        for r in range(n_rows):
            send_ref[r * rows : r * rows + chans, :] = own_ref[r * rows : r * rows + chans, :].astype(BF16)
            extra = own_ref[r * rows + chans : (r + 1) * rows, :]
            density = extra[0:1]
            high = density.astype(BF16).astype(F32)
            send_ref[r * rows + chans : (r + 1) * rows, :] = jnp.where(
                line == 0, high, jnp.where(line == 1, density - high, 0.0)
            ).astype(BF16)


def grid(got, before, last, n_rows, n_cols):
    n_send, rows, cap = got.shape
    group = 4
    total = n_rows * rows
    outs = [jax.ShapeDtypeStruct((total, n_cols), F32)]
    if last:
        outs.append(jax.ShapeDtypeStruct((total, n_cols), BF16))
    ins = [got] if before is None else [got, before]
    return call(
        functools.partial(grid_kernel, n_rows, n_cols, group, before is None, last),
        outs,
        [vmem_spec()] * len(ins),
        [
            pltpu.VMEM((2, total, group * cap), BF16),
            pltpu.VMEM((2, n_cols, group * cap), BF16),
        ],
        2 * n_send * cap * total * n_cols,
        n_send * rows * cap * 2,
        "grid_last" if last else "grid_part",
        32,
    )(*ins)


def lane_mask(shape, n_cols, sub, depth):
    lane = iota(shape, 1)
    width = n_cols + LANES
    keep_right = (lane >= n_cols) & (lane < n_cols + depth) & (sub == 0)
    keep_left = (lane >= width - depth) & (sub == 1)
    return (lane < n_cols) | keep_right | keep_left


def back_kernel(n_cols, n_pieces, index_ref, kernel_ref, *rest):
    pieces = [(rest[2 * i], rest[2 * i + 1]) for i in range(n_pieces)]
    side_ref, out_ref, wide_ref = rest[2 * n_pieces :]
    n_ext, all_chans = side_ref.shape[0], side_ref.shape[1]
    n_rows = n_ext - 2
    width = n_cols + LANES
    keep = lane_mask((1, width), n_cols, index_ref[2], 1)
    for h in range(n_ext):
        if h == 0 or h == n_ext - 1:
            mids = [edge[min(h, 1)] for _, edge in pieces]
        else:
            mids = [middle[h - 1] for middle, _ in pieces]
        mid = mids[0] if n_pieces == 1 else jnp.concatenate(mids, axis=0)
        ext = jnp.concatenate([mid, side_ref[h]], axis=1).astype(F32)
        ext = jnp.where(keep, ext, 0.0)
        at = slice(h * n_cols, (h + 1) * n_cols)
        wide_ref[0:all_chans, at] = pltpu.roll(ext, width - 1, 1)[:, :n_cols].astype(BF16)
        wide_ref[all_chans : 2 * all_chans, at] = mid
        wide_ref[2 * all_chans :, at] = pltpu.roll(ext, 1, 1)[:, :n_cols].astype(BF16)
    total = None
    for a in range(3):
        at = slice((2 - a) * n_cols, (2 - a + n_rows) * n_cols)
        part = dot_nn(kernel_ref[a], wide_ref[:, at])
        total = part if total is None else total + part
    out_ref[...] = total


def back(index, kernel, pieces, side, n_cols):
    n_ext, all_chans = side.shape[0], side.shape[1]
    n_out = kernel.shape[1]
    return call(
        functools.partial(back_kernel, n_cols, len(pieces)),
        jax.ShapeDtypeStruct((n_out, (n_ext - 2) * n_cols), F32),
        [smem_spec()] + [vmem_spec()] * (2 + 2 * len(pieces)),
        [pltpu.VMEM((3 * all_chans, n_ext * n_cols), BF16)],
        2 * n_ext * 9 * all_chans * n_out * n_cols,
        n_ext * all_chans * n_cols * 2,
        "back",
        32,
    )(index, kernel, *[x for piece in pieces for x in piece], side)


def grads_kernel(
    split, chans, index_ref, kernel_ref, gain_ref, own_ref, edge_ref, peer_ref, peer_edge_ref,
    side_ref, cot_ref, back_ref, hidden_ref, *rest,
):
    rest = list(rest)
    if split:
        keep_out, give_out = rest.pop(0), rest.pop(0)
    else:
        all_out = rest.pop(0)
    taps_ref, logs_ref, pre_ref, wide_ref, out_left_ref, pre_left_ref, acc_ref = rest
    n_rows, own, n_cols = cot_ref.shape
    n_hidden = kernel_ref.shape[1]
    rows = chans + META
    taps_rows = 3 * chans
    width = n_cols + LANES
    tile, chan, sub, n_tile = index_ref[0], index_ref[1], index_ref[2], index_ref[3]
    keep_two = lane_mask((1, width), n_cols, sub, 2)

    log_line = iota((16, width), 0)
    for i in range(n_rows + 4):
        if 2 <= i < n_rows + 2:
            mid = own_ref[i - 2]
            if peer_ref is not None:
                mid = mid + peer_ref[i - 2].astype(F32)
        else:
            e = i if i < 2 else i - n_rows
            mid = edge_ref[e].astype(F32)
            if peer_ref is not None:
                mid = mid + peer_edge_ref[e].astype(F32)
        side = side_ref[i, 0:rows].astype(F32)
        if peer_ref is not None:
            side = side + side_ref[i, rows : 2 * rows].astype(F32)
        ext = jnp.concatenate([mid, side], axis=1)
        density = ext[chans : chans + 1] + ext[chans + 1 : chans + 2]
        logs = jnp.log(1.0 + density)
        logs_ref[i] = logs
        shrink = jnp.where(keep_two, 1.0 / (1.0 + density), 0.0)
        feats = ext[0:chans] * shrink
        at = slice(i * width, (i + 1) * width)
        taps_ref[0:chans, at] = pltpu.roll(feats, 1, 1).astype(BF16)
        taps_ref[chans : 2 * chans, at] = feats.astype(BF16)
        taps_ref[2 * chans : taps_rows, at] = pltpu.roll(feats, width - 1, 1).astype(BF16)
        high = logs.astype(BF16).astype(F32)
        middle = (logs - high).astype(BF16).astype(F32)
        taps_ref[taps_rows:, at] = jnp.where(
            log_line == 0,
            high,
            jnp.where(log_line == 1, middle, jnp.where(log_line == 2, logs - high - middle, 0.0)),
        ).astype(BF16)

    nothing = jnp.zeros((own, n_cols), BF16)
    for h in range(n_rows + 2):
        for a in range(3):
            inside = 0 <= h - a < n_rows
            put = slice(a * own, (a + 1) * own)
            out_left_ref[put, h * n_cols : (h + 1) * n_cols] = cot_ref[h - a] if inside else nothing
            if not inside:
                pre_left_ref[put, h * width : h * width + n_cols] = nothing
        pre_left_ref[:, h * width + n_cols : (h + 1) * width] = jnp.zeros((3 * own, LANES), BF16)

    gain = gain_ref[...]
    keep_one = lane_mask((1, width), n_cols, sub, 1)
    group = 2
    for first in range(0, n_rows + 2, group):
        pre_all = None
        for a in range(3):
            at = slice((first + a) * width, (first + a + group) * width)
            part = dot_nn(kernel_ref[a], taps_ref[0:taps_rows, at])
            pre_all = part if pre_all is None else pre_all + part
        for k in range(group):
            h = first + k
            pre = pre_all[:, k * width : (k + 1) * width] + gain * logs_ref[h + 1]
            at = slice(h * n_cols, (h + 1) * n_cols)
            keep = keep_one
            if h == 0:
                keep = keep & (tile > 0)
            elif h == n_rows + 1:
                keep = keep & (tile < n_tile - 1)
            else:
                pre_ref[:, (h - 1) * n_cols : h * n_cols] = pre[:, :n_cols]
            half = 0.5 * pre
            hidden = jnp.where(keep, half + half * jnp.tanh(half), 0.0)
            hidden_ref[h] = hidden.astype(BF16)
            wide_ref[0:n_hidden, at] = pltpu.roll(hidden, 1, 1)[:, :n_cols].astype(BF16)
            wide_ref[n_hidden : 2 * n_hidden, at] = hidden[:, :n_cols].astype(BF16)
            wide_ref[2 * n_hidden :, at] = pltpu.roll(hidden, width - 1, 1)[:, :n_cols].astype(BF16)

    for r in range(n_rows):
        at = slice(r * n_cols, (r + 1) * n_cols)
        mine = pre_ref[pl.ds(pl.multiple_of(chan * own, own), own), at]
        s = 0.5 + 0.5 * jnp.tanh(0.5 * mine)
        grad = (back_ref[:, at] * s * (1.0 + mine * (1.0 - s))).astype(BF16)
        for a in range(3):
            h = r + a
            pre_left_ref[a * own : (a + 1) * own, h * width : h * width + n_cols] = grad

    three = 3 * own
    lanes = 3 * n_hidden
    half_rows = taps_rows // 2
    acc_ref[0:three, :] = dot_nt(out_left_ref[...], wide_ref[...])
    one = dot_nt(taps_ref[:, width : (n_rows + 3) * width], pre_left_ref[...])
    acc_ref[three:, :] = jnp.zeros((acc_ref.shape[0] - three, lanes), F32)
    acc_ref[three : three + half_rows, 0:three] = one[0:half_rows]
    acc_ref[three : three + half_rows, lanes // 2 : lanes // 2 + three] = one[half_rows:taps_rows]
    gains = one[taps_rows : taps_rows + 1] + one[taps_rows + 1 : taps_rows + 2] + one[taps_rows + 2 : taps_rows + 3]
    acc_ref[three + half_rows : three + half_rows + 1, 0:three] = gains
    if split:
        half = acc_ref.shape[0] // 2
        keep_out[...] = acc_ref[pl.ds(pl.multiple_of(sub * half, half), half), :]
        give_out[...] = acc_ref[pl.ds(pl.multiple_of((1 - sub) * half, half), half), :].astype(BF16)
    else:
        all_out[...] = acc_ref[...]


def grads(split, index, kernel, gain, own, edge, peer, peer_edge, side, cot, back_out):
    n_rows, n_own, n_cols = cot.shape
    n_hidden = kernel.shape[1]
    chans = kernel.shape[2] // 3
    width = n_cols + LANES
    lanes = 3 * n_hidden
    acc_rows = 3 * n_own + 3 * chans // 2 + 32
    body = functools.partial(grads_kernel, split, chans)
    ins = [own, edge, peer, peer_edge, side, cot, back_out]
    if peer is None:
        ins = [own, edge, side, cot, back_out]
        body = lambda i, k, g, o, e, *rest: grads_kernel(split, chans, i, k, g, o, e, None, None, *rest)
    outs = [jax.ShapeDtypeStruct((n_rows + 2, n_hidden, width), BF16)]
    if split:
        outs.append(jax.ShapeDtypeStruct((acc_rows // 2, lanes), F32))
        outs.append(jax.ShapeDtypeStruct((acc_rows // 2, lanes), BF16))
    else:
        outs.append(jax.ShapeDtypeStruct((acc_rows, lanes), F32))
    return call(
        body,
        outs,
        [smem_spec()] + [vmem_spec()] * (2 + len(ins)),
        [
            pltpu.VMEM((3 * chans + 16, (n_rows + 4) * width), BF16),
            pltpu.VMEM((n_rows + 4, 1, width), F32),
            pltpu.VMEM((n_hidden, n_rows * n_cols), F32),
            pltpu.VMEM((3 * n_hidden, (n_rows + 2) * n_cols), BF16),
            pltpu.VMEM((3 * n_own, (n_rows + 2) * n_cols), BF16),
            pltpu.VMEM((3 * n_own, (n_rows + 2) * width), BF16),
            pltpu.VMEM((acc_rows, lanes), F32),
        ],
        2 * (n_rows + 2) * 9 * n_cols * n_hidden * (n_own + chans),
        (n_rows + 2) * 3 * n_hidden * n_cols * 2,
        "grads",
        50,
    )(index, kernel, gain, *ins)


def encode_kernel(kernel_ref, hidden_ref, out_ref, wide_ref):
    n_ext, n_hidden, width = hidden_ref.shape
    n_rows = n_ext - 2
    n_cols = width - LANES
    for h in range(n_ext):
        hidden = hidden_ref[h].astype(F32)
        at = slice(h * n_cols, (h + 1) * n_cols)
        wide_ref[0:n_hidden, at] = pltpu.roll(hidden, 1, 1)[:, :n_cols].astype(BF16)
        wide_ref[n_hidden : 2 * n_hidden, at] = hidden_ref[h, :, 0:n_cols]
        wide_ref[2 * n_hidden :, at] = pltpu.roll(hidden, width - 1, 1)[:, :n_cols].astype(BF16)
    total = None
    for a in range(3):
        part = dot_nn(kernel_ref[a], wide_ref[:, a * n_cols : (a + n_rows) * n_cols])
        total = part if total is None else total + part
    for r in range(n_rows):
        out_ref[r] = total[:, r * n_cols : (r + 1) * n_cols].astype(BF16)


def encode(kernel, hidden):
    n_ext, n_hidden, width = hidden.shape
    own = kernel.shape[1]
    n_cols = width - LANES
    return call(
        encode_kernel,
        jax.ShapeDtypeStruct((n_ext - 2, own, n_cols), BF16),
        [vmem_spec()] * 2,
        [pltpu.VMEM((3 * n_hidden, n_ext * n_cols), BF16)],
        2 * n_ext * 9 * own * n_hidden * n_cols,
        hidden.size * 2,
        "encode",
        32,
    )(kernel, hidden)


def quarters_kernel(index_ref, keep_ref, got_ref, *outs):
    n = len(outs)
    rows = keep_ref.shape[0] // n
    for k in range(n):
        other = jnp.bitwise_xor(index_ref[0], k)
        at = pl.ds(pl.multiple_of(other * rows, rows), rows)
        outs[k][...] = (keep_ref[at, :] + got_ref[at, :].astype(F32)).astype(outs[k].dtype)


def quarters(index, keep, got, n):
    rows, lanes = keep.shape
    return call(
        quarters_kernel,
        [jax.ShapeDtypeStruct((rows // n, lanes), F32 if k == 0 else BF16) for k in range(n)],
        [smem_spec(), vmem_spec(), vmem_spec()],
        [],
        rows * lanes,
        rows * lanes * 8,
        "quarters",
        16,
    )(index, keep, got)


def finish_kernel(scale, own, chans, index_ref, mine_ref, other_ref, two_ref, one_ref, gain_ref, all_ref):
    n, rows, lanes = mine_ref.shape
    n_hidden = lanes // 3
    tile, sub = index_ref[0], index_ref[2]
    for k in range(n):
        at = jnp.bitwise_xor(tile, k) * rows
        here = pl.multiple_of(sub * (n * rows) + at, rows)
        there = pl.multiple_of((1 - sub) * (n * rows) + at, rows)
        all_ref[pl.ds(here, rows), :] = mine_ref[k].astype(F32) * scale
        all_ref[pl.ds(there, rows), :] = other_ref[k].astype(F32) * scale
    half_rows = 3 * chans // 2
    for a in range(3):
        for b in range(3):
            two_ref[a, b] = all_ref[a * own : (a + 1) * own, b * n_hidden : (b + 1) * n_hidden]
        lines = jnp.concatenate(
            [
                all_ref[3 * own : 3 * own + half_rows, s + a * own : s + (a + 1) * own]
                for s in (0, lanes // 2)
            ],
            axis=0,
        )
        for b in range(3):
            one_ref[a, b] = lines[b * chans : (b + 1) * chans]
    gain_ref[...] = all_ref[3 * own + half_rows : 3 * own + half_rows + 1, own : 2 * own]


def finish(index, mine, other, scale, own, chans):
    n, rows, lanes = mine.shape
    n_hidden = lanes // 3
    return call(
        functools.partial(finish_kernel, scale, own, chans),
        [
            jax.ShapeDtypeStruct((3, 3, own, n_hidden), F32),
            jax.ShapeDtypeStruct((3, 3, chans, own), F32),
            jax.ShapeDtypeStruct((1, own), F32),
        ],
        [smem_spec(), vmem_spec(), vmem_spec()],
        [pltpu.VMEM((2 * n * rows, lanes), F32)],
        n * rows * lanes,
        n * rows * lanes * 12,
        "finish",
        24,
    )(index, mine, other)


def step_perm(count, by):
    return [(i, i + by) for i in range(count) if 0 <= i + by < count]


def swap_sub(x):
    return lax.ppermute(x, "sub", [(0, 1), (1, 0)])


def swap_chan(x):
    return lax.ppermute(x, "chan", [(0, 1), (1, 0)])


def swap_tile(x, n_tile, k):
    return lax.ppermute(x, "tile", [(i, i ^ k) for i in range(n_tile)])


def edges(block, depth, n_tile):
    low = lax.ppermute(block[-depth:], "tile", step_perm(n_tile, 1))
    high = lax.ppermute(block[:depth], "tile", step_perm(n_tile, -1))
    return low, high


def near(block, sub):
    n_cols = block.shape[-1]
    return jnp.where(sub == 0, block[..., n_cols - LANES :], block[..., :LANES])


def side_rows(parts, sub):
    columns = [
        jnp.concatenate([near(edge[: edge.shape[0] // 2], sub), near(mid, sub), near(edge[edge.shape[0] // 2 :], sub)], axis=0)
        for mid, edge in parts
    ]
    both = columns[0] if len(columns) == 1 else jnp.concatenate(columns, axis=1)
    return swap_sub(both)


def body(obs_values, obs_weight, obs_tile, obs_cell, conv_one, conv_two, density_gain, cotangent):
    own, n_rows, n_cols = cotangent.shape
    n_tile = lax.axis_size("tile")
    n_sub = lax.axis_size("sub")
    n_chan = lax.axis_size("chan")
    pair = n_chan == 2
    n_tiles = n_tile * n_sub
    chans = obs_values.shape[1]
    n_hidden = own * n_chan
    cap = 2 * obs_values.shape[0] // n_tiles
    tile, chan, sub = lax.axis_index("tile"), lax.axis_index("chan"), lax.axis_index("sub")
    index = jnp.stack([tile, chan, sub, jnp.int32(n_tile)]).astype(jnp.int32)

    sent = route(obs_values, obs_weight, obs_tile, obs_cell, n_tiles, cap, 2)
    got = [
        lax.all_to_all(x, ("tile", "sub"), split_axis=0, concat_axis=0, tiled=True) for x in sent
    ]

    cotangent, conv_one, conv_two, density_gain, _ = lax.optimization_barrier(
        (cotangent, conv_one, conv_two, density_gain, sent[0])
    )
    cot = cotangent.transpose(1, 0, 2)
    low, high = edges(cot, 1, n_tile)
    cot_edge = jnp.concatenate([low, high], axis=0)
    if pair:
        pieces = [(cot, cot_edge), (swap_chan(cot), swap_chan(cot_edge))]
    else:
        pieces = [
            (
                lax.all_gather(cot, "chan", axis=1, tiled=True),
                lax.all_gather(cot_edge, "chan", axis=1, tiled=True),
            )
        ]
    cot_side = side_rows(pieces, sub)

    code_weights = conv_two.transpose(0, 2, 1, 3).reshape(3, own, 3 * n_hidden)
    one_own = conv_one.transpose(0, 1, 3, 2)
    if pair:
        split_two = conv_two.reshape(3, 3, own, n_chan, own)
        halves = [split_two[:, :, :, i] for i in range(2)]
        mine = jnp.where(chan == 0, halves[0], halves[1])
        yours = jnp.where(chan == 0, halves[1], halves[0])
        columns = jnp.concatenate([mine, swap_chan(yours)], axis=2)
        one_peer = swap_chan(one_own)
        gain_peer = swap_chan(density_gain)
        one_full = jnp.where(
            chan == 0,
            jnp.concatenate([one_own, one_peer], axis=3),
            jnp.concatenate([one_peer, one_own], axis=3),
        )
        gain = jnp.where(
            chan == 0,
            jnp.concatenate([density_gain, gain_peer]),
            jnp.concatenate([gain_peer, density_gain]),
        )
    else:
        columns = lax.all_to_all(conv_two, "chan", split_axis=3, concat_axis=2, tiled=True)
        one_full = lax.all_gather(one_own, "chan", axis=3, tiled=True)
        gain = lax.all_gather(density_gain, "chan", axis=0, tiled=True)
    back_weights = columns.transpose(0, 3, 1, 2).reshape(3, own, 3 * n_hidden)
    one_weights = one_full.transpose(0, 3, 1, 2).reshape(3, n_hidden, 3 * chans)
    gain = gain[:, None]

    got[0], back_weights, one_weights, code_weights, gain = lax.optimization_barrier(
        (got[0], back_weights, one_weights, code_weights, gain)
    )
    (part,) = grid(got[0], None, False, n_rows, n_cols)
    part, message = grid(got[1], part, True, n_rows, n_cols)
    shape = (n_rows, chans + META, n_cols)
    part = part.reshape(shape)
    message = message.reshape(shape)
    if not pair:
        part = lax.psum(part, "chan")
        density = part[:, chans]
        dense = density.astype(BF16)
        rest = (density - dense.astype(F32)).astype(BF16)
        message = part.astype(BF16).at[:, chans].set(dense).at[:, chans + 1].set(rest)
    low, high = edges(message, 2, n_tile)
    edge = jnp.concatenate([low, high], axis=0)
    if pair:
        peer, peer_edge = swap_chan(message), swap_chan(edge)
        side = side_rows([(message, edge), (peer, peer_edge)], sub)
    else:
        peer, peer_edge = None, None
        side = side_rows([(message, edge)], sub)
    cot_side, _ = lax.optimization_barrier((cot_side, message))
    back_out = back(index, back_weights, pieces, cot_side, n_cols)

    scale = 1.0 / math.sqrt(n_tiles * n_rows * n_cols)
    split = pair and n_tile == 4
    hidden, *partial = grads(
        split, index, one_weights, gain, part, edge, peer, peer_edge, side, cot, back_out
    )
    encoded = encode(code_weights, hidden).transpose(1, 0, 2)

    if split:
        keep, give = partial
        mine, *others = quarters(index, keep, swap_sub(give), n_tile)
        for k, other in enumerate(others, 1):
            mine = mine + swap_tile(other, n_tile, k).astype(F32)
        mine = mine.astype(BF16)
        mine = jnp.stack([mine] + [swap_tile(mine, n_tile, k) for k in range(1, n_tile)])
        grad_two, grad_one, grad_gain = finish(index, mine, swap_sub(mine), scale, own, chans)
        return encoded, grad_one.transpose(0, 1, 3, 2), grad_two, grad_gain[0]

    total = lax.psum(partial[0], ("tile", "sub")) * scale
    three = 3 * own
    half_rows = 3 * chans // 2
    lanes = 3 * n_hidden
    grad_two = total[:three].reshape(3, own, 3, n_hidden).transpose(0, 2, 1, 3)
    lines = total[three : three + half_rows]
    lines = jnp.concatenate([lines[:, :three], lines[:, lanes // 2 : lanes // 2 + three]], axis=0)
    grad_one = lines.reshape(3, chans, 3, own).transpose(2, 0, 3, 1)
    grad_gain = total[three + half_rows, own : 2 * own]
    return encoded, grad_one, grad_two, grad_gain


def solution(mesh):
    placed = (
        P(("member", "tile", "chan", "sub"), None),
        P(("member", "tile", "chan", "sub")),
        P(("member", "tile", "chan", "sub")),
        P(("member", "tile", "chan", "sub")),
        P(None, None, "chan", None),
        P(None, None, "chan", None),
        P("chan"),
        P(("member", "chan"), "tile", "sub"),
    )
    return jax.shard_map(
        body,
        mesh=mesh,
        in_specs=placed,
        out_specs=(
            P(("member", "chan"), "tile", "sub"),
            P("member", None, "chan", None),
            P("member", None, "chan", None),
            P(("member", "chan")),
        ),
        check_vma=False,
    )
```

time: 203 us -> 139 us (0.68)
  blocking collectives: 55.7 us -> 0 us
  Pallas kernels: 58.8 us -> 34.5 us
  waiting for transfers between devices: 27.5 us -> 37.2 us
  starting transfers between devices: 32.2 us -> 40.7 us
  local copies, waits for them, and re-layouts: 19.7 us -> 15.7 us
    all_to_all x2 -> x0, blocking collectives: 29.1 us -> none  [the longest x1 14.9 us: body(): lax.all_to_all(mine.reshape(n_tile, half // n_tile, lanes), 'tile', 0, 0,...]
    all_gather x2 -> x0, blocking collectives: 26.6 us -> none  [the longest x1 22.4 us: body(): one_full = lax.all_gather(conv_one, 'chan', axis=2, tiled=True)]
    pallas_call x4 -> x7, Pallas kernels: 50.1 us -> 31.2 us  [the longest x1 10.9 us: grads(): call(body, outs, [smem_spec()] + [vmem_spec()] * (2 + len(ins)), [pltpu.V...]
    ppermute x2 -> x7, waiting for transfers between devices: 0.01 us -> 13.9 us  [swap_chan(): return lax.ppermute(x, 'chan', [(0, 1), (1, 0)])]
    pallas_call x1, Pallas kernels: 8.75 us -> 3.27 us  [encode(): call(encode_kernel, jax.ShapeDtypeStruct((n_ext - 2, own, n_cols), BF16),...]
    ppermute x2 -> x7, starting transfers between devices: 3.49 us -> 7.9 us  [swap_chan(): return lax.ppermute(x, 'chan', [(0, 1), (1, 0)])]
    all_to_all x2, waiting for transfers between devices: 3.76 us -> 0.01 us  [body(): lax.all_to_all(x, ('tile', 'sub'), split_axis=0, concat_axis=0, tiled=True)]
    reshape x6 -> x0, local copies, waits for them, and re-layouts: 3.51 us -> none  [the longest x1 0.91 us: body(): one_weights = one_full.transpose(2, 0, 1, 3).reshape(n_hidden, 9 * chans)]
  transfers between devices with their start and end apart: 12 -> 23, of which waited for: 5 -> 10; matrix products, arithmetic and copies ran while one was open for 7% -> 11% of each run, Pallas kernels for 13% -> 9%
where the time goes in v2:
time: 139 us; the launch traced here: 138 us
  starting transfers between devices  40.7 us (29%)
  waiting for transfers between devices  37.2 us (27%)
  Pallas kernels  34.5 us (25%)
  local copies, waits for them, and re-layouts  15.7 us (11%)
  other arithmetic  9.16 us (7%)
    ppermute x6, waiting for transfers between devices, swap_tile(): return lax.ppermute(x, 'tile', [(i, i ^ k) for i in range(n_tile)])  14.7 us
    ppermute x7, waiting for transfers between devices, swap_chan(): return lax.ppermute(x, 'chan', [(0, 1), (1, 0)])  13.9 us
    all_to_all x2, starting transfers between devices, body(): lax.all_to_all(x, ('tile', 'sub'), split_axis=0, concat_axis=0, tiled=True)  12.5 us
    pallas_call x1, Pallas kernels, grads(): call(body, outs, [smem_spec()] + [vmem_spec()] * (2 + len(ins)), [pltpu.V...  10.9 us
    unnamed x45, local copies, waits for them, and re-layouts  10.5 us
    ppermute x6, starting transfers between devices, swap_tile(): return lax.ppermute(x, 'tile', [(i, i ^ k) for i in range(n_tile)])  8.92 us
    pallas_call x1, Pallas kernels, route(): call(functools.partial(route_kernel, n_tiles, cap, n_parts), [jax.ShapeDt...  8.41 us
    ppermute x2, starting transfers between devices, edges(): low = lax.ppermute(block[-depth:], 'tile', step_perm(n_tile, 1))  8.11 us
  transfers between devices with their start and end apart: 23, of which 10 were waited for; matrix products, arithmetic and copies ran while one was open for 11% of the time, Pallas kernels for 9%

profile of v2, /device:TPU:0, one launch (start us, length us, event | category | flops | bytes accessed | tf_op | source)
XLA Modules:
  0.0 138.4 jit_solution(749751249089279285)
XLA Ops:
  3.8 8.4 %route.1 = (bf16[8,72,512]{2,1,0:T(8,128)(2,1)}, bf16[8,72,512]{2,1,0:T(8,128)(2,1)}) custom-call(s32[32,128]{1,0:T(8,128)S(1)} %bitcast.59, bf16[32,128]{1,0:T(8,128)(2,1)S(1)} %bitcast.61, s32[32,128]{1,0:T(8,128)S(1)} %bitcast.60, bf16[64,4096]{1,0:T(8,128)(2,1)S(1)} %bitcast.58), custom_call_target="tpu_custom_call" | custom-call | flops 1342177280 | bytes 1179648 | tf_op jit(solution)/shard_map/route/pallas_call | solution.py:164
  12.2 6.5 %all-to-all-start = ((bf16[8,72,512]{2,1,0:T(8,128)(2,1)}), bf16[8,72,512]{2,1,0:T(8,128)(2,1)S(1)}, u32[]{:S(2)}, u32[]{:S(2)}) async-start(bf16[8,72,512]{2,1,0:T(8,128)(2,1)} %get-tuple-element.28), calls=%async_computation | async-start | bytes 1179648 | tf_op jit(solution)/shard_map/all_to_all | solution.py:614
  27.6 4.5 %collective-permute-start.8 = (bf16[1,128,384]{2,1,0:T(8,128)(2,1)S(1)}, bf16[1,128,384]{2,1,0:T(8,128)(2,1)S(1)}, u32[]{:S(2)}, u32[]{:S(2)}) collective-permute-start(bf16[1,128,384]{2,1,0:T(8,128)(2,1)S(1)} %get-tuple-element.69), channel_id=1, source_target_pairs={{0,4},{4,8},{8,12},{1,5},{5,9},{9,13},{2,6},{6,10},{10,14},{3,7},{... | collective-permute-start | bytes 294920 | tf_op jit(solution)/shard_map/ppermute | solution.py:580
  32.5 1.9 %collective-permute-done.8 = bf16[1,128,384]{2,1,0:T(8,128)(2,1)S(1)} collective-permute-done((bf16[1,128,384]{2,1,0:T(8,128)(2,1)S(1)}, bf16[1,128,384]{2,1,0:T(8,128)(2,1)S(1)}, u32[]{:S(2)}, u32[]{:S(2)}) %collective-permute-start.8) | collective-permute-done | bytes 98336 | tf_op jit(solution)/shard_map/ppermute | solution.py:580
  36.0 6.0 %all-to-all-start.1 = ((bf16[8,72,512]{2,1,0:T(8,128)(2,1)}), bf16[8,72,512]{2,1,0:T(8,128)(2,1)S(1)}, u32[]{:S(2)}, u32[]{:S(2)}) async-start(bf16[8,72,512]{2,1,0:T(8,128)(2,1)} %get-tuple-element.35), calls=%async_computation.1 | async-start | bytes 1179648 | tf_op jit(solution)/shard_map/all_to_all | solution.py:614
  42.0 1.9 %maximum_select_fusion = bf16[3,3,64,256]{3,2,1,0:T(8,128)(2,1)} fusion(bf16[3,3,64,128]{3,2,1,0:T(8,128)(2,1)} %collective-permute-done.1, bf16[3,3,64,128]{3,2,1,0:T(8,128)(2,1)} %bitcast.12, pred[]{:T(512)S(6)} %eq.4), kind=kLoop, calls=%fused_computation.7 | loop fusion | flops 1327104 | bytes 589825 | tf_op jit(solution)/shard_map/jit(_where)/select_n | solution.py:644
  44.0 1.9 %maximum_bitcast_fusion = bf16[3,128,3,256]{3,1,2,0:T(8,128)(2,1)} fusion(bf16[3,3,128,128]{2,3,1,0:T(8,128)(2,1)} %collective-permute-done, bf16[3,3,128,128]{2,3,1,0:T(8,128)(2,1)} %fusion.1), kind=kLoop, calls=%fused_computation.2 | loop fusion | flops 1179648 | bytes 1179648 | tf_op jit(solution)/shard_map/transpose | solution.py:658
  45.9 2.1 %copy.53 = bf16[3,128,3,256]{1,3,2,0:T(8,128)(2,1)} copy(bf16[3,128,3,256]{3,1,2,0:T(8,128)(2,1)} %maximum_bitcast_fusion) | data formatting | bytes 1179648 | tf_op jit(solution)/shard_map/transpose | solution.py:658
  48.0 5.8 %collective-permute-done.11.rest_3_ = bf16[2,128,384]{2,1,0:T(8,128)(2,1)S(1)} collective-permute-done((bf16[2,128,384]{2,1,0:T(8,128)(2,1)S(1)}, bf16[2,128,384]{2,1,0:T(8,128)(2,1)S(1)}, u32[]{:S(2)}, u32[]{:S(2)}) %collective-permute-start.11) | collective-permute-done | bytes 196640 | tf_op jit(solution)/shard_map/ppermute | solution.py:572
  53.9 1.9 %maximum_maximum_fusion = bf16[10,256,128]{2,1,0:T(8,128)(2,1)} fusion(bf16[1,128,128]{2,1,0:T(8,128)(2,1)S(1)} %get-tuple-element.75, bf16[8,128,128]{2,1,0:T(8,128)(2,1)S(1)} %slice_select_fusion, bf16[1,128,128]{2,1,0:T(8,128)(2,1)S(1)} %get-tuple-element.74, bf16[1,128,128]{2,1,0:T(8,128)(2,1)S(1)} %slice_select_fusion.10, ...), kind=kLoop, calls=%fused_computation.1 | loop fusion | flops 3932160 | bytes 1310720 | tf_op jit(solution)/shard_map/concatenate | solution.py:595
  55.8 2.6 %grid_part.1.rest_0_ = f32[576,384]{1,0:T(8,128)S(1)} custom-call(bf16[8,72,512]{2,1,0:T(8,128)(2,1)S(1)} %all-to-all-done.got_ref), custom_call_target="tpu_custom_call" | custom-call | flops 1811939328 | bytes 589824 | tf_op jit(solution)/shard_map/grid_part/pallas_call | solution.py:244
  60.5 2.7 %grid_last.1 = (f32[576,384]{1,0:T(8,128)S(1)}, bf16[576,384]{1,0:T(8,128)(2,1)S(1)}) custom-call(bf16[8,72,512]{2,1,0:T(8,128)(2,1)S(1)} %all-to-all-done.1.got_ref, f32[576,384]{1,0:T(8,128)S(1)} %copy-done.14), custom_call_target="tpu_custom_call" | custom-call | flops 1811939328 | bytes 589824 | tf_op jit(solution)/shard_map/grid_last/pallas_call | solution.py:244
  63.2 3.6 %collective-permute-start.3 = (bf16[2,72,384]{2,1,0:T(8,128)(2,1)S(1)}, bf16[2,72,384]{2,1,0:T(8,128)(2,1)S(1)}, u32[]{:S(2)}, u32[]{:S(2)}) collective-permute-start(bf16[2,72,384]{2,1,0:T(8,128)(2,1)S(1)} %bitcast.70), channel_id=1, source_target_pairs={{0,4},{4,8},{8,12},{1,5},{5,9},{9,13},{2,6},{6,10},{10,14},{3,7},{... | collective-permute-start | bytes 331784 | tf_op jit(solution)/shard_map/ppermute | solution.py:580
  69.8 4.5 %collective-permute-done.4 = bf16[2,72,384]{2,1,0:T(8,128)(2,1)S(1)} collective-permute-done((bf16[2,72,384]{2,1,0:T(8,128)(2,1)S(1)}, bf16[2,72,384]{2,1,0:T(8,128)(2,1)S(1)}, u32[]{:S(2)}, u32[]{:S(2)}) %collective-permute-start.4) | collective-permute-done | bytes 110624 | tf_op jit(solution)/shard_map/ppermute | solution.py:581
  75.9 8.1 %collective-permute-done.6.peer_edge_ref = bf16[4,72,384]{2,1,0:T(8,128)(2,1)S(1)} collective-permute-done((bf16[4,72,384]{2,1,0:T(8,128)(2,1)S(1)}, bf16[4,72,384]{2,1,0:T(8,128)(2,1)S(1)}, u32[]{:S(2)}, u32[]{:S(2)}) %collective-permute-start.6) | collective-permute-done | bytes 221216 | tf_op jit(solution)/shard_map/ppermute | solution.py:572
  87.4 4.2 %back.1.back_ref = f32[128,3072]{1,0:T(8,128)S(1)} custom-call(s32[4]{0:T(128)S(1)} %pad_add_fusion.index_ref, bf16[3,128,768]{2,1,0:T(8,128)(2,1)S(1)} %copy.58.kernel_ref, bf16[8,128,384]{2,1,0:T(8,128)(2,1)S(1)} %bitcast.53, bf16[2,128,384]{2,1,0:T(8,128)(2,1)S(1)} %copy-done.5, bf16[8,128,384]{2,1,0:T(8,128)(2,1)S(1)} %collective-permute-done.10.rest_2_, ...), custom_call_target="tpu_custom_call" | custom-call | flops 2264924160 | bytes 1966080 | tf_op jit(solution)/shard_map/back/pallas_call | solution.py:297
  92.8 10.9 %grads.1 = (bf16[10,256,512]{2,1,0:T(8,128)(2,1)}, f32[256,768]{1,0:T(8,128)S(1)}, bf16[256,768]{1,0:T(8,128)(2,1)S(1)}) custom-call(s32[4]{0:T(128)S(1)} %pad_add_fusion.index_ref, bf16[3,256,192]{2,1,0:T(8,128)(2,1)S(1)} %copy.59.kernel_ref, f32[256,1]{1,0:T(8,128)S(1)} %broadcast_select_fusion.gain_ref, f32[8,72,384]{2,1,0:T(8,128)} %bitcast.62, ...), custom_call_target="tpu_custom_call" | custom-call | flops 3397386240 | bytes 5898240 | tf_op jit(solution)/shard_map/grads/pallas_call | solution.py:441
  108.7 1.9 %collective-permute-start.16 = (bf16[64,768]{1,0:T(8,128)(2,1)S(1)}, bf16[64,768]{1,0:T(8,128)(2,1)S(1)}, u32[]{:S(2)}, u32[]{:S(2)}) collective-permute-start(bf16[64,768]{1,0:T(8,128)(2,1)S(1)} %get-tuple-element.48), channel_id=1, source_target_pairs={{0,12},{4,8},{8,4},{12,0},{1,13},{5,9},{9,5},{13,1},{2,14},{6,10},... | collective-permute-start | bytes 294920 | tf_op jit(solution)/shard_map/ppermute | solution.py:576
  111.3 7.2 %collective-permute-done.15 = bf16[64,768]{1,0:T(8,128)(2,1)S(1)} collective-permute-done((bf16[64,768]{1,0:T(8,128)(2,1)S(1)}, bf16[64,768]{1,0:T(8,128)(2,1)S(1)}, u32[]{:S(2)}, u32[]{:S(2)}) %collective-permute-start.15) | collective-permute-done | bytes 98336 | tf_op jit(solution)/shard_map/ppermute | solution.py:576
  118.5 2.2 %collective-permute-start.19 = (bf16[64,768]{1,0:T(8,128)(2,1)S(1)}, bf16[64,768]{1,0:T(8,128)(2,1)S(1)}, u32[]{:S(2)}, u32[]{:S(2)}) collective-permute-start(bf16[64,768]{1,0:T(8,128)(2,1)S(1)} %add_convert_fusion), channel_id=1, source_target_pairs={{0,12},{4,8},{8,4},{12,0},{1,13},{5,9},{9,5},{13,1},{2,14},{6,10},... | collective-permute-start | bytes 294920 | tf_op jit(solution)/shard_map/ppermute | solution.py:576
  123.0 3.1 %collective-permute-done.19 = bf16[64,768]{1,0:T(8,128)(2,1)S(1)} collective-permute-done((bf16[64,768]{1,0:T(8,128)(2,1)S(1)}, bf16[64,768]{1,0:T(8,128)(2,1)S(1)}, u32[]{:S(2)}, u32[]{:S(2)}) %collective-permute-start.19) | collective-permute-done | bytes 98336 | tf_op jit(solution)/shard_map/ppermute | solution.py:576
  126.1 3.8 %collective-permute-done.18 = bf16[64,768]{1,0:T(8,128)(2,1)S(1)} collective-permute-done((bf16[64,768]{1,0:T(8,128)(2,1)S(1)}, bf16[64,768]{1,0:T(8,128)(2,1)S(1)}, u32[]{:S(2)}, u32[]{:S(2)}) %collective-permute-start.18) | collective-permute-done | bytes 98336 | tf_op jit(solution)/shard_map/ppermute | solution.py:576
  132.0 3.3 %encode.1 = bf16[8,128,384]{2,1,0:T(8,128)(2,1)S(1)} custom-call(bf16[3,128,768]{2,1,0:T(8,128)(2,1)S(1)} %copy.60.kernel_ref, bf16[10,256,512]{2,1,0:T(8,128)(2,1)S(1)} %copy-done.11), custom_call_target="tpu_custom_call" | custom-call | flops 2264924160 | bytes 2621440 | tf_op jit(solution)/shard_map/encode/pallas_call | solution.py:483
  136.6 1.8 %finish.1 = (f32[3,3,128,256]{3,2,1,0:T(8,128)}, f32[3,3,64,128]{3,2,1,0:T(8,128)}, f32[1,128]{1,0:T(1,128)}) custom-call(s32[4]{0:T(128)S(1)} %pad_add_fusion.index_ref, bf16[4,64,768]{2,1,0:T(8,128)(2,1)S(1)} %pad_maximum_fusion.mine_ref, bf16[4,64,768]{2,1,0:T(8,128)(2,1)S(1)} %collective-permute-done.20.other_ref), custom_call_target="tpu_custom_call" | custom-call | flops 196608 | bytes 2359296 | tf_op jit(solution)/shard_map/finish/pallas_call | solution.py:547
  (108 shorter events, 36.6 us)
Async XLA Ops:
  12.2 23.7 %all-to-all-start = ((bf16[8,72,512]{2,1,0:T(8,128)(2,1)}), bf16[8,72,512]{2,1,0:T(8,128)(2,1)S(1)}, u32[]{:S(2)}, u32[]{:S(2)}) async-start(bf16[8,72,512]{2,1,0:T(8,128)(2,1)} %get-tuple-element.28), calls=%async_computation | async-start | bytes 1179648 | tf_op jit(solution)/shard_map/all_to_all | solution.py:614
  18.7 8.9 %collective-permute-start.2 = (f32[128]{0:T(128)S(1)}, f32[128]{0:T(128)S(1)}, u32[]{:S(2)}, u32[]{:S(2)}) collective-permute-start(f32[128]{0:T(128)S(1)} %copy-done.20), channel_id=1, source_target_pairs={{0,2},{2,0},{1,3},{3,1},{4,6},{6,4},{5,7},{7,5},{8,10},{10,8},{9,1... | collective-permute-start | bytes 1544 | tf_op jit(solution)/shard_map/ppermute | solution.py:572
  20.3 21.7 %collective-permute-start.1 = (bf16[3,3,64,128]{3,2,1,0:T(8,128)(2,1)}, bf16[3,3,64,128]{3,2,1,0:T(8,128)(2,1)}, u32[]{:S(2)}, u32[]{:S(2)}) collective-permute-start(bf16[3,3,64,128]{3,2,1,0:T(8,128)(2,1)} %bitcast.12), channel_id=1, source_target_pairs={{0,2},{2,0},{1,3},{3,1},{4,6},{6,4},{5,7},{7,5},{8,10},{10,8},{9,1... | collective-permute-start | bytes 442376 | tf_op jit(solution)/shard_map/ppermute | solution.py:572
  21.9 22.0 %collective-permute-start = (bf16[3,3,128,128]{2,3,1,0:T(8,128)(2,1)}, bf16[3,3,128,128]{2,3,1,0:T(8,128)(2,1)}, u32[]{:S(2)}, u32[]{:S(2)}) collective-permute-start(bf16[3,3,128,128]{2,3,1,0:T(8,128)(2,1)} %fusion), channel_id=1, source_target_pairs={{0,2},{2,0},{1,3},{3,1},{4,6},{6,4},{5,7},{7,5},{8,10},{10,8},{9,1... | collective-permute-start | bytes 884744 | tf_op jit(solution)/shard_map/ppermute | solution.py:572
  23.5 30.3 %collective-permute-start.10 = (bf16[8,128,384]{2,1,0:T(8,128)(2,1)S(1)}, bf16[8,128,384]{2,1,0:T(8,128)(2,1)S(1)}, u32[]{:S(2)}, u32[]{:S(2)}) collective-permute-start(bf16[8,128,384]{2,1,0:T(8,128)(2,1)S(1)} %bitcast.50), channel_id=1, source_target_pairs={{0,2},{2,0},{1,3},{3,1},{4,6},{6,4},{5,7},{7,5},{8,10},{10,8},{9,1... | collective-permute-start | bytes 2359304 | tf_op jit(solution)/shard_map/ppermute | solution.py:572
  24.8 9.6 %collective-permute-start.9 = (bf16[1,128,384]{2,1,0:T(8,128)(2,1)}, bf16[1,128,384]{2,1,0:T(8,128)(2,1)S(1)}, u32[]{:S(2)}, u32[]{:S(2)}) collective-permute-start(bf16[1,128,384]{2,1,0:T(8,128)(2,1)} %get-tuple-element.68), channel_id=1, source_target_pairs={{4,0},{8,4},{12,8},{5,1},{9,5},{13,9},{6,2},{10,6},{14,10},{7,3},{... | collective-permute-start | bytes 294920 | tf_op jit(solution)/shard_map/ppermute | solution.py:581
  27.6 6.7 %collective-permute-start.8 = (bf16[1,128,384]{2,1,0:T(8,128)(2,1)S(1)}, bf16[1,128,384]{2,1,0:T(8,128)(2,1)S(1)}, u32[]{:S(2)}, u32[]{:S(2)}) collective-permute-start(bf16[1,128,384]{2,1,0:T(8,128)(2,1)S(1)} %get-tuple-element.69), channel_id=1, source_target_pairs={{0,4},{4,8},{8,12},{1,5},{5,9},{9,13},{2,6},{6,10},{10,14},{3,7},{... | collective-permute-start | bytes 294920 | tf_op jit(solution)/shard_map/ppermute | solution.py:580
  34.4 19.5 %collective-permute-start.11 = (bf16[2,128,384]{2,1,0:T(8,128)(2,1)S(1)}, bf16[2,128,384]{2,1,0:T(8,128)(2,1)S(1)}, u32[]{:S(2)}, u32[]{:S(2)}) collective-permute-start(bf16[2,128,384]{2,1,0:T(8,128)(2,1)S(1)} %constant_dynamic-update-slice_fusion.2.rest_1_), channel_id=1, source_target_pairs={{0,2},{2,0},{1,3},{3,1},{4,6},{6,4},{5,7},{7,5},{8,10},{10,8},{9,1... | collective-permute-start | bytes 589832 | tf_op jit(solution)/shard_map/ppermute | solution.py:572
  36.0 23.4 %all-to-all-start.1 = ((bf16[8,72,512]{2,1,0:T(8,128)(2,1)}), bf16[8,72,512]{2,1,0:T(8,128)(2,1)S(1)}, u32[]{:S(2)}, u32[]{:S(2)}) async-start(bf16[8,72,512]{2,1,0:T(8,128)(2,1)} %get-tuple-element.35), calls=%async_computation.1 | async-start | bytes 1179648 | tf_op jit(solution)/shard_map/all_to_all | solution.py:614
  55.8 30.6 %collective-permute-start.12 = (bf16[10,256,128]{2,1,0:T(8,128)(2,1)}, bf16[10,256,128]{2,1,0:T(8,128)(2,1)}, u32[]{:S(2)}, u32[]{:S(2)}) collective-permute-start(bf16[10,256,128]{2,1,0:T(8,128)(2,1)} %maximum_maximum_fusion), channel_id=1, source_target_pairs={{0,1},{1,0},{2,3},{3,2},{4,5},{5,4},{6,7},{7,6},{8,9},{9,8},{10,11... | collective-permute-start | bytes 1966088 | tf_op jit(solution)/shard_map/ppermute | solution.py:568
  63.2 6.5 %collective-permute-start.3 = (bf16[2,72,384]{2,1,0:T(8,128)(2,1)S(1)}, bf16[2,72,384]{2,1,0:T(8,128)(2,1)S(1)}, u32[]{:S(2)}, u32[]{:S(2)}) collective-permute-start(bf16[2,72,384]{2,1,0:T(8,128)(2,1)S(1)} %bitcast.70), channel_id=1, source_target_pairs={{0,4},{4,8},{8,12},{1,5},{5,9},{9,13},{2,6},{6,10},{10,14},{3,7},{... | collective-permute-start | bytes 331784 | tf_op jit(solution)/shard_map/ppermute | solution.py:580
  66.8 17.1 %collective-permute-start.5 = (bf16[8,72,384]{2,1,0:T(8,128)(2,1)S(1)}, bf16[8,72,384]{2,1,0:T(8,128)(2,1)S(1)}, u32[]{:S(2)}, u32[]{:S(2)}) collective-permute-start(bf16[8,72,384]{2,1,0:T(8,128)(2,1)S(1)} %bitcast.57), channel_id=1, source_target_pairs={{0,2},{2,0},{1,3},{3,1},{4,6},{6,4},{5,7},{7,5},{8,10},{10,8},{9,1... | collective-permute-start | bytes 1327112 | tf_op jit(solution)/shard_map/ppermute | solution.py:572
  67.5 6.8 %collective-permute-start.4 = (bf16[2,72,384]{2,1,0:T(8,128)(2,1)S(1)}, bf16[2,72,384]{2,1,0:T(8,128)(2,1)S(1)}, u32[]{:S(2)}, u32[]{:S(2)}) collective-permute-start(bf16[2,72,384]{2,1,0:T(8,128)(2,1)S(1)} %bitcast.69), channel_id=1, source_target_pairs={{4,0},{8,4},{12,8},{5,1},{9,5},{13,9},{6,2},{10,6},{14,10},{7,3},{... | collective-permute-start | bytes 331784 | tf_op jit(solution)/shard_map/ppermute | solution.py:581
  74.3 9.7 %collective-permute-start.6 = (bf16[4,72,384]{2,1,0:T(8,128)(2,1)S(1)}, bf16[4,72,384]{2,1,0:T(8,128)(2,1)S(1)}, u32[]{:S(2)}, u32[]{:S(2)}) collective-permute-start(bf16[4,72,384]{2,1,0:T(8,128)(2,1)S(1)} %constant_dynamic-update-slice_fusion.edge_ref), channel_id=1, source_target_pairs={{0,2},{2,0},{1,3},{3,1},{4,6},{6,4},{5,7},{7,5},{8,10},{10,8},{9,1... | collective-permute-start | bytes 663560 | tf_op jit(solution)/shard_map/ppermute | solution.py:572
  84.8 7.9 %collective-permute-start.7 = (bf16[12,144,128]{2,1,0:T(8,128)(2,1)}, bf16[12,144,128]{2,1,0:T(8,128)(2,1)}, u32[]{:S(2)}, u32[]{:S(2)}) collective-permute-start(bf16[12,144,128]{2,1,0:T(8,128)(2,1)} %maximum_maximum_fusion.1), channel_id=1, source_target_pairs={{0,1},{1,0},{2,3},{3,2},{4,5},{5,4},{6,7},{7,6},{8,9},{9,8},{10,11... | collective-permute-start | bytes 1327112 | tf_op jit(solution)/shard_map/ppermute | solution.py:568
  103.7 26.3 %copy-start.16 = (bf16[3,3,128,256]{2,3,1,0:T(8,128)(2,1)S(1)}, bf16[3,3,128,256]{2,3,1,0:T(8,128)(2,1)}, u32[]{:S(2)}) copy-start(bf16[3,3,128,256]{2,3,1,0:T(8,128)(2,1)} %copy-done.15) | copy-start | bytes 1769476
  103.7 1.9 %collective-permute-start.13 = (bf16[256,768]{1,0:T(8,128)(2,1)S(1)}, bf16[256,768]{1,0:T(8,128)(2,1)S(1)}, u32[]{:S(2)}, u32[]{:S(2)}) collective-permute-start(bf16[256,768]{1,0:T(8,128)(2,1)S(1)} %get-tuple-element.44), channel_id=1, source_target_pairs={{0,1},{1,0},{2,3},{3,2},{4,5},{5,4},{6,7},{7,6},{8,9},{9,8},{10,11... | collective-permute-start | bytes 1179656 | tf_op jit(solution)/shard_map/ppermute | solution.py:568
  106.2 5.2 %collective-permute-start.14 = (bf16[64,768]{1,0:T(8,128)(2,1)S(1)}, bf16[64,768]{1,0:T(8,128)(2,1)S(1)}, u32[]{:S(2)}, u32[]{:S(2)}) collective-permute-start(bf16[64,768]{1,0:T(8,128)(2,1)S(1)} %get-tuple-element.46), channel_id=1, source_target_pairs={{0,4},{4,0},{8,12},{12,8},{1,5},{5,1},{9,13},{13,9},{2,6},{6,2},{1... | collective-permute-start | bytes 294920 | tf_op jit(solution)/shard_map/ppermute | solution.py:576
  107.7 10.8 %collective-permute-start.15 = (bf16[64,768]{1,0:T(8,128)(2,1)S(1)}, bf16[64,768]{1,0:T(8,128)(2,1)S(1)}, u32[]{:S(2)}, u32[]{:S(2)}) collective-permute-start(bf16[64,768]{1,0:T(8,128)(2,1)S(1)} %get-tuple-element.47), channel_id=1, source_target_pairs={{0,8},{4,12},{8,0},{12,4},{1,9},{5,13},{9,1},{13,5},{2,10},{6,14},... | collective-permute-start | bytes 294920 | tf_op jit(solution)/shard_map/ppermute | solution.py:576
  108.7 9.8 %collective-permute-start.16 = (bf16[64,768]{1,0:T(8,128)(2,1)S(1)}, bf16[64,768]{1,0:T(8,128)(2,1)S(1)}, u32[]{:S(2)}, u32[]{:S(2)}) collective-permute-start(bf16[64,768]{1,0:T(8,128)(2,1)S(1)} %get-tuple-element.48), channel_id=1, source_target_pairs={{0,12},{4,8},{8,4},{12,0},{1,13},{5,9},{9,5},{13,1},{2,14},{6,10},... | collective-permute-start | bytes 294920 | tf_op jit(solution)/shard_map/ppermute | solution.py:576
  118.5 7.6 %collective-permute-start.19 = (bf16[64,768]{1,0:T(8,128)(2,1)S(1)}, bf16[64,768]{1,0:T(8,128)(2,1)S(1)}, u32[]{:S(2)}, u32[]{:S(2)}) collective-permute-start(bf16[64,768]{1,0:T(8,128)(2,1)S(1)} %add_convert_fusion), channel_id=1, source_target_pairs={{0,12},{4,8},{8,4},{12,0},{1,13},{5,9},{9,5},{13,1},{2,14},{6,10},... | collective-permute-start | bytes 294920 | tf_op jit(solution)/shard_map/ppermute | solution.py:576
  120.7 9.2 %collective-permute-start.18 = (bf16[64,768]{1,0:T(8,128)(2,1)S(1)}, bf16[64,768]{1,0:T(8,128)(2,1)S(1)}, u32[]{:S(2)}, u32[]{:S(2)}) collective-permute-start(bf16[64,768]{1,0:T(8,128)(2,1)S(1)} %add_convert_fusion), channel_id=1, source_target_pairs={{0,8},{4,12},{8,0},{12,4},{1,9},{5,13},{9,1},{13,5},{2,10},{6,14},... | collective-permute-start | bytes 294920 | tf_op jit(solution)/shard_map/ppermute | solution.py:576
  121.9 8.0 %collective-permute-start.17 = (bf16[64,768]{1,0:T(8,128)(2,1)S(1)}, bf16[64,768]{1,0:T(8,128)(2,1)S(1)}, u32[]{:S(2)}, u32[]{:S(2)}) collective-permute-start(bf16[64,768]{1,0:T(8,128)(2,1)S(1)} %add_convert_fusion), channel_id=1, source_target_pairs={{0,4},{4,0},{8,12},{12,8},{1,5},{5,1},{9,13},{13,9},{2,6},{6,2},{1... | collective-permute-start | bytes 294920 | tf_op jit(solution)/shard_map/ppermute | solution.py:576
  129.9 6.7 %collective-permute-start.20 = (bf16[4,64,768]{2,1,0:T(8,128)(2,1)S(1)}, bf16[4,64,768]{2,1,0:T(8,128)(2,1)S(1)}, u32[]{:S(2)}, u32[]{:S(2)}) collective-permute-start(bf16[4,64,768]{2,1,0:T(8,128)(2,1)S(1)} %pad_maximum_fusion.mine_ref), channel_id=1, source_target_pairs={{0,1},{1,0},{2,3},{3,2},{4,5},{5,4},{6,7},{7,6},{8,9},{9,8},{10,11... | collective-permute-start | bytes 1179656 | tf_op jit(solution)/shard_map/ppermute | solution.py:568
  (20 other events, 117.6 us)

commit v3 on v2

--- a/solution.py
+++ b/solution.py
@@ -51,9 +51,21 @@
     )
 
 
-def route_kernel(n_tiles, cap, n_parts, tile_ref, weight_ref, cell_ref, values_ref, *rest):
-    outs = rest[:n_parts]
-    onehot_ref, slot_ref, weight32_ref, all_ref, info_ref, info_smem, sem = rest[n_parts:]
+def route_kernel(n_tiles, cap, relative, index_ref, tile_hbm, weight_hbm, cell_hbm, values_hbm, *rest):
+    n_outs = 5 if relative else 1
+    outs = rest[:n_outs]
+    (tile_ref, weight_ref, cell_ref, values_ref, onehot_ref, slot_ref, weight32_ref, all_ref,
+     info_ref, info_smem, sems) = rest[n_outs:]
+    loads = [
+        pltpu.make_async_copy(tile_hbm, tile_ref, sems.at[0]),
+        pltpu.make_async_copy(weight_hbm, weight_ref, sems.at[1]),
+        pltpu.make_async_copy(cell_hbm, cell_ref, sems.at[2]),
+        pltpu.make_async_copy(values_hbm, values_ref, sems.at[3]),
+    ]
+    for load in loads:
+        load.start()
+    all_ref[...] = jnp.zeros(all_ref.shape, BF16)
+    loads[0].wait()
     n_lines = tile_ref.shape[0]
     n_blocks = n_lines // 2
     n_obs_chans = values_ref.shape[0]
@@ -80,7 +92,7 @@
     info_ref[...] = jnp.where(
         iota((8, pairs), 0) == 0, base_row, any_spill
     ).astype(jnp.int32)
-    copy = pltpu.make_async_copy(info_ref, info_smem, sem)
+    copy = pltpu.make_async_copy(info_ref, info_smem, sems.at[4])
     copy.start()
     cum = dot_nn(onehot, upper)
     totals = dot_nn(onehot, jnp.ones((LANES, LANES), BF16))
@@ -90,8 +102,9 @@
     for t in range(n_tiles):
         slots = jnp.where(tiles == t, place[t * n_lines : (t + 1) * n_lines, :], slots)
     slot_ref[...] = slots
+    for load in loads[1:]:
+        load.wait()
     weight32_ref[...] = weight_ref[...].astype(F32)
-    all_ref[...] = jnp.zeros(all_ref.shape, BF16)
     meta_row = iota((16, BLOCK), 0)
     window = iota((BLOCK, BLOCK), 0, F32)
     copy.wait()
@@ -152,33 +165,46 @@
 
             lax.fori_loop(0, n_blocks, second, 0)
 
-    part = cap // n_parts
-    for p in range(n_parts):
-        outs[p][...] = all_ref[:, :, p * part : (p + 1) * part]
-
-
-def route(obs_values, obs_weight, obs_tile, obs_cell, n_tiles, cap, n_parts):
+    if relative:
+        me = index_ref[4]
+        outs[0][0] = all_ref[me]
+        outs[1][0] = all_ref[jnp.bitwise_xor(me, 1)]
+        for k in range(1, 4):
+            for s in range(2):
+                outs[k + 1][s] = all_ref[jnp.bitwise_xor(me, 2 * k + s)]
+    else:
+        outs[0][...] = all_ref[...]
+
+
+def route(index, obs_values, obs_weight, obs_tile, obs_cell, n_tiles, cap, relative):
     n_obs, chans = obs_values.shape
     n_lines = n_obs // LANES
     rows = chans + META
+    outs = [(n, rows, cap) for n in ((1, 1, 2, 2, 2) if relative else (n_tiles,))]
+    hbm_spec = pl.BlockSpec(memory_space=pltpu.HBM)
     return call(
-        functools.partial(route_kernel, n_tiles, cap, n_parts),
-        [jax.ShapeDtypeStruct((n_tiles, rows, cap // n_parts), BF16)] * n_parts,
-        [vmem_spec()] * 4,
+        functools.partial(route_kernel, n_tiles, cap, relative),
+        [jax.ShapeDtypeStruct(shape, BF16) for shape in outs],
+        [smem_spec()] + [hbm_spec] * 4,
         [
+            pltpu.VMEM((n_lines, LANES), jnp.int32),
+            pltpu.VMEM((n_lines, LANES), BF16),
+            pltpu.VMEM((n_lines, LANES), jnp.int32),
+            pltpu.VMEM((chans, n_obs), BF16),
             pltpu.VMEM((n_tiles * n_lines, LANES), BF16),
             pltpu.VMEM((n_lines, LANES), F32),
             pltpu.VMEM((n_lines, LANES), F32),
             pltpu.VMEM((n_tiles, rows, cap), BF16),
             pltpu.VMEM((8, n_tiles * n_lines), jnp.int32),
             pltpu.SMEM((8, n_tiles * n_lines), jnp.int32),
-            pltpu.SemaphoreType.DMA,
+            pltpu.SemaphoreType.DMA((5,)),
         ],
         2 * n_obs * n_tiles * BLOCK * 80,
         n_tiles * rows * cap * 2,
         "route",
         24,
     )(
+        index,
         obs_tile.reshape(n_lines, LANES),
         obs_weight.reshape(n_lines, LANES),
         obs_cell.reshape(n_lines, LANES),
@@ -186,13 +212,16 @@
     )
 
 
-def grid_kernel(n_rows, n_cols, group, first, last, got_ref, *rest):
+def grid_kernel(n_rows, n_cols, group, takes, first, last, *rest):
     rest = list(rest)
+    got_refs = [rest.pop(0) for _ in takes]
+    senders = [ref.at[i] for ref, n in zip(got_refs, takes) for i in range(n)]
     before_ref = None if first else rest.pop(0)
     own_ref = rest.pop(0)
     send_ref = rest.pop(0) if last else None
     left_ref, right_ref = rest
-    n_send, rows, cap = got_ref.shape
+    n_send = len(senders)
+    rows, cap = senders[0].shape
     chans = rows - META
     per_row = n_cols // LANES
     columns = iota((n_cols, cap), 0, F32)
@@ -203,8 +232,8 @@
         for i in range(group):
             s = g * group + i
             at = slice(i * cap, (i + 1) * cap)
-            values = got_ref[s, 0:chans, :]
-            meta = got_ref[s, chans:rows, :].astype(F32)
+            values = senders[s][0:chans, :]
+            meta = senders[s][chans:rows, :].astype(F32)
             weight = meta[0:1]
             high = meta[1:2]
             row = jnp.floor((high + 0.5) * (1.0 / per_row))
@@ -234,15 +263,18 @@
 
 
 def grid(got, before, last, n_rows, n_cols):
-    n_send, rows, cap = got.shape
-    group = 4
+    takes = [n for _, n in got]
+    got = [x for x, _ in got]
+    n_send = sum(takes)
+    rows, cap = got[0].shape[1:]
+    group = max(1, min(2048 // cap, n_send))
     total = n_rows * rows
     outs = [jax.ShapeDtypeStruct((total, n_cols), F32)]
     if last:
         outs.append(jax.ShapeDtypeStruct((total, n_cols), BF16))
-    ins = [got] if before is None else [got, before]
+    ins = list(got) if before is None else list(got) + [before]
     return call(
-        functools.partial(grid_kernel, n_rows, n_cols, group, before is None, last),
+        functools.partial(grid_kernel, n_rows, n_cols, group, takes, before is None, last),
         outs,
         [vmem_spec()] * len(ins),
         [
@@ -607,21 +639,20 @@
     n_hidden = own * n_chan
     cap = 2 * obs_values.shape[0] // n_tiles
     tile, chan, sub = lax.axis_index("tile"), lax.axis_index("chan"), lax.axis_index("sub")
-    index = jnp.stack([tile, chan, sub, jnp.int32(n_tile)]).astype(jnp.int32)
-
-    sent = route(obs_values, obs_weight, obs_tile, obs_cell, n_tiles, cap, 2)
-    got = [
-        lax.all_to_all(x, ("tile", "sub"), split_axis=0, concat_axis=0, tiled=True) for x in sent
-    ]
-
-    cotangent, conv_one, conv_two, density_gain, _ = lax.optimization_barrier(
-        (cotangent, conv_one, conv_two, density_gain, sent[0])
+    index = jnp.stack([tile, chan, sub, jnp.int32(n_tile), tile * n_sub + sub]).astype(jnp.int32)
+
+    bottom, top = cotangent[:, -1], cotangent[:, 0]
+    obs_tile, bottom, top = lax.optimization_barrier((obs_tile, bottom, top))
+    cot_edge = jnp.stack(
+        [
+            lax.ppermute(bottom, "tile", step_perm(n_tile, 1)),
+            lax.ppermute(top, "tile", step_perm(n_tile, -1)),
+        ]
     )
     cot = cotangent.transpose(1, 0, 2)
-    low, high = edges(cot, 1, n_tile)
-    cot_edge = jnp.concatenate([low, high], axis=0)
     if pair:
-        pieces = [(cot, cot_edge), (swap_chan(cot), swap_chan(cot_edge))]
+        cot_peer = swap_chan(cotangent).transpose(1, 0, 2)
+        pieces = [(cot, cot_edge), (cot_peer, swap_chan(cot_edge))]
     else:
         pieces = [
             (
@@ -631,6 +662,22 @@
         ]
     cot_side = side_rows(pieces, sub)
 
+    few = n_tiles == 8
+    sent = route(index, obs_values, obs_weight, obs_tile, obs_cell, n_tiles, cap, few)
+    if few:
+        far = [swap_tile(sent[k + 1], n_tile, k) for k in (1, 2, 3)]
+        steps = [
+            [(sent[0], 1), (swap_sub(sent[1]), 1), (far[0], 1), (swap_sub(far[0][1:]), 1)],
+            [(far[1], 1), (far[2], 1)],
+            [(swap_sub(far[1][1:]), 1), (swap_sub(far[2][1:]), 1)],
+        ]
+    else:
+        got = lax.all_to_all(sent[0], ("tile", "sub"), split_axis=0, concat_axis=0, tiled=True)
+        steps = [[(got, n_tiles)]]
+
+    conv_one, conv_two, density_gain, _ = lax.optimization_barrier(
+        (conv_one, conv_two, density_gain, sent[0])
+    )
     code_weights = conv_two.transpose(0, 2, 1, 3).reshape(3, own, 3 * n_hidden)
     one_own = conv_one.transpose(0, 1, 3, 2)
     if pair:
@@ -659,11 +706,10 @@
     one_weights = one_full.transpose(0, 3, 1, 2).reshape(3, n_hidden, 3 * chans)
     gain = gain[:, None]
 
-    got[0], back_weights, one_weights, code_weights, gain = lax.optimization_barrier(
-        (got[0], back_weights, one_weights, code_weights, gain)
-    )
-    (part,) = grid(got[0], None, False, n_rows, n_cols)
-    part, message = grid(got[1], part, True, n_rows, n_cols)
+    part = None
+    for step in steps[:-1]:
+        part = grid(step, part, False, n_rows, n_cols)[0]
+    part, message = grid(steps[-1], part, True, n_rows, n_cols)
     shape = (n_rows, chans + META, n_cols)
     part = part.reshape(shape)
     message = message.reshape(shape)
@@ -675,14 +721,14 @@
         message = part.astype(BF16).at[:, chans].set(dense).at[:, chans + 1].set(rest)
     low, high = edges(message, 2, n_tile)
     edge = jnp.concatenate([low, high], axis=0)
+    back_out = back(index, back_weights, pieces, cot_side, n_cols)
     if pair:
         peer, peer_edge = swap_chan(message), swap_chan(edge)
+        peer_edge, back_out = lax.optimization_barrier((peer_edge, back_out))
         side = side_rows([(message, edge), (peer, peer_edge)], sub)
     else:
         peer, peer_edge = None, None
         side = side_rows([(message, edge)], sub)
-    cot_side, _ = lax.optimization_barrier((cot_side, message))
-    back_out = back(index, back_weights, pieces, cot_side, n_cols)
 
     scale = 1.0 / math.sqrt(n_tiles * n_rows * n_cols)
     split = pair and n_tile == 4
@@ -696,7 +742,7 @@
         mine, *others = quarters(index, keep, swap_sub(give), n_tile)
         for k, other in enumerate(others, 1):
             mine = mine + swap_tile(other, n_tile, k).astype(F32)
-        mine = mine.astype(BF16)
+        mine, encoded = lax.optimization_barrier((mine.astype(BF16), encoded))
         mine = jnp.stack([mine] + [swap_tile(mine, n_tile, k) for k in range(1, n_tile)])
         grad_two, grad_one, grad_gain = finish(index, mine, swap_sub(mine), scale, own, chans)
         return encoded, grad_one.transpose(0, 1, 3, 2), grad_two, grad_gain[0]

time: 139 us -> 124 us (0.89)
  other arithmetic: 9.16 us -> 2.42 us
  waiting for transfers between devices: 37.2 us -> 33.2 us
  starting transfers between devices: 40.7 us -> 38.1 us
    all_to_all x2 -> x0, starting transfers between devices: 12.5 us -> none  [body(): lax.all_to_all(x, ('tile', 'sub'), split_axis=0, concat_axis=0, tiled=True)]
    ppermute x0 -> x2, starting transfers between devices: none -> 6.23 us  [the longest x1 4.93 us: body(): lax.ppermute(bottom, 'tile', step_perm(n_tile, 1))]
    ppermute x6 -> x9, starting transfers between devices: 8.92 us -> 14.7 us  [swap_tile(): return lax.ppermute(x, 'tile', [(i, i ^ k) for i in range(n_tile)])]
    ppermute x7, waiting for transfers between devices: 13.9 us -> 10.1 us  [swap_chan(): return lax.ppermute(x, 'chan', [(0, 1), (1, 0)])]
    reshape x0 -> x3, local copies, waits for them, and re-layouts: none -> 2.77 us  [the longest x1 1.3 us: body(): code_weights = conv_two.transpose(0, 2, 1, 3).reshape(3, own, 3 * n_hidden)]
    concatenate x2, other arithmetic: 2.67 us -> 0.08 us  [side_rows(): both = columns[0] if len(columns) == 1 else jnp.concatenate(columns, axis=1)]
    transpose x1, other arithmetic: 1.94 us -> 0.08 us  [body(): back_weights = columns.transpose(0, 3, 1, 2).reshape(3, own, 3 * n_hidden)]
    optimization_barrier x5 -> x1, local copies, waits for them, and re-layouts: 2.12 us -> 0.3 us  [body(): lax.optimization_barrier((conv_one, conv_two, density_gain, sent[0]))]
  transfers between devices with their start and end apart: 23 -> 28, of which waited for: 10 -> 11; matrix products, arithmetic and copies ran while one was open for 11% -> 7% of each run, Pallas kernels for 9% -> 17%
where the time goes in v3:
time: 124 us
  starting transfers between devices  38.1 us (31%)
  Pallas kernels  34.2 us (28%)
  waiting for transfers between devices  33.2 us (27%)
  local copies, waits for them, and re-layouts  14.6 us (12%)
  other arithmetic  2.42 us (2%)
    ppermute x9, starting transfers between devices, swap_tile(): return lax.ppermute(x, 'tile', [(i, i ^ k) for i in range(n_tile)])  14.7 us
    ppermute x9, waiting for transfers between devices, swap_tile(): return lax.ppermute(x, 'tile', [(i, i ^ k) for i in range(n_tile)])  13.6 us
    pallas_call x1, Pallas kernels, grads(): call(body, outs, [smem_spec()] + [vmem_spec()] * (2 + len(ins)), [pltpu.V...  10.2 us
    ppermute x7, waiting for transfers between devices, swap_chan(): return lax.ppermute(x, 'chan', [(0, 1), (1, 0)])  10.1 us
    unnamed x37, local copies, waits for them, and re-layouts  10 us
    pallas_call x1, Pallas kernels, route(): call(functools.partial(route_kernel, n_tiles, cap, relative), [jax.ShapeD...  9.09 us
    ppermute x1, starting transfers between devices, edges(): low = lax.ppermute(block[-depth:], 'tile', step_perm(n_tile, 1))  7.35 us
    ppermute x7, starting transfers between devices, swap_chan(): return lax.ppermute(x, 'chan', [(0, 1), (1, 0)])  6.89 us
  transfers between devices with their start and end apart: 28, of which 11 were waited for; matrix products, arithmetic and copies ran while one was open for 7% of the time, Pallas kernels for 17%

profile of v3, /device:TPU:0, one launch (start us, length us, event | category | flops | bytes accessed | tf_op | source)
XLA Modules:
  0.0 123.6 jit_solution(2406614380738295456)
XLA Ops:
  2.0 4.9 %collective-permute-start.14 = (bf16[128,384]{1,0:T(8,128)(2,1)S(1)}, bf16[128,384]{1,0:T(8,128)(2,1)S(1)}, u32[]{:S(2)}, u32[]{:S(2)}) collective-permute-start(bf16[128,384]{1,0:T(8,128)(2,1)S(1)} %get-tuple-element.42), channel_id=1, source_target_pairs={{0,4},{4,8},{8,12},{1,5},{5,9},{9,13},{2,6},{6,10},{10,14},{3,7},{... | collective-permute-start | bytes 294920 | tf_op jit(solution)/shard_map/ppermute | solution.py:648
  8.4 9.1 %route.1 = (bf16[1,72,1024]{2,1,0:T(8,128)(2,1)S(1)}, bf16[1,72,1024]{2,1,0:T(8,128)(2,1)S(1)}, bf16[2,72,1024]{2,1,0:T(8,128)(2,1)}, bf16[2,72,1024]{2,1,0:T(8,128)(2,1)}, bf16[2,72,1024]{2,1,0:T(8,128)(2,1)}) custom-call(s32[5]{0:T(128)S(1)} %stack.43.index_ref, s32[32,128]{1,0:T(8,128)S(1)} %bitcast.67, bf16[32,128]{1,0:T(8,128)(2,1)S(1)} %bitcast.69, ...), custom_call_target="tpu_custom_call" | custom-call | flops 1342177280 | bytes 1179648 | tf_op jit(solution)/shard_map/route/pallas_call | solution.py:185
  18.8 3.7 %collective-permute-start.2 = (bf16[2,72,1024]{2,1,0:T(8,128)(2,1)}, bf16[2,72,1024]{2,1,0:T(8,128)(2,1)S(1)}, u32[]{:S(2)}, u32[]{:S(2)}) collective-permute-start(bf16[2,72,1024]{2,1,0:T(8,128)(2,1)} %get-tuple-element.35), channel_id=1, source_target_pairs={{0,8},{4,12},{8,0},{12,4},{1,9},{5,13},{9,1},{13,5},{2,10},{6,14},... | collective-permute-start | bytes 884744 | tf_op jit(solution)/shard_map/ppermute | solution.py:608
  25.3 1.5 %collective-permute-start.13 = (bf16[3,3,128,128]{2,3,1,0:T(8,128)(2,1)S(1)}, bf16[3,3,128,128]{2,3,1,0:T(8,128)(2,1)S(1)}, u32[]{:S(2)}, u32[]{:S(2)}) collective-permute-start(bf16[3,3,128,128]{2,3,1,0:T(8,128)(2,1)S(1)} %fusion), channel_id=1, source_target_pairs={{0,2},{2,0},{1,3},{3,1},{4,6},{6,4},{5,7},{7,5},{8,10},{10,8},{9,1... | collective-permute-start | bytes 884744 | tf_op jit(solution)/shard_map/ppermute | solution.py:604
  27.4 7.8 %collective-permute-done.13 = bf16[3,3,128,128]{2,3,1,0:T(8,128)(2,1)S(1)} collective-permute-done((bf16[3,3,128,128]{2,3,1,0:T(8,128)(2,1)S(1)}, bf16[3,3,128,128]{2,3,1,0:T(8,128)(2,1)S(1)}, u32[]{:S(2)}, u32[]{:S(2)}) %collective-permute-start.13) | collective-permute-done | bytes 294944 | tf_op jit(solution)/shard_map/ppermute | solution.py:604
  35.2 1.5 %collective-permute-start.16 = (bf16[128,8,384]{2,0,1:T(8,128)(2,1)S(1)}, bf16[128,8,384]{2,0,1:T(8,128)(2,1)S(1)}, u32[]{:S(2)}, u32[]{:S(2)}) collective-permute-start(bf16[128,8,384]{2,0,1:T(8,128)(2,1)S(1)} %copy.77), channel_id=1, source_target_pairs={{0,2},{2,0},{1,3},{3,1},{4,6},{6,4},{5,7},{7,5},{8,10},{10,8},{9,1... | collective-permute-start | bytes 2359304 | tf_op jit(solution)/shard_map/ppermute | solution.py:604
  39.1 3.9 %collective-permute-done.2.rest_0_ = bf16[2,72,1024]{2,1,0:T(8,128)(2,1)S(1)} collective-permute-done((bf16[2,72,1024]{2,1,0:T(8,128)(2,1)}, bf16[2,72,1024]{2,1,0:T(8,128)(2,1)S(1)}, u32[]{:S(2)}, u32[]{:S(2)}) %collective-permute-start.2) | collective-permute-done | bytes 294944 | tf_op jit(solution)/shard_map/ppermute | solution.py:608
  43.0 1.5 %collective-permute-start.1 = (f32[128]{0:T(128)S(1)}, f32[128]{0:T(128)S(1)}, u32[]{:S(2)}, u32[]{:S(2)}) collective-permute-start(f32[128]{0:T(128)S(1)} %copy-done.16), channel_id=1, source_target_pairs={{0,2},{2,0},{1,3},{3,1},{4,6},{6,4},{5,7},{7,5},{8,10},{10,8},{9,1... | collective-permute-start | bytes 1544 | tf_op jit(solution)/shard_map/ppermute | solution.py:604
  48.2 2.6 %grid_part.2.rest_2_ = f32[576,384]{1,0:T(8,128)S(1)} custom-call(bf16[1,72,1024]{2,1,0:T(8,128)(2,1)S(1)} %copy-done.11, bf16[1,72,1024]{2,1,0:T(8,128)(2,1)S(1)} %collective-permute-done.6.rest_1_, bf16[2,72,1024]{2,1,0:T(8,128)(2,1)S(1)} %collective-permute-done.7.rest_2_, bf16[1,72,1024]{2,1,0:T(8,128)(2,1)S(1)} %collective-permute-done.8.rest_3_), custom_call_target="tpu_custom_call" | custom-call | flops 1811939328 | bytes 589824 | tf_op jit(solution)/shard_map/grid_part/pallas_call | solution.py:276
  53.8 7.4 %collective-permute-start.9 = (bf16[2,72,384]{2,1,0:T(8,128)(2,1)S(1)}, bf16[2,72,384]{2,1,0:T(8,128)(2,1)S(1)}, u32[]{:S(2)}, u32[]{:S(2)}) collective-permute-start(bf16[2,72,384]{2,1,0:T(8,128)(2,1)S(1)} %bitcast.84), channel_id=1, source_target_pairs={{0,4},{4,8},{8,12},{1,5},{5,9},{9,13},{2,6},{6,10},{10,14},{3,7},{... | collective-permute-start | bytes 331784 | tf_op jit(solution)/shard_map/ppermute | solution.py:612
  61.8 2.0 %collective-permute-done.9 = bf16[2,72,384]{2,1,0:T(8,128)(2,1)S(1)} collective-permute-done((bf16[2,72,384]{2,1,0:T(8,128)(2,1)S(1)}, bf16[2,72,384]{2,1,0:T(8,128)(2,1)S(1)}, u32[]{:S(2)}, u32[]{:S(2)}) %collective-permute-start.9) | collective-permute-done | bytes 110624 | tf_op jit(solution)/shard_map/ppermute | solution.py:612
  63.7 1.5 %collective-permute-start.10 = (bf16[2,72,384]{2,1,0:T(8,128)(2,1)S(1)}, bf16[2,72,384]{2,1,0:T(8,128)(2,1)S(1)}, u32[]{:S(2)}, u32[]{:S(2)}) collective-permute-start(bf16[2,72,384]{2,1,0:T(8,128)(2,1)S(1)} %bitcast.83), channel_id=1, source_target_pairs={{4,0},{8,4},{12,8},{5,1},{9,5},{13,9},{6,2},{10,6},{14,10},{7,3},{... | collective-permute-start | bytes 331784 | tf_op jit(solution)/shard_map/ppermute | solution.py:613
  65.2 5.6 %collective-permute-done.10 = bf16[2,72,384]{2,1,0:T(8,128)(2,1)S(1)} collective-permute-done((bf16[2,72,384]{2,1,0:T(8,128)(2,1)S(1)}, bf16[2,72,384]{2,1,0:T(8,128)(2,1)S(1)}, u32[]{:S(2)}, u32[]{:S(2)}) %collective-permute-start.10) | collective-permute-done | bytes 110624 | tf_op jit(solution)/shard_map/ppermute | solution.py:613
  71.7 2.3 %collective-permute-done.11.peer_ref = bf16[8,72,384]{2,1,0:T(8,128)(2,1)S(1)} collective-permute-done((bf16[8,72,384]{2,1,0:T(8,128)(2,1)S(1)}, bf16[8,72,384]{2,1,0:T(8,128)(2,1)S(1)}, u32[]{:S(2)}, u32[]{:S(2)}) %collective-permute-start.11) | collective-permute-done | bytes 442400 | tf_op jit(solution)/shard_map/ppermute | solution.py:604
  74.0 3.7 %back.1.back_ref = f32[128,3072]{1,0:T(8,128)S(1)} custom-call(s32[5]{0:T(128)S(1)} %stack.43.index_ref, bf16[3,128,768]{2,1,0:T(8,128)(2,1)S(1)} %copy.69.kernel_ref, bf16[8,128,384]{2,1,0:T(8,128)(2,1)S(1)} %bitcast.59, bf16[2,128,384]{2,1,0:T(8,128)(2,1)S(1)} %pad_maximum_fusion.1.rest_1_, bf16[8,128,384]{2,1,0:T(8,128)(2,1)S(1)} %bitcast.65, ...), custom_call_target="tpu_custom_call" | custom-call | flops 2264924160 | bytes 1966080 | tf_op jit(solution)/shard_map/back/pallas_call | solution.py:329
  82.9 10.2 %grads.1 = (bf16[10,256,512]{2,1,0:T(8,128)(2,1)}, f32[256,768]{1,0:T(8,128)S(1)}, bf16[256,768]{1,0:T(8,128)(2,1)}) custom-call(s32[5]{0:T(128)S(1)} %stack.43.index_ref, bf16[3,256,192]{2,1,0:T(8,128)(2,1)S(1)} %copy.70.kernel_ref, f32[256,1]{1,0:T(8,128)S(1)} %broadcast_select_fusion.gain_ref, f32[8,72,384]{2,1,0:T(8,128)} %bitcast.70, ...), custom_call_target="tpu_custom_call" | custom-call | flops 3397386240 | bytes 5898240 | tf_op jit(solution)/shard_map/grads/pallas_call | solution.py:473
  95.6 2.4 %collective-permute-start.21 = (bf16[64,768]{1,0:T(8,128)(2,1)S(1)}, bf16[64,768]{1,0:T(8,128)(2,1)S(1)}, u32[]{:S(2)}, u32[]{:S(2)}) collective-permute-start(bf16[64,768]{1,0:T(8,128)(2,1)S(1)} %get-tuple-element.49), channel_id=1, source_target_pairs={{0,4},{4,0},{8,12},{12,8},{1,5},{5,1},{9,13},{13,9},{2,6},{6,2},{1... | collective-permute-start | bytes 294920 | tf_op jit(solution)/shard_map/ppermute | solution.py:608
  100.7 1.7 %copy-done.8 = bf16[10,256,512]{2,1,0:T(8,128)(2,1)S(1)} copy-done((bf16[10,256,512]{2,1,0:T(8,128)(2,1)S(1)}, bf16[10,256,512]{2,1,0:T(8,128)(2,1)}, u32[]{:S(2)}) %copy-start.8) | copy-done | bytes 2621464
  102.4 3.4 %encode.1 = bf16[8,128,384]{2,1,0:T(8,128)(2,1)S(1)} custom-call(bf16[3,128,768]{2,1,0:T(8,128)(2,1)S(1)} %copy.72.kernel_ref, bf16[10,256,512]{2,1,0:T(8,128)(2,1)S(1)} %copy-done.8), custom_call_target="tpu_custom_call" | custom-call | flops 2264924160 | bytes 2621440 | tf_op jit(solution)/shard_map/encode/pallas_call | solution.py:515
  105.8 2.8 %collective-permute-done.22 = bf16[64,768]{1,0:T(8,128)(2,1)S(1)} collective-permute-done((bf16[64,768]{1,0:T(8,128)(2,1)S(1)}, bf16[64,768]{1,0:T(8,128)(2,1)S(1)}, u32[]{:S(2)}, u32[]{:S(2)}) %collective-permute-start.22) | collective-permute-done | bytes 98336 | tf_op jit(solution)/shard_map/ppermute | solution.py:608
  108.7 2.3 %collective-permute-start.26 = (bf16[64,768]{1,0:T(8,128)(2,1)S(1)}, bf16[64,768]{1,0:T(8,128)(2,1)S(1)}, u32[]{:S(2)}, u32[]{:S(2)}) collective-permute-start(bf16[64,768]{1,0:T(8,128)(2,1)S(1)} %add_convert_fusion), channel_id=1, source_target_pairs={{0,12},{4,8},{8,4},{12,0},{1,13},{5,9},{9,5},{13,1},{2,14},{6,10},... | collective-permute-start | bytes 294920 | tf_op jit(solution)/shard_map/ppermute | solution.py:608
  113.1 2.9 %collective-permute-done.26 = bf16[64,768]{1,0:T(8,128)(2,1)S(1)} collective-permute-done((bf16[64,768]{1,0:T(8,128)(2,1)S(1)}, bf16[64,768]{1,0:T(8,128)(2,1)S(1)}, u32[]{:S(2)}, u32[]{:S(2)}) %collective-permute-start.26) | collective-permute-done | bytes 98336 | tf_op jit(solution)/shard_map/ppermute | solution.py:608
  116.0 4.0 %collective-permute-done.25 = bf16[64,768]{1,0:T(8,128)(2,1)S(1)} collective-permute-done((bf16[64,768]{1,0:T(8,128)(2,1)S(1)}, bf16[64,768]{1,0:T(8,128)(2,1)S(1)}, u32[]{:S(2)}, u32[]{:S(2)}) %collective-permute-start.25) | collective-permute-done | bytes 98336 | tf_op jit(solution)/shard_map/ppermute | solution.py:608
  121.8 1.8 %finish.1 = (f32[3,3,128,256]{3,2,1,0:T(8,128)}, f32[3,3,64,128]{3,2,1,0:T(8,128)}, f32[1,128]{1,0:T(1,128)}) custom-call(s32[5]{0:T(128)S(1)} %stack.43.index_ref, bf16[4,64,768]{2,1,0:T(8,128)(2,1)S(1)} %pad_maximum_fusion.mine_ref, bf16[4,64,768]{2,1,0:T(8,128)(2,1)S(1)} %collective-permute-done.27.other_ref), custom_call_target="tpu_custom_call" | custom-call | flops 196608 | bytes 2359296 | tf_op jit(solution)/shard_map/finish/pallas_call | solution.py:579
  (113 shorter events, 32.1 us)
Async XLA Ops:
  2.0 23.3 %collective-permute-start.14 = (bf16[128,384]{1,0:T(8,128)(2,1)S(1)}, bf16[128,384]{1,0:T(8,128)(2,1)S(1)}, u32[]{:S(2)}, u32[]{:S(2)}) collective-permute-start(bf16[128,384]{1,0:T(8,128)(2,1)S(1)} %get-tuple-element.42), channel_id=1, source_target_pairs={{0,4},{4,8},{8,12},{1,5},{5,9},{9,13},{2,6},{6,10},{10,14},{3,7},{... | collective-permute-start | bytes 294920 | tf_op jit(solution)/shard_map/ppermute | solution.py:648
  6.9 19.8 %collective-permute-start.15 = (bf16[128,384]{1,0:T(8,128)(2,1)S(1)}, bf16[128,384]{1,0:T(8,128)(2,1)S(1)}, u32[]{:S(2)}, u32[]{:S(2)}) collective-permute-start(bf16[128,384]{1,0:T(8,128)(2,1)S(1)} %get-tuple-element.43), channel_id=1, source_target_pairs={{4,0},{8,4},{12,8},{5,1},{9,5},{13,9},{6,2},{10,6},{14,10},{7,3},{... | collective-permute-start | bytes 294920 | tf_op jit(solution)/shard_map/ppermute | solution.py:649
  18.8 24.2 %collective-permute-start.2 = (bf16[2,72,1024]{2,1,0:T(8,128)(2,1)}, bf16[2,72,1024]{2,1,0:T(8,128)(2,1)S(1)}, u32[]{:S(2)}, u32[]{:S(2)}) collective-permute-start(bf16[2,72,1024]{2,1,0:T(8,128)(2,1)} %get-tuple-element.35), channel_id=1, source_target_pairs={{0,8},{4,12},{8,0},{12,4},{1,9},{5,13},{9,1},{13,5},{2,10},{6,14},... | collective-permute-start | bytes 884744 | tf_op jit(solution)/shard_map/ppermute | solution.py:608
  22.4 22.1 %collective-permute-start.4 = (bf16[2,72,1024]{2,1,0:T(8,128)(2,1)}, bf16[2,72,1024]{2,1,0:T(8,128)(2,1)S(1)}, u32[]{:S(2)}, u32[]{:S(2)}) collective-permute-start(bf16[2,72,1024]{2,1,0:T(8,128)(2,1)} %get-tuple-element.36), channel_id=1, source_target_pairs={{0,12},{4,8},{8,4},{12,0},{1,13},{5,9},{9,5},{13,1},{2,14},{6,10},... | collective-permute-start | bytes 884744 | tf_op jit(solution)/shard_map/ppermute | solution.py:608
  23.8 21.3 %collective-permute-start.7 = (bf16[2,72,1024]{2,1,0:T(8,128)(2,1)}, bf16[2,72,1024]{2,1,0:T(8,128)(2,1)S(1)}, u32[]{:S(2)}, u32[]{:S(2)}) collective-permute-start(bf16[2,72,1024]{2,1,0:T(8,128)(2,1)} %get-tuple-element.38), channel_id=1, source_target_pairs={{0,4},{4,0},{8,12},{12,8},{1,5},{5,1},{9,13},{13,9},{2,6},{6,2},{1... | collective-permute-start | bytes 884744 | tf_op jit(solution)/shard_map/ppermute | solution.py:608
  25.3 9.9 %collective-permute-start.13 = (bf16[3,3,128,128]{2,3,1,0:T(8,128)(2,1)S(1)}, bf16[3,3,128,128]{2,3,1,0:T(8,128)(2,1)S(1)}, u32[]{:S(2)}, u32[]{:S(2)}) collective-permute-start(bf16[3,3,128,128]{2,3,1,0:T(8,128)(2,1)S(1)} %fusion), channel_id=1, source_target_pairs={{0,2},{2,0},{1,3},{3,1},{4,6},{6,4},{5,7},{7,5},{8,10},{10,8},{9,1... | collective-permute-start | bytes 884744 | tf_op jit(solution)/shard_map/ppermute | solution.py:604
  26.8 18.5 %collective-permute-start.17 = (bf16[2,128,384]{2,1,0:T(8,128)(2,1)S(1)}, bf16[2,128,384]{2,1,0:T(8,128)(2,1)S(1)}, u32[]{:S(2)}, u32[]{:S(2)}) collective-permute-start(bf16[2,128,384]{2,1,0:T(8,128)(2,1)S(1)} %pad_maximum_fusion.1.rest_1_), channel_id=1, source_target_pairs={{0,2},{2,0},{1,3},{3,1},{4,6},{6,4},{5,7},{7,5},{8,10},{10,8},{9,1... | collective-permute-start | bytes 589832 | tf_op jit(solution)/shard_map/ppermute | solution.py:604
  35.2 36.3 %collective-permute-start.16 = (bf16[128,8,384]{2,0,1:T(8,128)(2,1)S(1)}, bf16[128,8,384]{2,0,1:T(8,128)(2,1)S(1)}, u32[]{:S(2)}, u32[]{:S(2)}) collective-permute-start(bf16[128,8,384]{2,0,1:T(8,128)(2,1)S(1)} %copy.77), channel_id=1, source_target_pairs={{0,2},{2,0},{1,3},{3,1},{4,6},{6,4},{5,7},{7,5},{8,10},{10,8},{9,1... | collective-permute-start | bytes 2359304 | tf_op jit(solution)/shard_map/ppermute | solution.py:604
  43.0 36.0 %collective-permute-start.1 = (f32[128]{0:T(128)S(1)}, f32[128]{0:T(128)S(1)}, u32[]{:S(2)}, u32[]{:S(2)}) collective-permute-start(f32[128]{0:T(128)S(1)} %copy-done.16), channel_id=1, source_target_pairs={{0,2},{2,0},{1,3},{3,1},{4,6},{6,4},{5,7},{7,5},{8,10},{10,8},{9,1... | collective-permute-start | bytes 1544 | tf_op jit(solution)/shard_map/ppermute | solution.py:604
  44.5 34.9 %collective-permute-start = (bf16[3,3,64,128]{3,2,1,0:T(8,128)(2,1)}, bf16[3,3,64,128]{3,2,1,0:T(8,128)(2,1)}, u32[]{:S(2)}, u32[]{:S(2)}) collective-permute-start(bf16[3,3,64,128]{3,2,1,0:T(8,128)(2,1)} %bitcast.81), channel_id=1, source_target_pairs={{0,2},{2,0},{1,3},{3,1},{4,6},{6,4},{5,7},{7,5},{8,10},{10,8},{9,1... | collective-permute-start | bytes 442376 | tf_op jit(solution)/shard_map/ppermute | solution.py:604
  46.8 5.5 %collective-permute-start.3 = (bf16[1,72,1024]{2,1,0:T(8,128)(2,1)S(1)}, bf16[1,72,1024]{2,1,0:T(8,128)(2,1)S(1)}, u32[]{:S(2)}, u32[]{:S(2)}) collective-permute-start(bf16[1,72,1024]{2,1,0:T(8,128)(2,1)S(1)} %slice.154), channel_id=1, source_target_pairs={{0,1},{1,0},{2,3},{3,2},{4,5},{5,4},{6,7},{7,6},{8,9},{9,8},{10,11... | collective-permute-start | bytes 442376 | tf_op jit(solution)/shard_map/ppermute | solution.py:600
  47.0 5.3 %collective-permute-start.5 = (bf16[1,72,1024]{2,1,0:T(8,128)(2,1)S(1)}, bf16[1,72,1024]{2,1,0:T(8,128)(2,1)S(1)}, u32[]{:S(2)}, u32[]{:S(2)}) collective-permute-start(bf16[1,72,1024]{2,1,0:T(8,128)(2,1)S(1)} %slice.155), channel_id=1, source_target_pairs={{0,1},{1,0},{2,3},{3,2},{4,5},{5,4},{6,7},{7,6},{8,9},{9,8},{10,11... | collective-permute-start | bytes 442376 | tf_op jit(solution)/shard_map/ppermute | solution.py:600
  53.8 10.0 %collective-permute-start.9 = (bf16[2,72,384]{2,1,0:T(8,128)(2,1)S(1)}, bf16[2,72,384]{2,1,0:T(8,128)(2,1)S(1)}, u32[]{:S(2)}, u32[]{:S(2)}) collective-permute-start(bf16[2,72,384]{2,1,0:T(8,128)(2,1)S(1)} %bitcast.84), channel_id=1, source_target_pairs={{0,4},{4,8},{8,12},{1,5},{5,9},{9,13},{2,6},{6,10},{10,14},{3,7},{... | collective-permute-start | bytes 331784 | tf_op jit(solution)/shard_map/ppermute | solution.py:612
  61.2 12.8 %collective-permute-start.11 = (bf16[8,72,384]{2,1,0:T(8,128)(2,1)S(1)}, bf16[8,72,384]{2,1,0:T(8,128)(2,1)S(1)}, u32[]{:S(2)}, u32[]{:S(2)}) collective-permute-start(bf16[8,72,384]{2,1,0:T(8,128)(2,1)S(1)} %bitcast.63), channel_id=1, source_target_pairs={{0,2},{2,0},{1,3},{3,1},{4,6},{6,4},{5,7},{7,5},{8,10},{10,8},{9,1... | collective-permute-start | bytes 1327112 | tf_op jit(solution)/shard_map/ppermute | solution.py:604
  63.7 7.1 %collective-permute-start.10 = (bf16[2,72,384]{2,1,0:T(8,128)(2,1)S(1)}, bf16[2,72,384]{2,1,0:T(8,128)(2,1)S(1)}, u32[]{:S(2)}, u32[]{:S(2)}) collective-permute-start(bf16[2,72,384]{2,1,0:T(8,128)(2,1)S(1)} %bitcast.83), channel_id=1, source_target_pairs={{4,0},{8,4},{12,8},{5,1},{9,5},{13,9},{6,2},{10,6},{14,10},{7,3},{... | collective-permute-start | bytes 331784 | tf_op jit(solution)/shard_map/ppermute | solution.py:613
  70.9 8.1 %collective-permute-start.12 = (bf16[4,72,384]{2,1,0:T(8,128)(2,1)S(1)}, bf16[4,72,384]{2,1,0:T(8,128)(2,1)S(1)}, u32[]{:S(2)}, u32[]{:S(2)}) collective-permute-start(bf16[4,72,384]{2,1,0:T(8,128)(2,1)S(1)} %constant_dynamic-update-slice_fusion.edge_ref), channel_id=1, source_target_pairs={{0,2},{2,0},{1,3},{3,1},{4,6},{6,4},{5,7},{7,5},{8,10},{10,8},{9,1... | collective-permute-start | bytes 663560 | tf_op jit(solution)/shard_map/ppermute | solution.py:604
  71.6 2.5 %collective-permute-start.18 = (bf16[10,256,128]{2,1,0:T(8,128)(2,1)S(1)}, bf16[10,256,128]{2,1,0:T(8,128)(2,1)S(1)}, u32[]{:S(2)}, u32[]{:S(2)}) collective-permute-start(bf16[10,256,128]{2,1,0:T(8,128)(2,1)S(1)} %maximum_maximum_fusion), channel_id=1, source_target_pairs={{0,1},{1,0},{2,3},{3,2},{4,5},{5,4},{6,7},{7,6},{8,9},{9,8},{10,11... | collective-permute-start | bytes 1966088 | tf_op jit(solution)/shard_map/ppermute | solution.py:600
  79.0 2.1 %collective-permute-start.19 = (bf16[12,144,128]{2,1,0:T(8,128)(2,1)S(1)}, bf16[12,144,128]{2,1,0:T(8,128)(2,1)S(1)}, u32[]{:S(2)}, u32[]{:S(2)}) collective-permute-start(bf16[12,144,128]{2,1,0:T(8,128)(2,1)S(1)} %maximum_maximum_fusion.1), channel_id=1, source_target_pairs={{0,1},{1,0},{2,3},{3,2},{4,5},{5,4},{6,7},{7,6},{8,9},{9,8},{10,11... | collective-permute-start | bytes 1327112 | tf_op jit(solution)/shard_map/ppermute | solution.py:600
  95.6 10.2 %collective-permute-start.21 = (bf16[64,768]{1,0:T(8,128)(2,1)S(1)}, bf16[64,768]{1,0:T(8,128)(2,1)S(1)}, u32[]{:S(2)}, u32[]{:S(2)}) collective-permute-start(bf16[64,768]{1,0:T(8,128)(2,1)S(1)} %get-tuple-element.49), channel_id=1, source_target_pairs={{0,4},{4,0},{8,12},{12,8},{1,5},{5,1},{9,13},{13,9},{2,6},{6,2},{1... | collective-permute-start | bytes 294920 | tf_op jit(solution)/shard_map/ppermute | solution.py:608
  98.1 10.5 %collective-permute-start.22 = (bf16[64,768]{1,0:T(8,128)(2,1)S(1)}, bf16[64,768]{1,0:T(8,128)(2,1)S(1)}, u32[]{:S(2)}, u32[]{:S(2)}) collective-permute-start(bf16[64,768]{1,0:T(8,128)(2,1)S(1)} %get-tuple-element.50), channel_id=1, source_target_pairs={{0,8},{4,12},{8,0},{12,4},{1,9},{5,13},{9,1},{13,5},{2,10},{6,14},... | collective-permute-start | bytes 294920 | tf_op jit(solution)/shard_map/ppermute | solution.py:608
  99.3 9.3 %collective-permute-start.23 = (bf16[64,768]{1,0:T(8,128)(2,1)S(1)}, bf16[64,768]{1,0:T(8,128)(2,1)S(1)}, u32[]{:S(2)}, u32[]{:S(2)}) collective-permute-start(bf16[64,768]{1,0:T(8,128)(2,1)S(1)} %get-tuple-element.51), channel_id=1, source_target_pairs={{0,12},{4,8},{8,4},{12,0},{1,13},{5,9},{9,5},{13,1},{2,14},{6,10},... | collective-permute-start | bytes 294920 | tf_op jit(solution)/shard_map/ppermute | solution.py:608
  108.7 7.4 %collective-permute-start.26 = (bf16[64,768]{1,0:T(8,128)(2,1)S(1)}, bf16[64,768]{1,0:T(8,128)(2,1)S(1)}, u32[]{:S(2)}, u32[]{:S(2)}) collective-permute-start(bf16[64,768]{1,0:T(8,128)(2,1)S(1)} %add_convert_fusion), channel_id=1, source_target_pairs={{0,12},{4,8},{8,4},{12,0},{1,13},{5,9},{9,5},{13,1},{2,14},{6,10},... | collective-permute-start | bytes 294920 | tf_op jit(solution)/shard_map/ppermute | solution.py:608
  111.0 9.0 %collective-permute-start.25 = (bf16[64,768]{1,0:T(8,128)(2,1)S(1)}, bf16[64,768]{1,0:T(8,128)(2,1)S(1)}, u32[]{:S(2)}, u32[]{:S(2)}) collective-permute-start(bf16[64,768]{1,0:T(8,128)(2,1)S(1)} %add_convert_fusion), channel_id=1, source_target_pairs={{0,8},{4,12},{8,0},{12,4},{1,9},{5,13},{9,1},{13,5},{2,10},{6,14},... | collective-permute-start | bytes 294920 | tf_op jit(solution)/shard_map/ppermute | solution.py:608
  112.0 8.0 %collective-permute-start.24 = (bf16[64,768]{1,0:T(8,128)(2,1)S(1)}, bf16[64,768]{1,0:T(8,128)(2,1)S(1)}, u32[]{:S(2)}, u32[]{:S(2)}) collective-permute-start(bf16[64,768]{1,0:T(8,128)(2,1)S(1)} %add_convert_fusion), channel_id=1, source_target_pairs={{0,4},{4,0},{8,12},{12,8},{1,5},{5,1},{9,13},{13,9},{2,6},{6,2},{1... | collective-permute-start | bytes 294920 | tf_op jit(solution)/shard_map/ppermute | solution.py:608
  (21 other events, 105.6 us)

commit v4 on v3

--- a/solution.py
+++ b/solution.py
@@ -36,7 +36,7 @@
     return pl.BlockSpec(memory_space=pltpu.SMEM)
 
 
-def call(kernel, out_shape, in_specs, scratch, flops, moved, name, vmem=48):
+def call(kernel, out_shape, in_specs, scratch, flops, moved, name, vmem=32):
     n_out = len(out_shape) if isinstance(out_shape, (tuple, list)) else None
     out_specs = vmem_spec() if n_out is None else [vmem_spec() for _ in range(n_out)]
     return pl.pallas_call(
@@ -202,7 +202,6 @@
         2 * n_obs * n_tiles * BLOCK * 80,
         n_tiles * rows * cap * 2,
         "route",
-        24,
     )(
         index,
         obs_tile.reshape(n_lines, LANES),
@@ -284,7 +283,6 @@
         2 * n_send * cap * total * n_cols,
         n_send * rows * cap * 2,
         "grid_last" if last else "grid_part",
-        32,
     )(*ins)
 
 
@@ -334,7 +332,6 @@
         2 * n_ext * 9 * all_chans * n_out * n_cols,
         n_ext * all_chans * n_cols * 2,
         "back",
-        32,
     )(index, kernel, *[x for piece in pieces for x in piece], side)
 
 
@@ -347,7 +344,7 @@
         keep_out, give_out = rest.pop(0), rest.pop(0)
     else:
         all_out = rest.pop(0)
-    taps_ref, logs_ref, pre_ref, wide_ref, out_left_ref, pre_left_ref, acc_ref = rest
+    taps_ref, logs_ref, wide_ref, out_left_ref, pre_left_ref, acc_ref = rest
     n_rows, own, n_cols = cot_ref.shape
     n_hidden = kernel_ref.shape[1]
     rows = chans + META
@@ -398,7 +395,7 @@
                 pre_left_ref[put, h * width : h * width + n_cols] = nothing
         pre_left_ref[:, h * width + n_cols : (h + 1) * width] = jnp.zeros((3 * own, LANES), BF16)
 
-    gain = gain_ref[...]
+    gain = gain_ref[:, 0:1]
     keep_one = lane_mask((1, width), n_cols, sub, 1)
     group = 2
     for first in range(0, n_rows + 2, group):
@@ -417,22 +414,21 @@
             elif h == n_rows + 1:
                 keep = keep & (tile < n_tile - 1)
             else:
-                pre_ref[:, (h - 1) * n_cols : h * n_cols] = pre[:, :n_cols]
+                mine = pre[0:own, :n_cols]
+                for c in range(1, n_hidden // own):
+                    mine = jnp.where(chan == c, pre[c * own : (c + 1) * own, :n_cols], mine)
+                s = 0.5 + 0.5 * jnp.tanh(0.5 * mine)
+                there = slice((h - 1) * n_cols, h * n_cols)
+                grad = (back_ref[:, there] * s * (1.0 + mine * (1.0 - s))).astype(BF16)
+                for a in range(3):
+                    put = (h - 1 + a) * width
+                    pre_left_ref[a * own : (a + 1) * own, put : put + n_cols] = grad
             half = 0.5 * pre
             hidden = jnp.where(keep, half + half * jnp.tanh(half), 0.0)
             hidden_ref[h] = hidden.astype(BF16)
             wide_ref[0:n_hidden, at] = pltpu.roll(hidden, 1, 1)[:, :n_cols].astype(BF16)
             wide_ref[n_hidden : 2 * n_hidden, at] = hidden[:, :n_cols].astype(BF16)
             wide_ref[2 * n_hidden :, at] = pltpu.roll(hidden, width - 1, 1)[:, :n_cols].astype(BF16)
-
-    for r in range(n_rows):
-        at = slice(r * n_cols, (r + 1) * n_cols)
-        mine = pre_ref[pl.ds(pl.multiple_of(chan * own, own), own), at]
-        s = 0.5 + 0.5 * jnp.tanh(0.5 * mine)
-        grad = (back_ref[:, at] * s * (1.0 + mine * (1.0 - s))).astype(BF16)
-        for a in range(3):
-            h = r + a
-            pre_left_ref[a * own : (a + 1) * own, h * width : h * width + n_cols] = grad
 
     three = 3 * own
     lanes = 3 * n_hidden
@@ -477,7 +473,6 @@
         [
             pltpu.VMEM((3 * chans + 16, (n_rows + 4) * width), BF16),
             pltpu.VMEM((n_rows + 4, 1, width), F32),
-            pltpu.VMEM((n_hidden, n_rows * n_cols), F32),
             pltpu.VMEM((3 * n_hidden, (n_rows + 2) * n_cols), BF16),
             pltpu.VMEM((3 * n_own, (n_rows + 2) * n_cols), BF16),
             pltpu.VMEM((3 * n_own, (n_rows + 2) * width), BF16),
@@ -486,7 +481,6 @@
         2 * (n_rows + 2) * 9 * n_cols * n_hidden * (n_own + chans),
         (n_rows + 2) * 3 * n_hidden * n_cols * 2,
         "grads",
-        50,
     )(index, kernel, gain, *ins)
 
 
@@ -520,7 +514,6 @@
         2 * n_ext * 9 * own * n_hidden * n_cols,
         hidden.size * 2,
         "encode",
-        32,
     )(kernel, hidden)
 
 
@@ -543,7 +536,6 @@
         rows * lanes,
         rows * lanes * 8,
         "quarters",
-        16,
     )(index, keep, got)
 
 
@@ -588,8 +580,82 @@
         n * rows * lanes,
         n * rows * lanes * 12,
         "finish",
-        24,
     )(index, mine, other)
+
+
+def offer_kernel(index_ref, two_ref, one_ref, gain_ref, out_ref):
+    own = two_ref.shape[2]
+    chans = one_ref.shape[2]
+    at = pl.ds(pl.multiple_of((1 - index_ref[1]) * own, own), own)
+    gain = gain_ref[...]
+    high = gain.astype(BF16).astype(F32)
+    middle = (gain - high).astype(BF16).astype(F32)
+    line = iota((8, own), 0)
+    terms = jnp.where(
+        line == 0, high, jnp.where(line == 1, middle, jnp.where(line == 2, gain - high - middle, 0.0))
+    ).astype(BF16)
+    for a in range(3):
+        for b in range(3):
+            out_ref[a, b, 0:own] = two_ref[a, b, :, at]
+            out_ref[a, b, own : own + chans] = one_ref[a, b]
+            out_ref[a, b, own + chans :] = terms
+
+
+def offer(index, two, one, gain):
+    own, chans = two.shape[2], one.shape[2]
+    return call(
+        offer_kernel,
+        jax.ShapeDtypeStruct((3, 3, own + chans + 8, own), BF16),
+        [smem_spec()] + [vmem_spec()] * 3,
+        [],
+        9 * own * (own + chans),
+        9 * own * (own + chans) * 4,
+        "offer",
+    )(index, two, one, gain[None])
+
+
+def arrange_kernel(index_ref, two_ref, one_ref, gain_ref, theirs_ref, back_ref, code_ref, first_ref, column_ref):
+    own = two_ref.shape[2]
+    chans = one_ref.shape[2]
+    chan = index_ref[1]
+    mine = pl.ds(pl.multiple_of(chan * own, own), own)
+    peer = pl.ds(pl.multiple_of((1 - chan) * own, own), own)
+
+    def turned(block):
+        return block.astype(F32).T.astype(BF16)
+
+    for a in range(3):
+        for b in range(3):
+            left = b * 2 * own
+            back_ref[a, :, left : left + own] = turned(two_ref[a, b, :, mine])
+            back_ref[a, :, left + own : left + 2 * own] = turned(theirs_ref[a, b, 0:own])
+            code_ref[a, :, left : left + 2 * own] = two_ref[a, b]
+        first_ref[a, mine, :] = turned(jnp.concatenate([one_ref[a, b] for b in range(3)], axis=0))
+        first_ref[a, peer, :] = turned(
+            jnp.concatenate([theirs_ref[a, b, own : own + chans] for b in range(3)], axis=0)
+        )
+    terms = theirs_ref[0, 0, own + chans :].astype(F32)
+    other = terms[0:1] + terms[1:2] + terms[2:3]
+    column_ref[mine, :] = jnp.broadcast_to(gain_ref[...], (own, own)).T
+    column_ref[peer, :] = jnp.broadcast_to(other, (own, own)).T
+
+
+def arrange(index, two, one, gain, theirs):
+    own, chans = two.shape[2], one.shape[2]
+    return call(
+        arrange_kernel,
+        [
+            jax.ShapeDtypeStruct((3, own, 6 * own), BF16),
+            jax.ShapeDtypeStruct((3, own, 6 * own), BF16),
+            jax.ShapeDtypeStruct((3, 2 * own, 3 * chans), BF16),
+            jax.ShapeDtypeStruct((2 * own, LANES), F32),
+        ],
+        [smem_spec()] + [vmem_spec()] * 4,
+        [],
+        9 * own * (4 * own + 2 * chans),
+        9 * own * (4 * own + 2 * chans) * 4,
+        "arrange",
+    )(index, two, one, gain[None], theirs)
 
 
 def step_perm(count, by):
@@ -633,7 +699,7 @@
     n_tile = lax.axis_size("tile")
     n_sub = lax.axis_size("sub")
     n_chan = lax.axis_size("chan")
-    pair = n_chan == 2
+    pair = n_chan == 2 and own == LANES
     n_tiles = n_tile * n_sub
     chans = obs_values.shape[1]
     n_hidden = own * n_chan
@@ -642,73 +708,66 @@
     index = jnp.stack([tile, chan, sub, jnp.int32(n_tile), tile * n_sub + sub]).astype(jnp.int32)
 
     bottom, top = cotangent[:, -1], cotangent[:, 0]
-    obs_tile, bottom, top = lax.optimization_barrier((obs_tile, bottom, top))
-    cot_edge = jnp.stack(
-        [
-            lax.ppermute(bottom, "tile", step_perm(n_tile, 1)),
-            lax.ppermute(top, "tile", step_perm(n_tile, -1)),
-        ]
-    )
-    cot = cotangent.transpose(1, 0, 2)
+    one_own = conv_one.transpose(0, 1, 3, 2)
     if pair:
-        cot_peer = swap_chan(cotangent).transpose(1, 0, 2)
-        pieces = [(cot, cot_edge), (cot_peer, swap_chan(cot_edge))]
-    else:
-        pieces = [
-            (
-                lax.all_gather(cot, "chan", axis=1, tiled=True),
-                lax.all_gather(cot_edge, "chan", axis=1, tiled=True),
-            )
-        ]
-    cot_side = side_rows(pieces, sub)
+        offered = offer(index, conv_two, one_own, density_gain)
+        obs_tile, bottom, top, offered = lax.optimization_barrier((obs_tile, bottom, top, offered))
+        theirs = swap_chan(offered)
+    low = lax.ppermute(bottom, "tile", step_perm(n_tile, 1))
+    high = lax.ppermute(top, "tile", step_perm(n_tile, -1))
 
     few = n_tiles == 8
     sent = route(index, obs_values, obs_weight, obs_tile, obs_cell, n_tiles, cap, few)
+    if pair:
+        sent, low, high, theirs = lax.optimization_barrier((sent, low, high, theirs))
     if few:
+        beside = swap_sub(sent[1])
         far = [swap_tile(sent[k + 1], n_tile, k) for k in (1, 2, 3)]
         steps = [
-            [(sent[0], 1), (swap_sub(sent[1]), 1), (far[0], 1), (swap_sub(far[0][1:]), 1)],
-            [(far[1], 1), (far[2], 1)],
+            [(sent[0], 1), (beside, 1)],
+            [(far[0], 1), (swap_sub(far[0][1:]), 1), (far[1], 1), (far[2], 1)],
             [(swap_sub(far[1][1:]), 1), (swap_sub(far[2][1:]), 1)],
         ]
     else:
         got = lax.all_to_all(sent[0], ("tile", "sub"), split_axis=0, concat_axis=0, tiled=True)
         steps = [[(got, n_tiles)]]
 
-    conv_one, conv_two, density_gain, _ = lax.optimization_barrier(
-        (conv_one, conv_two, density_gain, sent[0])
-    )
-    code_weights = conv_two.transpose(0, 2, 1, 3).reshape(3, own, 3 * n_hidden)
-    one_own = conv_one.transpose(0, 1, 3, 2)
     if pair:
-        split_two = conv_two.reshape(3, 3, own, n_chan, own)
-        halves = [split_two[:, :, :, i] for i in range(2)]
-        mine = jnp.where(chan == 0, halves[0], halves[1])
-        yours = jnp.where(chan == 0, halves[1], halves[0])
-        columns = jnp.concatenate([mine, swap_chan(yours)], axis=2)
-        one_peer = swap_chan(one_own)
-        gain_peer = swap_chan(density_gain)
-        one_full = jnp.where(
-            chan == 0,
-            jnp.concatenate([one_own, one_peer], axis=3),
-            jnp.concatenate([one_peer, one_own], axis=3),
-        )
-        gain = jnp.where(
-            chan == 0,
-            jnp.concatenate([density_gain, gain_peer]),
-            jnp.concatenate([gain_peer, density_gain]),
+        cotangent, _ = lax.optimization_barrier((cotangent, sent[0]))
+        cot = cotangent.transpose(1, 0, 2)
+        cot_edge = jnp.stack([low, high])
+        cot_peer = swap_chan(cotangent)
+        pieces = [(cot, cot_edge), (cot_peer.transpose(1, 0, 2), swap_chan(cot_edge))]
+    else:
+        cot = cotangent.transpose(1, 0, 2)
+        pieces = [
+            (
+                lax.all_gather(cot, "chan", axis=1, tiled=True),
+                lax.all_gather(jnp.stack([low, high]), "chan", axis=1, tiled=True),
+            )
+        ]
+    cot_side = side_rows(pieces, sub)
+
+    if pair:
+        back_weights, code_weights, one_weights, gain = arrange(
+            index, conv_two, one_own, density_gain, theirs
         )
     else:
         columns = lax.all_to_all(conv_two, "chan", split_axis=3, concat_axis=2, tiled=True)
         one_full = lax.all_gather(one_own, "chan", axis=3, tiled=True)
         gain = lax.all_gather(density_gain, "chan", axis=0, tiled=True)
-    back_weights = columns.transpose(0, 3, 1, 2).reshape(3, own, 3 * n_hidden)
-    one_weights = one_full.transpose(0, 3, 1, 2).reshape(3, n_hidden, 3 * chans)
-    gain = gain[:, None]
+        gain = jnp.broadcast_to(gain[:, None], (n_hidden, LANES))
+        code_weights = conv_two.transpose(0, 2, 1, 3).reshape(3, own, 3 * n_hidden)
+        back_weights = columns.transpose(0, 3, 1, 2).reshape(3, own, 3 * n_hidden)
+        one_weights = one_full.transpose(0, 3, 1, 2).reshape(3, n_hidden, 3 * chans)
 
     part = None
     for step in steps[:-1]:
         part = grid(step, part, False, n_rows, n_cols)[0]
+    if few:
+        part, back_weights, one_weights, code_weights, gain = lax.optimization_barrier(
+            (part, back_weights, one_weights, code_weights, gain)
+        )
     part, message = grid(steps[-1], part, True, n_rows, n_cols)
     shape = (n_rows, chans + META, n_cols)
     part = part.reshape(shape)

time: 124 us -> 116 us (0.935)
  local copies, waits for them, and re-layouts: 14.6 us -> 3.51 us
  waiting for transfers between devices: 33.2 us -> 41.2 us
  other arithmetic: 2.42 us -> 0.38 us
  starting transfers between devices: 38.1 us -> 36.1 us
    ppermute x9, waiting for transfers between devices: 13.6 us -> 28 us  [swap_tile(): return lax.ppermute(x, 'tile', [(i, i ^ k) for i in range(n_tile)])]
    unnamed x37 -> x18, local copies, waits for them, and re-layouts: 10 us -> 1.39 us
    ppermute x7 -> x5, waiting for transfers between devices: 10.1 us -> 4.22 us  [swap_chan(): return lax.ppermute(x, 'chan', [(0, 1), (1, 0)])]
    reshape x3 -> x0, local copies, waits for them, and re-layouts: 2.77 us -> none  [the longest x1 1.3 us: body(): code_weights = conv_two.transpose(0, 2, 1, 3).reshape(3, own, 3 * n_hidden)]
    ppermute x1, waiting for transfers between devices: 1.96 us -> 0.01 us  [edges(): low = lax.ppermute(block[-depth:], 'tile', step_perm(n_tile, 1))]
    ppermute x8, waiting for transfers between devices: 1.9 us -> 3.75 us  [swap_sub(): return lax.ppermute(x, 'sub', [(0, 1), (1, 0)])]
    slice x0 -> x1, local copies, waits for them, and re-layouts: none -> 1.82 us  [body(): bottom, top = (cotangent[:, -1], cotangent[:, 0])]
    pallas_call x1, Pallas kernels: 10.2 us -> 8.63 us  [grads(): call(body, outs, [smem_spec()] + [vmem_spec()] * (2 + len(ins)), [pltpu.V...]
  transfers between devices with their start and end apart: 28 -> 26, of which waited for: 11 -> 11; matrix products, arithmetic and copies ran while one was open for 7% -> 1% of each run, Pallas kernels for 17% -> 19%
where the time goes in v4:
time: 116 us
  waiting for transfers between devices  41.2 us (36%)
  starting transfers between devices  36.1 us (31%)
  Pallas kernels  33.3 us (29%)
  local copies, waits for them, and re-layouts  3.51 us (3%)
    ppermute x9, waiting for transfers between devices, swap_tile(): return lax.ppermute(x, 'tile', [(i, i ^ k) for i in range(n_tile)])  28 us
    ppermute x9, starting transfers between devices, swap_tile(): return lax.ppermute(x, 'tile', [(i, i ^ k) for i in range(n_tile)])  14.2 us
    pallas_call x1, Pallas kernels, grads(): call(body, outs, [smem_spec()] + [vmem_spec()] * (2 + len(ins)), [pltpu.V...  8.63 us
    pallas_call x1, Pallas kernels, route(): call(functools.partial(route_kernel, n_tiles, cap, relative), [jax.ShapeD...  8.2 us
    ppermute x5, starting transfers between devices, swap_chan(): return lax.ppermute(x, 'chan', [(0, 1), (1, 0)])  7.31 us
    ppermute x1, starting transfers between devices, edges(): low = lax.ppermute(block[-depth:], 'tile', step_perm(n_tile, 1))  7.18 us
    pallas_call x3, Pallas kernels, grid(): call(functools.partial(grid_kernel, n_rows, n_cols, group, takes, before...  5.51 us
    ppermute x1, waiting for transfers between devices, edges(): high = lax.ppermute(block[:depth], 'tile', step_perm(n_tile, -1))  5.28 us
  transfers between devices with their start and end apart: 26, of which 11 were waited for; matrix products, arithmetic and copies ran while one was open for 1% of the time, Pallas kernels for 19%

profile of v4, /device:TPU:0, one launch (start us, length us, event | category | flops | bytes accessed | tf_op | source)
XLA Modules:
  0.0 115.7 jit_solution(8768759160662332345)
XLA Ops:
  0.7 1.8 %fusion.1 = (bf16[128,1,384]{2,1,0:T(2,128)(2,1)S(1)}, bf16[128,1,384]{2,1,0:T(2,128)(2,1)S(1)}) fusion(bf16[128,8,384]{2,1,0:T(8,128)(2,1)} %param.15), kind=kLoop, calls=%fused_computation.23 | loop fusion | bytes 393216 | tf_op jit(solution)/shard_map/slice | solution.py:710
  3.3 3.0 %collective-permute-start.2 = (bf16[3,3,200,128]{3,2,1,0:T(8,128)(2,1)S(1)}, bf16[3,3,200,128]{3,2,1,0:T(8,128)(2,1)S(1)}, u32[]{:S(2)}, u32[]{:S(2)}) collective-permute-start(bf16[3,3,200,128]{3,2,1,0:T(8,128)(2,1)S(1)} %offer.1), channel_id=1, source_target_pairs={{0,2},{2,0},{1,3},{3,1},{4,6},{6,4},{5,7},{7,5},{8,10},{10,8},{9,1... | collective-permute-start | bytes 1382408 | tf_op jit(solution)/shard_map/ppermute | solution.py:670
  6.3 3.5 %collective-permute-start = (bf16[128,384]{1,0:T(8,128)(2,1)S(1)}, bf16[128,384]{1,0:T(8,128)(2,1)S(1)}, u32[]{:S(2)}, u32[]{:S(2)}) collective-permute-start(bf16[128,384]{1,0:T(8,128)(2,1)S(1)} %get-tuple-element.53), channel_id=1, source_target_pairs={{0,4},{4,8},{8,12},{1,5},{5,9},{9,13},{2,6},{6,10},{10,14},{3,7},{... | collective-permute-start | bytes 294920 | tf_op jit(solution)/shard_map/ppermute | solution.py:716
  11.1 8.2 %route.1 = (bf16[1,72,1024]{2,1,0:T(8,128)(2,1)S(1)}, bf16[1,72,1024]{2,1,0:T(8,128)(2,1)S(1)}, bf16[2,72,1024]{2,1,0:T(8,128)(2,1)S(1)}, bf16[2,72,1024]{2,1,0:T(8,128)(2,1)S(1)}, bf16[2,72,1024]{2,1,0:T(8,128)(2,1)S(1)}) custom-call(s32[5]{0:T(128)S(1)} %stack.43.index_ref, s32[32,128]{1,0:T(8,128)S(1)} %bitcast.43, bf16[32,128]{1,0:T(8,128)(2,1)S(1)} %bitcast.45, ...), custom_call_target="tpu_custom_call" | custom-call | flops 1342177280 | bytes 1179648 | tf_op jit(solution)/shard_map/route/pallas_call | solution.py:185
  20.1 2.6 %collective-permute-start.3 = (bf16[2,72,1024]{2,1,0:T(8,128)(2,1)S(1)}, bf16[2,72,1024]{2,1,0:T(8,128)(2,1)S(1)}, u32[]{:S(2)}, u32[]{:S(2)}) collective-permute-start(bf16[2,72,1024]{2,1,0:T(8,128)(2,1)S(1)} %get-tuple-element.56), channel_id=1, source_target_pairs={{0,4},{4,0},{8,12},{12,8},{1,5},{5,1},{9,13},{13,9},{2,6},{6,2},{1... | collective-permute-start | bytes 884744 | tf_op jit(solution)/shard_map/ppermute | solution.py:674
  22.7 2.6 %collective-permute-start.5 = (bf16[2,72,1024]{2,1,0:T(8,128)(2,1)S(1)}, bf16[2,72,1024]{2,1,0:T(8,128)(2,1)S(1)}, u32[]{:S(2)}, u32[]{:S(2)}) collective-permute-start(bf16[2,72,1024]{2,1,0:T(8,128)(2,1)S(1)} %get-tuple-element.57), channel_id=1, source_target_pairs={{0,8},{4,12},{8,0},{12,4},{1,9},{5,13},{9,1},{13,5},{2,10},{6,14},... | collective-permute-start | bytes 884744 | tf_op jit(solution)/shard_map/ppermute | solution.py:674
  29.5 6.3 %collective-permute-done.3.rest_0_ = bf16[2,72,1024]{2,1,0:T(8,128)(2,1)S(1)} collective-permute-done((bf16[2,72,1024]{2,1,0:T(8,128)(2,1)S(1)}, bf16[2,72,1024]{2,1,0:T(8,128)(2,1)S(1)}, u32[]{:S(2)}, u32[]{:S(2)}) %collective-permute-start.3) | collective-permute-done | bytes 294944 | tf_op jit(solution)/shard_map/ppermute | solution.py:674
  35.9 10.2 %collective-permute-done.5.rest_2_ = bf16[2,72,1024]{2,1,0:T(8,128)(2,1)S(1)} collective-permute-done((bf16[2,72,1024]{2,1,0:T(8,128)(2,1)S(1)}, bf16[2,72,1024]{2,1,0:T(8,128)(2,1)S(1)}, u32[]{:S(2)}, u32[]{:S(2)}) %collective-permute-start.5) | collective-permute-done | bytes 294944 | tf_op jit(solution)/shard_map/ppermute | solution.py:674
  46.9 2.7 %grid_part.3.rest_2_ = f32[576,384]{1,0:T(8,128)S(1)} custom-call(bf16[2,72,1024]{2,1,0:T(8,128)(2,1)S(1)} %collective-permute-done.3.rest_0_, bf16[1,72,1024]{2,1,0:T(8,128)(2,1)S(1)} %collective-permute-done.4.rest_1_, bf16[2,72,1024]{2,1,0:T(8,128)(2,1)S(1)} %collective-permute-done.5.rest_2_, bf16[2,72,1024]{2,1,0:T(8,128)(2,1)S(1)} %collective-permute-done.6.rest_3_, ...), custom_call_target="tpu_custom_call" | custom-call | flops 1811939328 | bytes 589824 | tf_op jit(solution)/shard_map/grid_part/pallas_call | solution.py:275
  51.0 7.2 %collective-permute-start.10 = (bf16[2,72,384]{2,1,0:T(8,128)(2,1)S(1)}, bf16[2,72,384]{2,1,0:T(8,128)(2,1)S(1)}, u32[]{:S(2)}, u32[]{:S(2)}) collective-permute-start(bf16[2,72,384]{2,1,0:T(8,128)(2,1)S(1)} %bitcast.53), channel_id=1, source_target_pairs={{0,4},{4,8},{8,12},{1,5},{5,9},{9,13},{2,6},{6,10},{10,14},{3,7},{... | collective-permute-start | bytes 331784 | tf_op jit(solution)/shard_map/ppermute | solution.py:678
  61.3 5.3 %collective-permute-done.11 = bf16[2,72,384]{2,1,0:T(8,128)(2,1)S(1)} collective-permute-done((bf16[2,72,384]{2,1,0:T(8,128)(2,1)S(1)}, bf16[2,72,384]{2,1,0:T(8,128)(2,1)S(1)}, u32[]{:S(2)}, u32[]{:S(2)}) %collective-permute-start.11) | collective-permute-done | bytes 110624 | tf_op jit(solution)/shard_map/ppermute | solution.py:679
  67.4 3.9 %collective-permute-done.12.peer_ref = bf16[8,72,384]{2,1,0:T(8,128)(2,1)S(1)} collective-permute-done((bf16[8,72,384]{2,1,0:T(8,128)(2,1)S(1)}, bf16[8,72,384]{2,1,0:T(8,128)(2,1)S(1)}, u32[]{:S(2)}, u32[]{:S(2)}) %collective-permute-start.12) | collective-permute-done | bytes 442400 | tf_op jit(solution)/shard_map/ppermute | solution.py:670
  71.3 3.7 %back.1.back_ref = f32[128,3072]{1,0:T(8,128)S(1)} custom-call(s32[5]{0:T(128)S(1)} %stack.43.index_ref, bf16[3,128,768]{2,1,0:T(8,128)(2,1)S(1)} %get-tuple-element.71.kernel_ref, bf16[8,128,384]{2,1,0:T(8,128)(2,1)S(1)} %bitcast.31, bf16[2,128,384]{2,1,0:T(8,128)(2,1)S(1)} %pad_maximum_fusion.1.rest_1_, bf16[8,128,384]{2,1,0:T(8,128)(2,1)S(1)} %bitcast.39, ...), custom_call_target="tpu_custom_call" | custom-call | flops 2264924160 | bytes 1966080 | tf_op jit(solution)/shard_map/back/pallas_call | solution.py:327
  75.4 1.8 %collective-permute-done.17.side_ref = bf16[12,144,128]{2,1,0:T(8,128)(2,1)S(1)} collective-permute-done((bf16[12,144,128]{2,1,0:T(8,128)(2,1)S(1)}, bf16[12,144,128]{2,1,0:T(8,128)(2,1)S(1)}, u32[]{:S(2)}, u32[]{:S(2)}) %collective-permute-start.17) | collective-permute-done | bytes 442400 | tf_op jit(solution)/shard_map/ppermute | solution.py:666
  77.2 8.6 %grads.1 = (bf16[10,256,512]{2,1,0:T(8,128)(2,1)S(1)}, f32[256,768]{1,0:T(8,128)S(1)}, bf16[256,768]{1,0:T(8,128)(2,1)S(1)}) custom-call(s32[5]{0:T(128)S(1)} %stack.43.index_ref, bf16[3,256,192]{2,1,0:T(8,128)(2,1)S(1)} %get-tuple-element.66.kernel_ref, f32[256,128]{1,0:T(8,128)S(1)} %get-tuple-element.67.gain_ref, f32[8,72,384]{2,1,0:T(8,128)S(1)} %bitcast.46, ...), custom_call_target="tpu_custom_call" | custom-call | flops 3397386240 | bytes 5898240 | tf_op jit(solution)/shard_map/grads/pallas_call | solution.py:469
  86.1 1.6 %collective-permute-done.18.got_ref = bf16[256,768]{1,0:T(8,128)(2,1)S(1)} collective-permute-done((bf16[256,768]{1,0:T(8,128)(2,1)S(1)}, bf16[256,768]{1,0:T(8,128)(2,1)S(1)}, u32[]{:S(2)}, u32[]{:S(2)}) %collective-permute-start.18) | collective-permute-done | bytes 393248 | tf_op jit(solution)/shard_map/ppermute | solution.py:666
  88.3 1.6 %collective-permute-start.19 = (bf16[64,768]{1,0:T(8,128)(2,1)S(1)}, bf16[64,768]{1,0:T(8,128)(2,1)S(1)}, u32[]{:S(2)}, u32[]{:S(2)}) collective-permute-start(bf16[64,768]{1,0:T(8,128)(2,1)S(1)} %get-tuple-element.80), channel_id=1, source_target_pairs={{0,4},{4,0},{8,12},{12,8},{1,5},{5,1},{9,13},{13,9},{2,6},{6,2},{1... | collective-permute-start | bytes 294920 | tf_op jit(solution)/shard_map/ppermute | solution.py:674
  89.9 2.8 %collective-permute-start.21 = (bf16[64,768]{1,0:T(8,128)(2,1)S(1)}, bf16[64,768]{1,0:T(8,128)(2,1)S(1)}, u32[]{:S(2)}, u32[]{:S(2)}) collective-permute-start(bf16[64,768]{1,0:T(8,128)(2,1)S(1)} %get-tuple-element.82), channel_id=1, source_target_pairs={{0,12},{4,8},{8,4},{12,0},{1,13},{5,9},{9,5},{13,1},{2,14},{6,10},... | collective-permute-start | bytes 294920 | tf_op jit(solution)/shard_map/ppermute | solution.py:674
  92.7 3.4 %encode.1 = bf16[8,128,384]{2,1,0:T(8,128)(2,1)S(1)} custom-call(bf16[3,128,768]{2,1,0:T(8,128)(2,1)S(1)} %get-tuple-element.83.kernel_ref, bf16[10,256,512]{2,1,0:T(8,128)(2,1)S(1)} %get-tuple-element.84.hidden_ref), custom_call_target="tpu_custom_call" | custom-call | flops 2264924160 | bytes 2621440 | tf_op jit(solution)/shard_map/encode/pallas_call | solution.py:509
  96.1 4.0 %collective-permute-done.20 = bf16[64,768]{1,0:T(8,128)(2,1)S(1)} collective-permute-done((bf16[64,768]{1,0:T(8,128)(2,1)S(1)}, bf16[64,768]{1,0:T(8,128)(2,1)S(1)}, u32[]{:S(2)}, u32[]{:S(2)}) %collective-permute-start.20) | collective-permute-done | bytes 98336 | tf_op jit(solution)/shard_map/ppermute | solution.py:674
  101.7 2.1 %collective-permute-start.23 = (bf16[64,768]{1,0:T(8,128)(2,1)S(1)}, bf16[64,768]{1,0:T(8,128)(2,1)S(1)}, u32[]{:S(2)}, u32[]{:S(2)}) collective-permute-start(bf16[64,768]{1,0:T(8,128)(2,1)S(1)} %add_convert_fusion), channel_id=1, source_target_pairs={{0,8},{4,12},{8,0},{12,4},{1,9},{5,13},{9,1},{13,5},{2,10},{6,14},... | collective-permute-start | bytes 294920 | tf_op jit(solution)/shard_map/ppermute | solution.py:674
  104.6 3.0 %collective-permute-done.24 = bf16[64,768]{1,0:T(8,128)(2,1)S(1)} collective-permute-done((bf16[64,768]{1,0:T(8,128)(2,1)S(1)}, bf16[64,768]{1,0:T(8,128)(2,1)S(1)}, u32[]{:S(2)}, u32[]{:S(2)}) %collective-permute-start.24) | collective-permute-done | bytes 98336 | tf_op jit(solution)/shard_map/ppermute | solution.py:674
  107.6 4.4 %collective-permute-done.23 = bf16[64,768]{1,0:T(8,128)(2,1)S(1)} collective-permute-done((bf16[64,768]{1,0:T(8,128)(2,1)S(1)}, bf16[64,768]{1,0:T(8,128)(2,1)S(1)}, u32[]{:S(2)}, u32[]{:S(2)}) %collective-permute-start.23) | collective-permute-done | bytes 98336 | tf_op jit(solution)/shard_map/ppermute | solution.py:674
  113.9 1.8 %finish.1 = (f32[3,3,128,256]{3,2,1,0:T(8,128)}, f32[3,3,64,128]{3,2,1,0:T(8,128)}, f32[1,128]{1,0:T(1,128)}) custom-call(s32[5]{0:T(128)S(1)} %stack.43.index_ref, bf16[4,64,768]{2,1,0:T(8,128)(2,1)S(1)} %pad_maximum_fusion.mine_ref, bf16[4,64,768]{2,1,0:T(8,128)(2,1)S(1)} %collective-permute-done.25.other_ref), custom_call_target="tpu_custom_call" | custom-call | flops 196608 | bytes 2359296 | tf_op jit(solution)/shard_map/finish/pallas_call | solution.py:571
  (81 shorter events, 18.5 us)
Async XLA Ops:
  3.3 16.1 %collective-permute-start.2 = (bf16[3,3,200,128]{3,2,1,0:T(8,128)(2,1)S(1)}, bf16[3,3,200,128]{3,2,1,0:T(8,128)(2,1)S(1)}, u32[]{:S(2)}, u32[]{:S(2)}) collective-permute-start(bf16[3,3,200,128]{3,2,1,0:T(8,128)(2,1)S(1)} %offer.1), channel_id=1, source_target_pairs={{0,2},{2,0},{1,3},{3,1},{4,6},{6,4},{5,7},{7,5},{8,10},{10,8},{9,1... | collective-permute-start | bytes 1382408 | tf_op jit(solution)/shard_map/ppermute | solution.py:670
  6.3 13.0 %collective-permute-start = (bf16[128,384]{1,0:T(8,128)(2,1)S(1)}, bf16[128,384]{1,0:T(8,128)(2,1)S(1)}, u32[]{:S(2)}, u32[]{:S(2)}) collective-permute-start(bf16[128,384]{1,0:T(8,128)(2,1)S(1)} %get-tuple-element.53), channel_id=1, source_target_pairs={{0,4},{4,8},{8,12},{1,5},{5,9},{9,13},{2,6},{6,10},{10,14},{3,7},{... | collective-permute-start | bytes 294920 | tf_op jit(solution)/shard_map/ppermute | solution.py:716
  9.8 9.6 %collective-permute-start.1 = (bf16[128,384]{1,0:T(8,128)(2,1)S(1)}, bf16[128,384]{1,0:T(8,128)(2,1)S(1)}, u32[]{:S(2)}, u32[]{:S(2)}) collective-permute-start(bf16[128,384]{1,0:T(8,128)(2,1)S(1)} %get-tuple-element.54), channel_id=1, source_target_pairs={{4,0},{8,4},{12,8},{5,1},{9,5},{13,9},{6,2},{10,6},{14,10},{7,3},{... | collective-permute-start | bytes 294920 | tf_op jit(solution)/shard_map/ppermute | solution.py:717
  19.4 8.6 %collective-permute-start.7 = (bf16[1,72,1024]{2,1,0:T(8,128)(2,1)S(1)}, bf16[1,72,1024]{2,1,0:T(8,128)(2,1)S(1)}, u32[]{:S(2)}, u32[]{:S(2)}) collective-permute-start(bf16[1,72,1024]{2,1,0:T(8,128)(2,1)S(1)} %get-tuple-element.60), channel_id=1, source_target_pairs={{0,1},{1,0},{2,3},{3,2},{4,5},{5,4},{6,7},{7,6},{8,9},{9,8},{10,11... | collective-permute-start | bytes 442376 | tf_op jit(solution)/shard_map/ppermute | solution.py:666
  19.5 16.4 %collective-permute-start.15 = (bf16[2,128,384]{2,1,0:T(8,128)(2,1)S(1)}, bf16[2,128,384]{2,1,0:T(8,128)(2,1)S(1)}, u32[]{:S(2)}, u32[]{:S(2)}) collective-permute-start(bf16[2,128,384]{2,1,0:T(8,128)(2,1)S(1)} %pad_maximum_fusion.1.rest_1_), channel_id=1, source_target_pairs={{0,2},{2,0},{1,3},{3,1},{4,6},{6,4},{5,7},{7,5},{8,10},{10,8},{9,1... | collective-permute-start | bytes 589832 | tf_op jit(solution)/shard_map/ppermute | solution.py:670
  20.1 15.7 %collective-permute-start.3 = (bf16[2,72,1024]{2,1,0:T(8,128)(2,1)S(1)}, bf16[2,72,1024]{2,1,0:T(8,128)(2,1)S(1)}, u32[]{:S(2)}, u32[]{:S(2)}) collective-permute-start(bf16[2,72,1024]{2,1,0:T(8,128)(2,1)S(1)} %get-tuple-element.56), channel_id=1, source_target_pairs={{0,4},{4,0},{8,12},{12,8},{1,5},{5,1},{9,13},{13,9},{2,6},{6,2},{1... | collective-permute-start | bytes 884744 | tf_op jit(solution)/shard_map/ppermute | solution.py:674
  22.7 23.4 %collective-permute-start.5 = (bf16[2,72,1024]{2,1,0:T(8,128)(2,1)S(1)}, bf16[2,72,1024]{2,1,0:T(8,128)(2,1)S(1)}, u32[]{:S(2)}, u32[]{:S(2)}) collective-permute-start(bf16[2,72,1024]{2,1,0:T(8,128)(2,1)S(1)} %get-tuple-element.57), channel_id=1, source_target_pairs={{0,8},{4,12},{8,0},{12,4},{1,9},{5,13},{9,1},{13,5},{2,10},{6,14},... | collective-permute-start | bytes 884744 | tf_op jit(solution)/shard_map/ppermute | solution.py:674
  25.4 41.7 %collective-permute-start.14 = (bf16[128,8,384]{2,0,1:T(8,128)(2,1)S(1)}, bf16[128,8,384]{2,0,1:T(8,128)(2,1)S(1)}, u32[]{:S(2)}, u32[]{:S(2)}) collective-permute-start(bf16[128,8,384]{2,0,1:T(8,128)(2,1)S(1)} %copy.23), channel_id=1, source_target_pairs={{0,2},{2,0},{1,3},{3,1},{4,6},{6,4},{5,7},{7,5},{8,10},{10,8},{9,1... | collective-permute-start | bytes 2359304 | tf_op jit(solution)/shard_map/ppermute | solution.py:670
  28.0 18.3 %collective-permute-start.6 = (bf16[2,72,1024]{2,1,0:T(8,128)(2,1)S(1)}, bf16[2,72,1024]{2,1,0:T(8,128)(2,1)S(1)}, u32[]{:S(2)}, u32[]{:S(2)}) collective-permute-start(bf16[2,72,1024]{2,1,0:T(8,128)(2,1)S(1)} %get-tuple-element.58), channel_id=1, source_target_pairs={{0,12},{4,8},{8,4},{12,0},{1,13},{5,9},{9,5},{13,1},{2,14},{6,10},... | collective-permute-start | bytes 884744 | tf_op jit(solution)/shard_map/ppermute | solution.py:674
  35.8 11.0 %collective-permute-start.4 = (bf16[1,72,1024]{2,1,0:T(8,128)(2,1)S(1)}, bf16[1,72,1024]{2,1,0:T(8,128)(2,1)S(1)}, u32[]{:S(2)}, u32[]{:S(2)}) collective-permute-start(bf16[1,72,1024]{2,1,0:T(8,128)(2,1)S(1)} %slice.144), channel_id=1, source_target_pairs={{0,1},{1,0},{2,3},{3,2},{4,5},{5,4},{6,7},{7,6},{8,9},{9,8},{10,11... | collective-permute-start | bytes 442376 | tf_op jit(solution)/shard_map/ppermute | solution.py:666
  46.2 3.3 %collective-permute-start.8 = (bf16[1,72,1024]{2,1,0:T(8,128)(2,1)S(1)}, bf16[1,72,1024]{2,1,0:T(8,128)(2,1)S(1)}, u32[]{:S(2)}, u32[]{:S(2)}) collective-permute-start(bf16[1,72,1024]{2,1,0:T(8,128)(2,1)S(1)} %slice.145), channel_id=1, source_target_pairs={{0,1},{1,0},{2,3},{3,2},{4,5},{5,4},{6,7},{7,6},{8,9},{9,8},{10,11... | collective-permute-start | bytes 442376 | tf_op jit(solution)/shard_map/ppermute | solution.py:666
  46.3 3.2 %collective-permute-start.9 = (bf16[1,72,1024]{2,1,0:T(8,128)(2,1)S(1)}, bf16[1,72,1024]{2,1,0:T(8,128)(2,1)S(1)}, u32[]{:S(2)}, u32[]{:S(2)}) collective-permute-start(bf16[1,72,1024]{2,1,0:T(8,128)(2,1)S(1)} %slice.146), channel_id=1, source_target_pairs={{0,1},{1,0},{2,3},{3,2},{4,5},{5,4},{6,7},{7,6},{8,9},{9,8},{10,11... | collective-permute-start | bytes 442376 | tf_op jit(solution)/shard_map/ppermute | solution.py:666
  51.0 10.2 %collective-permute-start.10 = (bf16[2,72,384]{2,1,0:T(8,128)(2,1)S(1)}, bf16[2,72,384]{2,1,0:T(8,128)(2,1)S(1)}, u32[]{:S(2)}, u32[]{:S(2)}) collective-permute-start(bf16[2,72,384]{2,1,0:T(8,128)(2,1)S(1)} %bitcast.53), channel_id=1, source_target_pairs={{0,4},{4,8},{8,12},{1,5},{5,9},{9,13},{2,6},{6,10},{10,14},{3,7},{... | collective-permute-start | bytes 331784 | tf_op jit(solution)/shard_map/ppermute | solution.py:678
  58.2 13.1 %collective-permute-start.12 = (bf16[8,72,384]{2,1,0:T(8,128)(2,1)S(1)}, bf16[8,72,384]{2,1,0:T(8,128)(2,1)S(1)}, u32[]{:S(2)}, u32[]{:S(2)}) collective-permute-start(bf16[8,72,384]{2,1,0:T(8,128)(2,1)S(1)} %bitcast.35), channel_id=1, source_target_pairs={{0,2},{2,0},{1,3},{3,1},{4,6},{6,4},{5,7},{7,5},{8,10},{10,8},{9,1... | collective-permute-start | bytes 1327112 | tf_op jit(solution)/shard_map/ppermute | solution.py:670
  59.8 6.8 %collective-permute-start.11 = (bf16[2,72,384]{2,1,0:T(8,128)(2,1)S(1)}, bf16[2,72,384]{2,1,0:T(8,128)(2,1)S(1)}, u32[]{:S(2)}, u32[]{:S(2)}) collective-permute-start(bf16[2,72,384]{2,1,0:T(8,128)(2,1)S(1)} %bitcast.52), channel_id=1, source_target_pairs={{4,0},{8,4},{12,8},{5,1},{9,5},{13,9},{6,2},{10,6},{14,10},{7,3},{... | collective-permute-start | bytes 331784 | tf_op jit(solution)/shard_map/ppermute | solution.py:679
  66.6 8.7 %collective-permute-start.13 = (bf16[4,72,384]{2,1,0:T(8,128)(2,1)S(1)}, bf16[4,72,384]{2,1,0:T(8,128)(2,1)S(1)}, u32[]{:S(2)}, u32[]{:S(2)}) collective-permute-start(bf16[4,72,384]{2,1,0:T(8,128)(2,1)S(1)} %constant_dynamic-update-slice_fusion.edge_ref), channel_id=1, source_target_pairs={{0,2},{2,0},{1,3},{3,1},{4,6},{6,4},{5,7},{7,5},{8,10},{10,8},{9,1... | collective-permute-start | bytes 663560 | tf_op jit(solution)/shard_map/ppermute | solution.py:670
  67.3 4.1 %collective-permute-start.16 = (bf16[10,256,128]{2,1,0:T(8,128)(2,1)S(1)}, bf16[10,256,128]{2,1,0:T(8,128)(2,1)S(1)}, u32[]{:S(2)}, u32[]{:S(2)}) collective-permute-start(bf16[10,256,128]{2,1,0:T(8,128)(2,1)S(1)} %maximum_maximum_fusion), channel_id=1, source_target_pairs={{0,1},{1,0},{2,3},{3,2},{4,5},{5,4},{6,7},{7,6},{8,9},{9,8},{10,11... | collective-permute-start | bytes 1966088 | tf_op jit(solution)/shard_map/ppermute | solution.py:666
  75.4 1.9 %collective-permute-start.17 = (bf16[12,144,128]{2,1,0:T(8,128)(2,1)S(1)}, bf16[12,144,128]{2,1,0:T(8,128)(2,1)S(1)}, u32[]{:S(2)}, u32[]{:S(2)}) collective-permute-start(bf16[12,144,128]{2,1,0:T(8,128)(2,1)S(1)} %maximum_maximum_fusion.1), channel_id=1, source_target_pairs={{0,1},{1,0},{2,3},{3,2},{4,5},{5,4},{6,7},{7,6},{8,9},{9,8},{10,11... | collective-permute-start | bytes 1327112 | tf_op jit(solution)/shard_map/ppermute | solution.py:666
  88.3 7.8 %collective-permute-start.19 = (bf16[64,768]{1,0:T(8,128)(2,1)S(1)}, bf16[64,768]{1,0:T(8,128)(2,1)S(1)}, u32[]{:S(2)}, u32[]{:S(2)}) collective-permute-start(bf16[64,768]{1,0:T(8,128)(2,1)S(1)} %get-tuple-element.80), channel_id=1, source_target_pairs={{0,4},{4,0},{8,12},{12,8},{1,5},{5,1},{9,13},{13,9},{2,6},{6,2},{1... | collective-permute-start | bytes 294920 | tf_op jit(solution)/shard_map/ppermute | solution.py:674
  89.9 10.2 %collective-permute-start.20 = (bf16[64,768]{1,0:T(8,128)(2,1)S(1)}, bf16[64,768]{1,0:T(8,128)(2,1)S(1)}, u32[]{:S(2)}, u32[]{:S(2)}) collective-permute-start(bf16[64,768]{1,0:T(8,128)(2,1)S(1)} %get-tuple-element.81), channel_id=1, source_target_pairs={{0,8},{4,12},{8,0},{12,4},{1,9},{5,13},{9,1},{13,5},{2,10},{6,14},... | collective-permute-start | bytes 294920 | tf_op jit(solution)/shard_map/ppermute | solution.py:674
  89.9 10.2 %collective-permute-start.21 = (bf16[64,768]{1,0:T(8,128)(2,1)S(1)}, bf16[64,768]{1,0:T(8,128)(2,1)S(1)}, u32[]{:S(2)}, u32[]{:S(2)}) collective-permute-start(bf16[64,768]{1,0:T(8,128)(2,1)S(1)} %get-tuple-element.82), channel_id=1, source_target_pairs={{0,12},{4,8},{8,4},{12,0},{1,13},{5,9},{9,5},{13,1},{2,14},{6,10},... | collective-permute-start | bytes 294920 | tf_op jit(solution)/shard_map/ppermute | solution.py:674
  100.1 7.5 %collective-permute-start.24 = (bf16[64,768]{1,0:T(8,128)(2,1)S(1)}, bf16[64,768]{1,0:T(8,128)(2,1)S(1)}, u32[]{:S(2)}, u32[]{:S(2)}) collective-permute-start(bf16[64,768]{1,0:T(8,128)(2,1)S(1)} %add_convert_fusion), channel_id=1, source_target_pairs={{0,12},{4,8},{8,4},{12,0},{1,13},{5,9},{9,5},{13,1},{2,14},{6,10},... | collective-permute-start | bytes 294920 | tf_op jit(solution)/shard_map/ppermute | solution.py:674
  101.7 10.3 %collective-permute-start.23 = (bf16[64,768]{1,0:T(8,128)(2,1)S(1)}, bf16[64,768]{1,0:T(8,128)(2,1)S(1)}, u32[]{:S(2)}, u32[]{:S(2)}) collective-permute-start(bf16[64,768]{1,0:T(8,128)(2,1)S(1)} %add_convert_fusion), channel_id=1, source_target_pairs={{0,8},{4,12},{8,0},{12,4},{1,9},{5,13},{9,1},{13,5},{2,10},{6,14},... | collective-permute-start | bytes 294920 | tf_op jit(solution)/shard_map/ppermute | solution.py:674
  103.8 8.2 %collective-permute-start.22 = (bf16[64,768]{1,0:T(8,128)(2,1)S(1)}, bf16[64,768]{1,0:T(8,128)(2,1)S(1)}, u32[]{:S(2)}, u32[]{:S(2)}) collective-permute-start(bf16[64,768]{1,0:T(8,128)(2,1)S(1)} %add_convert_fusion), channel_id=1, source_target_pairs={{0,4},{4,0},{8,12},{12,8},{1,5},{5,1},{9,13},{13,9},{2,6},{6,2},{1... | collective-permute-start | bytes 294920 | tf_op jit(solution)/shard_map/ppermute | solution.py:674
  (10 other events, 65.5 us)

commit v5 on v4

--- a/solution.py
+++ b/solution.py
@@ -84,13 +84,11 @@
     ).astype(BF16)
     total_row = dot_nt(jnp.ones((8, LANES), BF16), onehot)
     offset_row = dot_nt(total_row.astype(BF16), earlier)
-    base_row = jnp.minimum(jnp.floor(offset_row * (1.0 / LANES)) * LANES, float(cap - BLOCK))
-    even = iota((8, pairs), 1) % 2 == 0
-    base_pair = jnp.where(even, base_row, pltpu.roll(base_row, 1, 1))
-    spill = jnp.where(offset_row + total_row > base_pair + BLOCK, 1.0, 0.0)
-    any_spill = jnp.max(spill, axis=1, keepdims=True)
+    odd = iota((8, pairs), 1) % 2 == 1
+    both = jnp.where(odd, total_row + pltpu.roll(total_row, 1, 1), 0.0)
+    spill = jnp.where(jnp.max(both, axis=1, keepdims=True) > LANES, 1.0, 0.0)
     info_ref[...] = jnp.where(
-        iota((8, pairs), 0) == 0, base_row, any_spill
+        iota((8, pairs), 0) == 0, offset_row, spill
     ).astype(jnp.int32)
     copy = pltpu.make_async_copy(info_ref, info_smem, sems.at[4])
     copy.start()
@@ -106,7 +104,8 @@
         load.wait()
     weight32_ref[...] = weight_ref[...].astype(F32)
     meta_row = iota((16, BLOCK), 0)
-    window = iota((BLOCK, BLOCK), 0, F32)
+    window = iota((LANES, BLOCK), 0, F32)
+    blank = jnp.zeros((n_obs_chans + 16, LANES), F32)
     copy.wait()
 
     def line(ref, b):
@@ -125,45 +124,37 @@
         ).astype(BF16)
         return jnp.concatenate([values, meta], axis=0)
 
-    def add(t, base, wide, key):
+    def add(t, wide, tile, slot, start):
+        key = jnp.where(tile == t, slot - start.astype(F32), -1.0)
         chosen = jnp.where(window == key, 1.0, 0.0).astype(BF16)
-        part = dot_nt(wide, chosen)[: n_obs_chans + META].astype(BF16)
+        part = jnp.concatenate([dot_nt(wide, chosen), blank], axis=1)
+        base = jnp.minimum(start // LANES * LANES, cap - BLOCK)
+        turn = jnp.bitwise_and(start - base, BLOCK - 1)
+        part = pltpu.roll(part, turn, 1)[: n_obs_chans + META].astype(BF16)
         where = pl.ds(pl.multiple_of(base, LANES), BLOCK)
         all_ref[t, :, where] = all_ref[t, :, where] + part
 
-    def first(b):
+    def place_block(b, skip):
         wide = columns(b)
         tile = line(tile_ref, b)
         slot = line(slot_ref, b)
         for t in range(n_tiles):
-            base = info_smem[0, t * n_lines + 2 * b]
-            key = jnp.where(tile == t, slot - base.astype(F32), -1.0)
-            add(t, base, wide, key)
+            add(t, wide, tile, slot, info_smem[0, t * n_lines + 2 * b] + skip)
 
     def first_two(i, carry):
-        first(2 * i)
-        first(2 * i + 1)
+        place_block(2 * i, 0)
+        place_block(2 * i + 1, 0)
         return carry
 
     lax.fori_loop(0, n_blocks // 2, first_two, 0)
 
-    if cap > BLOCK:
-
-        @pl.when(info_smem[1, 0] > 0)
-        def _():
-            def second(b, carry):
-                wide = columns(b)
-                tile = line(tile_ref, b)
-                slot = line(slot_ref, b)
-                for t in range(n_tiles):
-                    start = info_smem[0, t * n_lines + 2 * b]
-                    base = jnp.minimum(start + BLOCK, cap - BLOCK)
-                    far = (tile == t) & (slot >= (start + BLOCK).astype(F32))
-                    key = jnp.where(far, slot - base.astype(F32), -1.0)
-                    add(t, base, wide, key)
-                return carry
-
-            lax.fori_loop(0, n_blocks, second, 0)
+    @pl.when(info_smem[1, 0] > 0)
+    def _():
+        def rest_of(b, carry):
+            place_block(b, LANES)
+            return carry
+
+        lax.fori_loop(0, n_blocks, rest_of, 0)
 
     if relative:
         me = index_ref[4]
@@ -214,63 +205,66 @@
 def grid_kernel(n_rows, n_cols, group, takes, first, last, *rest):
     rest = list(rest)
     got_refs = [rest.pop(0) for _ in takes]
-    senders = [ref.at[i] for ref, n in zip(got_refs, takes) for i in range(n)]
+    senders = [ref.at[i] for ref, picked in zip(got_refs, takes) for i in picked]
     before_ref = None if first else rest.pop(0)
     own_ref = rest.pop(0)
-    send_ref = rest.pop(0) if last else None
+    send_refs = [rest.pop(0) for _ in range(3)] if last else None
     left_ref, right_ref = rest
     n_send = len(senders)
     rows, cap = senders[0].shape
     chans = rows - META
+    data = n_rows * chans
     per_row = n_cols // LANES
     columns = iota((n_cols, cap), 0, F32)
-    row_ids = iota((META, cap), 0)
+    row_ids = iota((2 * n_rows, cap), 0, F32)
     total = None
     for g in range(n_send // group):
         slot = g % 2
         for i in range(group):
-            s = g * group + i
+            sender = senders[g * group + i]
             at = slice(i * cap, (i + 1) * cap)
-            values = senders[s][0:chans, :]
-            meta = senders[s][chans:rows, :].astype(F32)
+            values = sender[0:chans, :]
+            meta = sender[chans:rows, :].astype(F32)
             weight = meta[0:1]
             high = meta[1:2]
             row = jnp.floor((high + 0.5) * (1.0 / per_row))
             column = (high - row * per_row) * LANES + meta[2:3]
             right_ref[slot, :, at] = jnp.where(columns == column, weight, 0.0).astype(BF16)
+            in_row = jnp.where(row_ids == row, 1.0, 0.0)
             for r in range(n_rows):
-                mask = jnp.where(row == r, 1.0, 0.0)
-                left_ref[slot, r * rows : r * rows + chans, at] = values * mask.astype(BF16)
-                left_ref[slot, r * rows + chans : (r + 1) * rows, at] = jnp.where(
-                    row_ids == 0, mask, 0.0
-                ).astype(BF16)
+                left_ref[slot, r * chans : (r + 1) * chans, at] = values * in_row[r : r + 1].astype(BF16)
+            left_ref[slot, data:, at] = in_row.astype(BF16)
         part = dot_nt(left_ref[slot], right_ref[slot])
         total = part if total is None else total + part
     if before_ref is not None:
         total = total + before_ref[...]
     own_ref[...] = total
     if last:
-        line = iota((META, n_cols), 0)
-        for r in range(n_rows):
-            send_ref[r * rows : r * rows + chans, :] = own_ref[r * rows : r * rows + chans, :].astype(BF16)
-            extra = own_ref[r * rows + chans : (r + 1) * rows, :]
-            density = extra[0:1]
-            high = density.astype(BF16).astype(F32)
-            send_ref[r * rows + chans : (r + 1) * rows, :] = jnp.where(
-                line == 0, high, jnp.where(line == 1, density - high, 0.0)
+        send_ref, low_ref, high_ref = send_refs
+        density = own_ref[data : data + n_rows, :]
+        high = density.astype(BF16).astype(F32)
+        low = density - high
+        send_ref[0:data, :] = own_ref[0:data, :].astype(BF16)
+        send_ref[data:, :] = jnp.concatenate([high, low], axis=0).astype(BF16)
+        for ref, at in ((high_ref, 0), (low_ref, n_rows - 2)):
+            ref[0 : 2 * chans, :] = own_ref[at * chans : (at + 2) * chans, :].astype(BF16)
+            ref[2 * chans :, :] = jnp.concatenate(
+                [high[at : at + 2], low[at : at + 2], jnp.zeros((4, n_cols), F32)], axis=0
             ).astype(BF16)
 
 
 def grid(got, before, last, n_rows, n_cols):
-    takes = [n for _, n in got]
+    takes = [picked for _, picked in got]
     got = [x for x, _ in got]
-    n_send = sum(takes)
+    n_send = sum(len(picked) for picked in takes)
     rows, cap = got[0].shape[1:]
     group = max(1, min(2048 // cap, n_send))
-    total = n_rows * rows
+    chans = rows - META
+    total = n_rows * chans + 2 * n_rows
     outs = [jax.ShapeDtypeStruct((total, n_cols), F32)]
     if last:
         outs.append(jax.ShapeDtypeStruct((total, n_cols), BF16))
+        outs += [jax.ShapeDtypeStruct((2 * chans + 8, n_cols), BF16)] * 2
     ins = list(got) if before is None else list(got) + [before]
     return call(
         functools.partial(grid_kernel, n_rows, n_cols, group, takes, before is None, last),
@@ -347,32 +341,54 @@
     taps_ref, logs_ref, wide_ref, out_left_ref, pre_left_ref, acc_ref = rest
     n_rows, own, n_cols = cot_ref.shape
     n_hidden = kernel_ref.shape[1]
-    rows = chans + META
     taps_rows = 3 * chans
     width = n_cols + LANES
     tile, chan, sub, n_tile = index_ref[0], index_ref[1], index_ref[2], index_ref[3]
     keep_two = lane_mask((1, width), n_cols, sub, 2)
 
     log_line = iota((16, width), 0)
+    data = n_rows * chans
+    middle_rows = data + 2 * n_rows
+    edge_rows = 2 * chans + 8
+    side_half = middle_rows + 2 * edge_rows
+    lefts = [(own_ref, edge_ref)] + ([] if peer_ref is None else [(peer_ref, peer_edge_ref)])
+    sources = []
     for i in range(n_rows + 4):
-        if 2 <= i < n_rows + 2:
-            mid = own_ref[i - 2]
-            if peer_ref is not None:
-                mid = mid + peer_ref[i - 2].astype(F32)
-        else:
-            e = i if i < 2 else i - n_rows
-            mid = edge_ref[e].astype(F32)
-            if peer_ref is not None:
-                mid = mid + peer_edge_ref[e].astype(F32)
-        side = side_ref[i, 0:rows].astype(F32)
-        if peer_ref is not None:
-            side = side + side_ref[i, rows : 2 * rows].astype(F32)
-        ext = jnp.concatenate([mid, side], axis=1)
-        density = ext[chans : chans + 1] + ext[chans + 1 : chans + 2]
+        found = []
+        for p, (middle_ref, ends_ref) in enumerate(lefts):
+            if 2 <= i < n_rows + 2:
+                r = i - 2
+                base, lines = r * chans, (data + r, data + n_rows + r)
+                found.append((middle_ref, base, lines, p * side_half))
+            else:
+                e = i if i < 2 else i - n_rows
+                start = e // 2 * edge_rows
+                base = start + e % 2 * chans
+                lines = (start + 2 * chans + e % 2, start + 2 * chans + 2 + e % 2)
+                found.append((ends_ref, base, lines, p * side_half + middle_rows))
+        sources.append(found)
+
+    def gather(found, wanted):
+        total = None
+        for ref, base, lines, at in found:
+            for line in [base] if wanted == chans else lines:
+                ext = jnp.concatenate(
+                    [
+                        ref[line : line + wanted, :].astype(F32),
+                        side_ref[at + line : at + line + wanted, :].astype(F32),
+                    ],
+                    axis=1,
+                )
+                total = ext if total is None else total + ext
+        return total
+
+    for i in range(n_rows + 4):
+        ext = gather(sources[i], chans)
+        density = gather(sources[i], 1)
         logs = jnp.log(1.0 + density)
         logs_ref[i] = logs
         shrink = jnp.where(keep_two, 1.0 / (1.0 + density), 0.0)
-        feats = ext[0:chans] * shrink
+        feats = ext * shrink
         at = slice(i * width, (i + 1) * width)
         taps_ref[0:chans, at] = pltpu.roll(feats, 1, 1).astype(BF16)
         taps_ref[chans : 2 * chans, at] = feats.astype(BF16)
@@ -674,12 +690,6 @@
     return lax.ppermute(x, "tile", [(i, i ^ k) for i in range(n_tile)])
 
 
-def edges(block, depth, n_tile):
-    low = lax.ppermute(block[-depth:], "tile", step_perm(n_tile, 1))
-    high = lax.ppermute(block[:depth], "tile", step_perm(n_tile, -1))
-    return low, high
-
-
 def near(block, sub):
     n_cols = block.shape[-1]
     return jnp.where(sub == 0, block[..., n_cols - LANES :], block[..., :LANES])
@@ -721,16 +731,16 @@
     if pair:
         sent, low, high, theirs = lax.optimization_barrier((sent, low, high, theirs))
     if few:
+        far = [swap_tile(sent[k + 1], n_tile, k) for k in (1, 2, 3)]
         beside = swap_sub(sent[1])
-        far = [swap_tile(sent[k + 1], n_tile, k) for k in (1, 2, 3)]
         steps = [
-            [(sent[0], 1), (beside, 1)],
-            [(far[0], 1), (swap_sub(far[0][1:]), 1), (far[1], 1), (far[2], 1)],
-            [(swap_sub(far[1][1:]), 1), (swap_sub(far[2][1:]), 1)],
+            [(sent[0], (0,)), (beside, (0,))],
+            [(far[0], (0,)), (swap_sub(far[0][1:]), (0,)), (far[1], (0,)), (far[2], (0,))],
+            [(swap_sub(far[1][1:]), (0,)), (swap_sub(far[2][1:]), (0,))],
         ]
     else:
         got = lax.all_to_all(sent[0], ("tile", "sub"), split_axis=0, concat_axis=0, tiled=True)
-        steps = [[(got, n_tiles)]]
+        steps = [[(got, tuple(range(n_tiles)))]]
 
     if pair:
         cotangent, _ = lax.optimization_barrier((cotangent, sent[0]))
@@ -768,26 +778,33 @@
         part, back_weights, one_weights, code_weights, gain = lax.optimization_barrier(
             (part, back_weights, one_weights, code_weights, gain)
         )
-    part, message = grid(steps[-1], part, True, n_rows, n_cols)
-    shape = (n_rows, chans + META, n_cols)
-    part = part.reshape(shape)
-    message = message.reshape(shape)
+    part, message, up, down = grid(steps[-1], part, True, n_rows, n_cols)
+    data = n_rows * chans
     if not pair:
         part = lax.psum(part, "chan")
-        density = part[:, chans]
+        density = part[data : data + n_rows]
         dense = density.astype(BF16)
         rest = (density - dense.astype(F32)).astype(BF16)
-        message = part.astype(BF16).at[:, chans].set(dense).at[:, chans + 1].set(rest)
-    low, high = edges(message, 2, n_tile)
+        message = jnp.concatenate([part[:data].astype(BF16), dense, rest], axis=0)
+        blank = jnp.zeros((4, n_cols), BF16)
+        up, down = [
+            jnp.concatenate(
+                [message[r * chans : (r + 2) * chans], dense[r : r + 2], rest[r : r + 2], blank], axis=0
+            )
+            for r in (n_rows - 2, 0)
+        ]
+    low = lax.ppermute(up, "tile", step_perm(n_tile, 1))
+    high = lax.ppermute(down, "tile", step_perm(n_tile, -1))
     edge = jnp.concatenate([low, high], axis=0)
     back_out = back(index, back_weights, pieces, cot_side, n_cols)
     if pair:
         peer, peer_edge = swap_chan(message), swap_chan(edge)
-        peer_edge, back_out = lax.optimization_barrier((peer_edge, back_out))
-        side = side_rows([(message, edge), (peer, peer_edge)], sub)
+        peer, peer_edge, back_out = lax.optimization_barrier((peer, peer_edge, back_out))
+        side = [message, edge, peer, peer_edge]
     else:
         peer, peer_edge = None, None
-        side = side_rows([(message, edge)], sub)
+        side = [message, edge]
+    side = swap_sub(jnp.concatenate([near(x, sub) for x in side], axis=0))
 
     scale = 1.0 / math.sqrt(n_tiles * n_rows * n_cols)
     split = pair and n_tile == 4

time: 116 us -> 113 us (0.974)
  Pallas kernels: 33.3 us -> 31.2 us
    pallas_call x1, Pallas kernels: 8.2 us -> 6.5 us  [route(): call(functools.partial(route_kernel, n_tiles, cap, relative), [jax.ShapeD...]
  transfers between devices with their start and end apart: 26 -> 26, of which waited for: 11 -> 10; matrix products, arithmetic and copies ran while one was open for 1% -> 1% of each run, Pallas kernels for 19% -> 17%
where the time goes in v5:
time: 113 us
  waiting for transfers between devices  40.6 us (36%)
  starting transfers between devices  36.3 us (32%)
  Pallas kernels  31.2 us (28%)
  local copies, waits for them, and re-layouts  3.48 us (3%)
    ppermute x9, waiting for transfers between devices, swap_tile(): return lax.ppermute(x, 'tile', [(i, i ^ k) for i in range(n_tile)])  28.1 us
    ppermute x9, starting transfers between devices, swap_tile(): return lax.ppermute(x, 'tile', [(i, i ^ k) for i in range(n_tile)])  13.8 us
    pallas_call x1, Pallas kernels, grads(): call(body, outs, [smem_spec()] + [vmem_spec()] * (2 + len(ins)), [pltpu.V...  8.62 us
    ppermute x5, starting transfers between devices, swap_chan(): return lax.ppermute(x, 'chan', [(0, 1), (1, 0)])  7.71 us
    ppermute x1, starting transfers between devices, body(): low = lax.ppermute(up, 'tile', step_perm(n_tile, 1))  7.18 us
    pallas_call x1, Pallas kernels, route(): call(functools.partial(route_kernel, n_tiles, cap, relative), [jax.ShapeD...  6.5 us
    ppermute x1, waiting for transfers between devices, body(): high = lax.ppermute(down, 'tile', step_perm(n_tile, -1))  5.23 us
    pallas_call x3, Pallas kernels, grid(): call(functools.partial(grid_kernel, n_rows, n_cols, group, takes, before...  5.07 us
  transfers between devices with their start and end apart: 26, of which 10 were waited for; matrix products, arithmetic and copies ran while one was open for 1% of the time, Pallas kernels for 17%

profile of v5, /device:TPU:0, one launch (start us, length us, event | category | flops | bytes accessed | tf_op | source)
XLA Modules:
  0.0 113.0 jit_solution(7211795904393287002)
XLA Ops:
  0.7 1.8 %fusion.1 = (bf16[128,1,384]{2,1,0:T(2,128)(2,1)S(1)}, bf16[128,1,384]{2,1,0:T(2,128)(2,1)S(1)}) fusion(bf16[128,8,384]{2,1,0:T(8,128)(2,1)} %param.15), kind=kLoop, calls=%fused_computation.21 | loop fusion | bytes 393216 | tf_op jit(solution)/shard_map/slice | solution.py:720
  3.3 3.0 %collective-permute-start.2 = (bf16[3,3,200,128]{3,2,1,0:T(8,128)(2,1)S(1)}, bf16[3,3,200,128]{3,2,1,0:T(8,128)(2,1)S(1)}, u32[]{:S(2)}, u32[]{:S(2)}) collective-permute-start(bf16[3,3,200,128]{3,2,1,0:T(8,128)(2,1)S(1)} %offer.1), channel_id=1, source_target_pairs={{0,2},{2,0},{1,3},{3,1},{4,6},{6,4},{5,7},{7,5},{8,10},{10,8},{9,1... | collective-permute-start | bytes 1382408 | tf_op jit(solution)/shard_map/ppermute | solution.py:686
  6.3 3.5 %collective-permute-start = (bf16[128,384]{1,0:T(8,128)(2,1)S(1)}, bf16[128,384]{1,0:T(8,128)(2,1)S(1)}, u32[]{:S(2)}, u32[]{:S(2)}) collective-permute-start(bf16[128,384]{1,0:T(8,128)(2,1)S(1)} %get-tuple-element.56), channel_id=1, source_target_pairs={{0,4},{4,8},{8,12},{1,5},{5,9},{9,13},{2,6},{6,10},{10,14},{3,7},{... | collective-permute-start | bytes 294920 | tf_op jit(solution)/shard_map/ppermute | solution.py:726
  11.1 6.5 %route.1 = (bf16[1,72,1024]{2,1,0:T(8,128)(2,1)S(1)}, bf16[1,72,1024]{2,1,0:T(8,128)(2,1)S(1)}, bf16[2,72,1024]{2,1,0:T(8,128)(2,1)S(1)}, bf16[2,72,1024]{2,1,0:T(8,128)(2,1)S(1)}, bf16[2,72,1024]{2,1,0:T(8,128)(2,1)S(1)}) custom-call(s32[5]{0:T(128)S(1)} %stack.43.index_ref, s32[32,128]{1,0:T(8,128)S(1)} %bitcast.37, bf16[32,128]{1,0:T(8,128)(2,1)S(1)} %bitcast.39, ...), custom_call_target="tpu_custom_call" | custom-call | flops 1342177280 | bytes 1179648 | tf_op jit(solution)/shard_map/route/pallas_call | solution.py:176
  18.8 2.3 %collective-permute-start.3 = (bf16[2,72,1024]{2,1,0:T(8,128)(2,1)S(1)}, bf16[2,72,1024]{2,1,0:T(8,128)(2,1)S(1)}, u32[]{:S(2)}, u32[]{:S(2)}) collective-permute-start(bf16[2,72,1024]{2,1,0:T(8,128)(2,1)S(1)} %get-tuple-element.59), channel_id=1, source_target_pairs={{0,4},{4,0},{8,12},{12,8},{1,5},{5,1},{9,13},{13,9},{2,6},{6,2},{1... | collective-permute-start | bytes 884744 | tf_op jit(solution)/shard_map/ppermute | solution.py:690
  21.0 2.6 %collective-permute-start.5 = (bf16[2,72,1024]{2,1,0:T(8,128)(2,1)S(1)}, bf16[2,72,1024]{2,1,0:T(8,128)(2,1)S(1)}, u32[]{:S(2)}, u32[]{:S(2)}) collective-permute-start(bf16[2,72,1024]{2,1,0:T(8,128)(2,1)S(1)} %get-tuple-element.60), channel_id=1, source_target_pairs={{0,8},{4,12},{8,0},{12,4},{1,9},{5,13},{9,1},{13,5},{2,10},{6,14},... | collective-permute-start | bytes 884744 | tf_op jit(solution)/shard_map/ppermute | solution.py:690
  27.7 6.4 %collective-permute-done.3.rest_0_ = bf16[2,72,1024]{2,1,0:T(8,128)(2,1)S(1)} collective-permute-done((bf16[2,72,1024]{2,1,0:T(8,128)(2,1)S(1)}, bf16[2,72,1024]{2,1,0:T(8,128)(2,1)S(1)}, u32[]{:S(2)}, u32[]{:S(2)}) %collective-permute-start.3) | collective-permute-done | bytes 294944 | tf_op jit(solution)/shard_map/ppermute | solution.py:690
  34.2 10.2 %collective-permute-done.5.rest_2_ = bf16[2,72,1024]{2,1,0:T(8,128)(2,1)S(1)} collective-permute-done((bf16[2,72,1024]{2,1,0:T(8,128)(2,1)S(1)}, bf16[2,72,1024]{2,1,0:T(8,128)(2,1)S(1)}, u32[]{:S(2)}, u32[]{:S(2)}) %collective-permute-start.5) | collective-permute-done | bytes 294944 | tf_op jit(solution)/shard_map/ppermute | solution.py:690
  45.1 2.5 %grid_part.3.rest_2_ = f32[528,384]{1,0:T(8,128)S(1)} custom-call(bf16[2,72,1024]{2,1,0:T(8,128)(2,1)S(1)} %collective-permute-done.3.rest_0_, bf16[1,72,1024]{2,1,0:T(8,128)(2,1)S(1)} %collective-permute-done.4.rest_1_, bf16[2,72,1024]{2,1,0:T(8,128)(2,1)S(1)} %collective-permute-done.5.rest_2_, bf16[2,72,1024]{2,1,0:T(8,128)(2,1)S(1)} %collective-permute-done.6.rest_3_, ...), custom_call_target="tpu_custom_call" | custom-call | flops 1660944384 | bytes 589824 | tf_op jit(solution)/shard_map/grid_part/pallas_call | solution.py:269
  49.0 7.2 %collective-permute-start.10 = (bf16[136,384]{1,0:T(8,128)(2,1)S(1)}, bf16[136,384]{1,0:T(8,128)(2,1)S(1)}, u32[]{:S(2)}, u32[]{:S(2)}) collective-permute-start(bf16[136,384]{1,0:T(8,128)(2,1)S(1)} %get-tuple-element.73), channel_id=1, source_target_pairs={{0,4},{4,8},{8,12},{1,5},{5,9},{9,13},{2,6},{6,10},{10,14},{3,7},{... | collective-permute-start | bytes 313352 | tf_op jit(solution)/shard_map/ppermute | solution.py:796
  59.6 5.2 %collective-permute-done.11 = bf16[136,384]{1,0:T(8,128)(2,1)S(1)} collective-permute-done((bf16[136,384]{1,0:T(8,128)(2,1)S(1)}, bf16[136,384]{1,0:T(8,128)(2,1)S(1)}, u32[]{:S(2)}, u32[]{:S(2)}) %collective-permute-start.11) | collective-permute-done | bytes 104480 | tf_op jit(solution)/shard_map/ppermute | solution.py:797
  65.5 3.7 %back.1.back_ref = f32[128,3072]{1,0:T(8,128)S(1)} custom-call(s32[5]{0:T(128)S(1)} %stack.43.index_ref, bf16[3,128,768]{2,1,0:T(8,128)(2,1)S(1)} %get-tuple-element.76.kernel_ref, bf16[8,128,384]{2,1,0:T(8,128)(2,1)S(1)} %bitcast.27, bf16[2,128,384]{2,1,0:T(8,128)(2,1)S(1)} %pad_maximum_fusion.2.rest_1_, bf16[8,128,384]{2,1,0:T(8,128)(2,1)S(1)} %bitcast.33, ...), custom_call_target="tpu_custom_call" | custom-call | flops 2264924160 | bytes 1966080 | tf_op jit(solution)/shard_map/back/pallas_call | solution.py:321
  69.2 3.5 %collective-permute-done.13.peer_edge_ref = bf16[272,384]{1,0:T(8,128)(2,1)S(1)} collective-permute-done((bf16[272,384]{1,0:T(8,128)(2,1)S(1)}, bf16[272,384]{1,0:T(8,128)(2,1)S(1)}, u32[]{:S(2)}, u32[]{:S(2)}) %collective-permute-start.13) | collective-permute-done | bytes 208928 | tf_op jit(solution)/shard_map/ppermute | solution.py:686
  72.8 1.7 %collective-permute-done.17.side_ref = bf16[1600,128]{1,0:T(8,128)(2,1)S(1)} collective-permute-done((bf16[1600,128]{1,0:T(8,128)(2,1)S(1)}, bf16[1600,128]{1,0:T(8,128)(2,1)S(1)}, u32[]{:S(2)}, u32[]{:S(2)}) %collective-permute-start.17) | collective-permute-done | bytes 409632 | tf_op jit(solution)/shard_map/ppermute | solution.py:682
  74.6 8.6 %grads.1 = (bf16[10,256,512]{2,1,0:T(8,128)(2,1)S(1)}, f32[256,768]{1,0:T(8,128)S(1)}, bf16[256,768]{1,0:T(8,128)(2,1)S(1)}) custom-call(s32[5]{0:T(128)S(1)} %stack.43.index_ref, bf16[3,256,192]{2,1,0:T(8,128)(2,1)S(1)} %get-tuple-element.69.kernel_ref, f32[256,128]{1,0:T(8,128)S(1)} %get-tuple-element.70.gain_ref, ...), custom_call_target="tpu_custom_call" | custom-call | flops 3397386240 | bytes 5898240 | tf_op jit(solution)/shard_map/grads/pallas_call | solution.py:485
  83.4 1.6 %collective-permute-done.18.got_ref = bf16[256,768]{1,0:T(8,128)(2,1)S(1)} collective-permute-done((bf16[256,768]{1,0:T(8,128)(2,1)S(1)}, bf16[256,768]{1,0:T(8,128)(2,1)S(1)}, u32[]{:S(2)}, u32[]{:S(2)}) %collective-permute-start.18) | collective-permute-done | bytes 393248 | tf_op jit(solution)/shard_map/ppermute | solution.py:682
  85.6 1.6 %collective-permute-start.19 = (bf16[64,768]{1,0:T(8,128)(2,1)S(1)}, bf16[64,768]{1,0:T(8,128)(2,1)S(1)}, u32[]{:S(2)}, u32[]{:S(2)}) collective-permute-start(bf16[64,768]{1,0:T(8,128)(2,1)S(1)} %get-tuple-element.86), channel_id=1, source_target_pairs={{0,4},{4,0},{8,12},{12,8},{1,5},{5,1},{9,13},{13,9},{2,6},{6,2},{1... | collective-permute-start | bytes 294920 | tf_op jit(solution)/shard_map/ppermute | solution.py:690
  87.3 2.8 %collective-permute-start.21 = (bf16[64,768]{1,0:T(8,128)(2,1)S(1)}, bf16[64,768]{1,0:T(8,128)(2,1)S(1)}, u32[]{:S(2)}, u32[]{:S(2)}) collective-permute-start(bf16[64,768]{1,0:T(8,128)(2,1)S(1)} %get-tuple-element.88), channel_id=1, source_target_pairs={{0,12},{4,8},{8,4},{12,0},{1,13},{5,9},{9,5},{13,1},{2,14},{6,10},... | collective-permute-start | bytes 294920 | tf_op jit(solution)/shard_map/ppermute | solution.py:690
  90.1 3.3 %encode.1 = bf16[8,128,384]{2,1,0:T(8,128)(2,1)S(1)} custom-call(bf16[3,128,768]{2,1,0:T(8,128)(2,1)S(1)} %get-tuple-element.89.kernel_ref, bf16[10,256,512]{2,1,0:T(8,128)(2,1)S(1)} %get-tuple-element.90.hidden_ref), custom_call_target="tpu_custom_call" | custom-call | flops 2264924160 | bytes 2621440 | tf_op jit(solution)/shard_map/encode/pallas_call | solution.py:525
  93.4 4.0 %collective-permute-done.20 = bf16[64,768]{1,0:T(8,128)(2,1)S(1)} collective-permute-done((bf16[64,768]{1,0:T(8,128)(2,1)S(1)}, bf16[64,768]{1,0:T(8,128)(2,1)S(1)}, u32[]{:S(2)}, u32[]{:S(2)}) %collective-permute-start.20) | collective-permute-done | bytes 98336 | tf_op jit(solution)/shard_map/ppermute | solution.py:690
  98.6 2.5 %collective-permute-start.23 = (bf16[64,768]{1,0:T(8,128)(2,1)S(1)}, bf16[64,768]{1,0:T(8,128)(2,1)S(1)}, u32[]{:S(2)}, u32[]{:S(2)}) collective-permute-start(bf16[64,768]{1,0:T(8,128)(2,1)S(1)} %add_convert_fusion), channel_id=1, source_target_pairs={{0,8},{4,12},{8,0},{12,4},{1,9},{5,13},{9,1},{13,5},{2,10},{6,14},... | collective-permute-start | bytes 294920 | tf_op jit(solution)/shard_map/ppermute | solution.py:690
  101.9 3.0 %collective-permute-done.24 = bf16[64,768]{1,0:T(8,128)(2,1)S(1)} collective-permute-done((bf16[64,768]{1,0:T(8,128)(2,1)S(1)}, bf16[64,768]{1,0:T(8,128)(2,1)S(1)}, u32[]{:S(2)}, u32[]{:S(2)}) %collective-permute-start.24) | collective-permute-done | bytes 98336 | tf_op jit(solution)/shard_map/ppermute | solution.py:690
  104.9 4.4 %collective-permute-done.23 = bf16[64,768]{1,0:T(8,128)(2,1)S(1)} collective-permute-done((bf16[64,768]{1,0:T(8,128)(2,1)S(1)}, bf16[64,768]{1,0:T(8,128)(2,1)S(1)}, u32[]{:S(2)}, u32[]{:S(2)}) %collective-permute-start.23) | collective-permute-done | bytes 98336 | tf_op jit(solution)/shard_map/ppermute | solution.py:690
  111.2 1.8 %finish.1 = (f32[3,3,128,256]{3,2,1,0:T(8,128)}, f32[3,3,64,128]{3,2,1,0:T(8,128)}, f32[1,128]{1,0:T(1,128)}) custom-call(s32[5]{0:T(128)S(1)} %stack.43.index_ref, bf16[4,64,768]{2,1,0:T(8,128)(2,1)S(1)} %pad_maximum_fusion.1.mine_ref, bf16[4,64,768]{2,1,0:T(8,128)(2,1)S(1)} %collective-permute-done.25.other_ref), custom_call_target="tpu_custom_call" | custom-call | flops 196608 | bytes 2359296 | tf_op jit(solution)/shard_map/finish/pallas_call | solution.py:587
  (79 shorter events, 18.0 us)
Async XLA Ops:
  3.3 14.4 %collective-permute-start.2 = (bf16[3,3,200,128]{3,2,1,0:T(8,128)(2,1)S(1)}, bf16[3,3,200,128]{3,2,1,0:T(8,128)(2,1)S(1)}, u32[]{:S(2)}, u32[]{:S(2)}) collective-permute-start(bf16[3,3,200,128]{3,2,1,0:T(8,128)(2,1)S(1)} %offer.1), channel_id=1, source_target_pairs={{0,2},{2,0},{1,3},{3,1},{4,6},{6,4},{5,7},{7,5},{8,10},{10,8},{9,1... | collective-permute-start | bytes 1382408 | tf_op jit(solution)/shard_map/ppermute | solution.py:686
  6.3 11.3 %collective-permute-start = (bf16[128,384]{1,0:T(8,128)(2,1)S(1)}, bf16[128,384]{1,0:T(8,128)(2,1)S(1)}, u32[]{:S(2)}, u32[]{:S(2)}) collective-permute-start(bf16[128,384]{1,0:T(8,128)(2,1)S(1)} %get-tuple-element.56), channel_id=1, source_target_pairs={{0,4},{4,8},{8,12},{1,5},{5,9},{9,13},{2,6},{6,10},{10,14},{3,7},{... | collective-permute-start | bytes 294920 | tf_op jit(solution)/shard_map/ppermute | solution.py:726
  9.8 7.9 %collective-permute-start.1 = (bf16[128,384]{1,0:T(8,128)(2,1)S(1)}, bf16[128,384]{1,0:T(8,128)(2,1)S(1)}, u32[]{:S(2)}, u32[]{:S(2)}) collective-permute-start(bf16[128,384]{1,0:T(8,128)(2,1)S(1)} %get-tuple-element.57), channel_id=1, source_target_pairs={{4,0},{8,4},{12,8},{5,1},{9,5},{13,9},{6,2},{10,6},{14,10},{7,3},{... | collective-permute-start | bytes 294920 | tf_op jit(solution)/shard_map/ppermute | solution.py:727
  17.7 8.6 %collective-permute-start.7 = (bf16[1,72,1024]{2,1,0:T(8,128)(2,1)S(1)}, bf16[1,72,1024]{2,1,0:T(8,128)(2,1)S(1)}, u32[]{:S(2)}, u32[]{:S(2)}) collective-permute-start(bf16[1,72,1024]{2,1,0:T(8,128)(2,1)S(1)} %get-tuple-element.63), channel_id=1, source_target_pairs={{0,1},{1,0},{2,3},{3,2},{4,5},{5,4},{6,7},{7,6},{8,9},{9,8},{10,11... | collective-permute-start | bytes 442376 | tf_op jit(solution)/shard_map/ppermute | solution.py:682
  17.8 16.4 %collective-permute-start.15 = (bf16[2,128,384]{2,1,0:T(8,128)(2,1)S(1)}, bf16[2,128,384]{2,1,0:T(8,128)(2,1)S(1)}, u32[]{:S(2)}, u32[]{:S(2)}) collective-permute-start(bf16[2,128,384]{2,1,0:T(8,128)(2,1)S(1)} %pad_maximum_fusion.2.rest_1_), channel_id=1, source_target_pairs={{0,2},{2,0},{1,3},{3,1},{4,6},{6,4},{5,7},{7,5},{8,10},{10,8},{9,1... | collective-permute-start | bytes 589832 | tf_op jit(solution)/shard_map/ppermute | solution.py:686
  18.8 15.3 %collective-permute-start.3 = (bf16[2,72,1024]{2,1,0:T(8,128)(2,1)S(1)}, bf16[2,72,1024]{2,1,0:T(8,128)(2,1)S(1)}, u32[]{:S(2)}, u32[]{:S(2)}) collective-permute-start(bf16[2,72,1024]{2,1,0:T(8,128)(2,1)S(1)} %get-tuple-element.59), channel_id=1, source_target_pairs={{0,4},{4,0},{8,12},{12,8},{1,5},{5,1},{9,13},{13,9},{2,6},{6,2},{1... | collective-permute-start | bytes 884744 | tf_op jit(solution)/shard_map/ppermute | solution.py:690
  21.0 23.4 %collective-permute-start.5 = (bf16[2,72,1024]{2,1,0:T(8,128)(2,1)S(1)}, bf16[2,72,1024]{2,1,0:T(8,128)(2,1)S(1)}, u32[]{:S(2)}, u32[]{:S(2)}) collective-permute-start(bf16[2,72,1024]{2,1,0:T(8,128)(2,1)S(1)} %get-tuple-element.60), channel_id=1, source_target_pairs={{0,8},{4,12},{8,0},{12,4},{1,9},{5,13},{9,1},{13,5},{2,10},{6,14},... | collective-permute-start | bytes 884744 | tf_op jit(solution)/shard_map/ppermute | solution.py:690
  23.7 32.4 %collective-permute-start.14 = (bf16[128,8,384]{2,0,1:T(8,128)(2,1)S(1)}, bf16[128,8,384]{2,0,1:T(8,128)(2,1)S(1)}, u32[]{:S(2)}, u32[]{:S(2)}) collective-permute-start(bf16[128,8,384]{2,0,1:T(8,128)(2,1)S(1)} %copy.23), channel_id=1, source_target_pairs={{0,2},{2,0},{1,3},{3,1},{4,6},{6,4},{5,7},{7,5},{8,10},{10,8},{9,1... | collective-permute-start | bytes 2359304 | tf_op jit(solution)/shard_map/ppermute | solution.py:686
  26.3 18.3 %collective-permute-start.6 = (bf16[2,72,1024]{2,1,0:T(8,128)(2,1)S(1)}, bf16[2,72,1024]{2,1,0:T(8,128)(2,1)S(1)}, u32[]{:S(2)}, u32[]{:S(2)}) collective-permute-start(bf16[2,72,1024]{2,1,0:T(8,128)(2,1)S(1)} %get-tuple-element.61), channel_id=1, source_target_pairs={{0,12},{4,8},{8,4},{12,0},{1,13},{5,9},{9,5},{13,1},{2,14},{6,10},... | collective-permute-start | bytes 884744 | tf_op jit(solution)/shard_map/ppermute | solution.py:690
  34.1 11.0 %collective-permute-start.4 = (bf16[1,72,1024]{2,1,0:T(8,128)(2,1)S(1)}, bf16[1,72,1024]{2,1,0:T(8,128)(2,1)S(1)}, u32[]{:S(2)}, u32[]{:S(2)}) collective-permute-start(bf16[1,72,1024]{2,1,0:T(8,128)(2,1)S(1)} %slice.106), channel_id=1, source_target_pairs={{0,1},{1,0},{2,3},{3,2},{4,5},{5,4},{6,7},{7,6},{8,9},{9,8},{10,11... | collective-permute-start | bytes 442376 | tf_op jit(solution)/shard_map/ppermute | solution.py:682
  44.5 3.1 %collective-permute-start.8 = (bf16[1,72,1024]{2,1,0:T(8,128)(2,1)S(1)}, bf16[1,72,1024]{2,1,0:T(8,128)(2,1)S(1)}, u32[]{:S(2)}, u32[]{:S(2)}) collective-permute-start(bf16[1,72,1024]{2,1,0:T(8,128)(2,1)S(1)} %slice.107), channel_id=1, source_target_pairs={{0,1},{1,0},{2,3},{3,2},{4,5},{5,4},{6,7},{7,6},{8,9},{9,8},{10,11... | collective-permute-start | bytes 442376 | tf_op jit(solution)/shard_map/ppermute | solution.py:682
  44.6 3.0 %collective-permute-start.9 = (bf16[1,72,1024]{2,1,0:T(8,128)(2,1)S(1)}, bf16[1,72,1024]{2,1,0:T(8,128)(2,1)S(1)}, u32[]{:S(2)}, u32[]{:S(2)}) collective-permute-start(bf16[1,72,1024]{2,1,0:T(8,128)(2,1)S(1)} %slice.108), channel_id=1, source_target_pairs={{0,1},{1,0},{2,3},{3,2},{4,5},{5,4},{6,7},{7,6},{8,9},{9,8},{10,11... | collective-permute-start | bytes 442376 | tf_op jit(solution)/shard_map/ppermute | solution.py:682
  49.0 10.6 %collective-permute-start.10 = (bf16[136,384]{1,0:T(8,128)(2,1)S(1)}, bf16[136,384]{1,0:T(8,128)(2,1)S(1)}, u32[]{:S(2)}, u32[]{:S(2)}) collective-permute-start(bf16[136,384]{1,0:T(8,128)(2,1)S(1)} %get-tuple-element.73), channel_id=1, source_target_pairs={{0,4},{4,8},{8,12},{1,5},{5,9},{9,13},{2,6},{6,10},{10,14},{3,7},{... | collective-permute-start | bytes 313352 | tf_op jit(solution)/shard_map/ppermute | solution.py:796
  56.2 9.2 %collective-permute-start.16 = (bf16[10,256,128]{2,1,0:T(8,128)(2,1)S(1)}, bf16[10,256,128]{2,1,0:T(8,128)(2,1)S(1)}, u32[]{:S(2)}, u32[]{:S(2)}) collective-permute-start(bf16[10,256,128]{2,1,0:T(8,128)(2,1)S(1)} %maximum_maximum_fusion), channel_id=1, source_target_pairs={{0,1},{1,0},{2,3},{3,2},{4,5},{5,4},{6,7},{7,6},{8,9},{9,8},{10,11... | collective-permute-start | bytes 1966088 | tf_op jit(solution)/shard_map/ppermute | solution.py:682
  56.5 16.1 %collective-permute-start.12 = (bf16[528,384]{1,0:T(8,128)(2,1)S(1)}, bf16[528,384]{1,0:T(8,128)(2,1)S(1)}, u32[]{:S(2)}, u32[]{:S(2)}) collective-permute-start(bf16[528,384]{1,0:T(8,128)(2,1)S(1)} %get-tuple-element.75), channel_id=1, source_target_pairs={{0,2},{2,0},{1,3},{3,1},{4,6},{6,4},{5,7},{7,5},{8,10},{10,8},{9,1... | collective-permute-start | bytes 1216520 | tf_op jit(solution)/shard_map/ppermute | solution.py:686
  58.1 6.7 %collective-permute-start.11 = (bf16[136,384]{1,0:T(8,128)(2,1)S(1)}, bf16[136,384]{1,0:T(8,128)(2,1)S(1)}, u32[]{:S(2)}, u32[]{:S(2)}) collective-permute-start(bf16[136,384]{1,0:T(8,128)(2,1)S(1)} %get-tuple-element.74), channel_id=1, source_target_pairs={{4,0},{8,4},{12,8},{5,1},{9,5},{13,9},{6,2},{10,6},{14,10},{7,3},{... | collective-permute-start | bytes 313352 | tf_op jit(solution)/shard_map/ppermute | solution.py:797
  64.9 7.8 %collective-permute-start.13 = (bf16[272,384]{1,0:T(8,128)(2,1)S(1)}, bf16[272,384]{1,0:T(8,128)(2,1)S(1)}, u32[]{:S(2)}, u32[]{:S(2)}) collective-permute-start(bf16[272,384]{1,0:T(8,128)(2,1)S(1)} %constant_dynamic-update-slice_fusion.edge_ref), channel_id=1, source_target_pairs={{0,2},{2,0},{1,3},{3,1},{4,6},{6,4},{5,7},{7,5},{8,10},{10,8},{9,1... | collective-permute-start | bytes 626696 | tf_op jit(solution)/shard_map/ppermute | solution.py:686
  72.8 1.8 %collective-permute-start.17 = (bf16[1600,128]{1,0:T(8,128)(2,1)S(1)}, bf16[1600,128]{1,0:T(8,128)(2,1)S(1)}, u32[]{:S(2)}, u32[]{:S(2)}) collective-permute-start(bf16[1600,128]{1,0:T(8,128)(2,1)S(1)} %pad_maximum_fusion), channel_id=1, source_target_pairs={{0,1},{1,0},{2,3},{3,2},{4,5},{5,4},{6,7},{7,6},{8,9},{9,8},{10,11... | collective-permute-start | bytes 1228808 | tf_op jit(solution)/shard_map/ppermute | solution.py:682
  85.6 7.8 %collective-permute-start.19 = (bf16[64,768]{1,0:T(8,128)(2,1)S(1)}, bf16[64,768]{1,0:T(8,128)(2,1)S(1)}, u32[]{:S(2)}, u32[]{:S(2)}) collective-permute-start(bf16[64,768]{1,0:T(8,128)(2,1)S(1)} %get-tuple-element.86), channel_id=1, source_target_pairs={{0,4},{4,0},{8,12},{12,8},{1,5},{5,1},{9,13},{13,9},{2,6},{6,2},{1... | collective-permute-start | bytes 294920 | tf_op jit(solution)/shard_map/ppermute | solution.py:690
  87.3 10.1 %collective-permute-start.20 = (bf16[64,768]{1,0:T(8,128)(2,1)S(1)}, bf16[64,768]{1,0:T(8,128)(2,1)S(1)}, u32[]{:S(2)}, u32[]{:S(2)}) collective-permute-start(bf16[64,768]{1,0:T(8,128)(2,1)S(1)} %get-tuple-element.87), channel_id=1, source_target_pairs={{0,8},{4,12},{8,0},{12,4},{1,9},{5,13},{9,1},{13,5},{2,10},{6,14},... | collective-permute-start | bytes 294920 | tf_op jit(solution)/shard_map/ppermute | solution.py:690
  87.3 10.1 %collective-permute-start.21 = (bf16[64,768]{1,0:T(8,128)(2,1)S(1)}, bf16[64,768]{1,0:T(8,128)(2,1)S(1)}, u32[]{:S(2)}, u32[]{:S(2)}) collective-permute-start(bf16[64,768]{1,0:T(8,128)(2,1)S(1)} %get-tuple-element.88), channel_id=1, source_target_pairs={{0,12},{4,8},{8,4},{12,0},{1,13},{5,9},{9,5},{13,1},{2,14},{6,10},... | collective-permute-start | bytes 294920 | tf_op jit(solution)/shard_map/ppermute | solution.py:690
  97.5 7.5 %collective-permute-start.24 = (bf16[64,768]{1,0:T(8,128)(2,1)S(1)}, bf16[64,768]{1,0:T(8,128)(2,1)S(1)}, u32[]{:S(2)}, u32[]{:S(2)}) collective-permute-start(bf16[64,768]{1,0:T(8,128)(2,1)S(1)} %add_convert_fusion), channel_id=1, source_target_pairs={{0,12},{4,8},{8,4},{12,0},{1,13},{5,9},{9,5},{13,1},{2,14},{6,10},... | collective-permute-start | bytes 294920 | tf_op jit(solution)/shard_map/ppermute | solution.py:690
  98.6 10.8 %collective-permute-start.23 = (bf16[64,768]{1,0:T(8,128)(2,1)S(1)}, bf16[64,768]{1,0:T(8,128)(2,1)S(1)}, u32[]{:S(2)}, u32[]{:S(2)}) collective-permute-start(bf16[64,768]{1,0:T(8,128)(2,1)S(1)} %add_convert_fusion), channel_id=1, source_target_pairs={{0,8},{4,12},{8,0},{12,4},{1,9},{5,13},{9,1},{13,5},{2,10},{6,14},... | collective-permute-start | bytes 294920 | tf_op jit(solution)/shard_map/ppermute | solution.py:690
  101.1 8.3 %collective-permute-start.22 = (bf16[64,768]{1,0:T(8,128)(2,1)S(1)}, bf16[64,768]{1,0:T(8,128)(2,1)S(1)}, u32[]{:S(2)}, u32[]{:S(2)}) collective-permute-start(bf16[64,768]{1,0:T(8,128)(2,1)S(1)} %add_convert_fusion), channel_id=1, source_target_pairs={{0,4},{4,0},{8,12},{12,8},{1,5},{5,1},{9,13},{13,9},{2,6},{6,2},{1... | collective-permute-start | bytes 294920 | tf_op jit(solution)/shard_map/ppermute | solution.py:690
  (10 other events, 63.8 us)

commit v6 on v5

--- a/solution.py
+++ b/solution.py
@@ -141,12 +141,12 @@
         for t in range(n_tiles):
             add(t, wide, tile, slot, info_smem[0, t * n_lines + 2 * b] + skip)
 
-    def first_two(i, carry):
-        place_block(2 * i, 0)
-        place_block(2 * i + 1, 0)
+    def first_some(i, carry):
+        for j in range(8):
+            place_block(8 * i + j, 0)
         return carry
 
-    lax.fori_loop(0, n_blocks // 2, first_two, 0)
+    lax.fori_loop(0, n_blocks // 8, first_some, 0)
 
     @pl.when(info_smem[1, 0] > 0)
     def _():
@@ -413,7 +413,7 @@
 
     gain = gain_ref[:, 0:1]
     keep_one = lane_mask((1, width), n_cols, sub, 1)
-    group = 2
+    group = 1
     for first in range(0, n_rows + 2, group):
         pre_all = None
         for a in range(3):

time: 113 us -> 112 us (level)
  Pallas kernels: 31.2 us -> 29.5 us
    pallas_call x1, Pallas kernels: 6.5 us -> 5.21 us  [route(): call(functools.partial(route_kernel, n_tiles, cap, relative), [jax.ShapeD...]
  transfers between devices with their start and end apart: 26 -> 26, of which waited for: 10 -> 11; matrix products, arithmetic and copies ran while one was open for 1% -> 1% of each run, Pallas kernels for 17% -> 16%
where the time goes in v6:
time: 112 us
  waiting for transfers between devices  41.7 us (37%)
  starting transfers between devices  35.8 us (32%)
  Pallas kernels  29.5 us (26%)
  local copies, waits for them, and re-layouts  3.48 us (3%)
    ppermute x9, waiting for transfers between devices, swap_tile(): return lax.ppermute(x, 'tile', [(i, i ^ k) for i in range(n_tile)])  28.7 us
    ppermute x9, starting transfers between devices, swap_tile(): return lax.ppermute(x, 'tile', [(i, i ^ k) for i in range(n_tile)])  13.1 us
    pallas_call x1, Pallas kernels, grads(): call(body, outs, [smem_spec()] + [vmem_spec()] * (2 + len(ins)), [pltpu.V...  8.22 us
    ppermute x5, starting transfers between devices, swap_chan(): return lax.ppermute(x, 'chan', [(0, 1), (1, 0)])  7.92 us
    ppermute x1, starting transfers between devices, body(): low = lax.ppermute(up, 'tile', step_perm(n_tile, 1))  7.17 us
    ppermute x1, waiting for transfers between devices, body(): high = lax.ppermute(down, 'tile', step_perm(n_tile, -1))  5.24 us
    pallas_call x1, Pallas kernels, route(): call(functools.partial(route_kernel, n_tiles, cap, relative), [jax.ShapeD...  5.21 us
    pallas_call x3, Pallas kernels, grid(): call(functools.partial(grid_kernel, n_rows, n_cols, group, takes, before...  5.08 us
  transfers between devices with their start and end apart: 26, of which 11 were waited for; matrix products, arithmetic and copies ran while one was open for 1% of the time, Pallas kernels for 16%

profile of v6, /device:TPU:0, one launch (start us, length us, event | category | flops | bytes accessed | tf_op | source)
XLA Modules:
  0.0 111.9 jit_solution(4683583767822045563)
XLA Ops:
  0.7 1.8 %fusion.1 = (bf16[128,1,384]{2,1,0:T(2,128)(2,1)S(1)}, bf16[128,1,384]{2,1,0:T(2,128)(2,1)S(1)}) fusion(bf16[128,8,384]{2,1,0:T(8,128)(2,1)} %param.15), kind=kLoop, calls=%fused_computation.21 | loop fusion | bytes 393216 | tf_op jit(solution)/shard_map/slice | solution.py:720
  3.3 3.0 %collective-permute-start.2 = (bf16[3,3,200,128]{3,2,1,0:T(8,128)(2,1)S(1)}, bf16[3,3,200,128]{3,2,1,0:T(8,128)(2,1)S(1)}, u32[]{:S(2)}, u32[]{:S(2)}) collective-permute-start(bf16[3,3,200,128]{3,2,1,0:T(8,128)(2,1)S(1)} %offer.1), channel_id=1, source_target_pairs={{0,2},{2,0},{1,3},{3,1},{4,6},{6,4},{5,7},{7,5},{8,10},{10,8},{9,1... | collective-permute-start | bytes 1382408 | tf_op jit(solution)/shard_map/ppermute | solution.py:686
  6.3 3.5 %collective-permute-start = (bf16[128,384]{1,0:T(8,128)(2,1)S(1)}, bf16[128,384]{1,0:T(8,128)(2,1)S(1)}, u32[]{:S(2)}, u32[]{:S(2)}) collective-permute-start(bf16[128,384]{1,0:T(8,128)(2,1)S(1)} %get-tuple-element.56), channel_id=1, source_target_pairs={{0,4},{4,8},{8,12},{1,5},{5,9},{9,13},{2,6},{6,10},{10,14},{3,7},{... | collective-permute-start | bytes 294920 | tf_op jit(solution)/shard_map/ppermute | solution.py:726
  11.1 5.2 %route.1 = (bf16[1,72,1024]{2,1,0:T(8,128)(2,1)S(1)}, bf16[1,72,1024]{2,1,0:T(8,128)(2,1)S(1)}, bf16[2,72,1024]{2,1,0:T(8,128)(2,1)S(1)}, bf16[2,72,1024]{2,1,0:T(8,128)(2,1)S(1)}, bf16[2,72,1024]{2,1,0:T(8,128)(2,1)S(1)}) custom-call(s32[5]{0:T(128)S(1)} %stack.43.index_ref, s32[32,128]{1,0:T(8,128)S(1)} %bitcast.37, bf16[32,128]{1,0:T(8,128)(2,1)S(1)} %bitcast.39, ...), custom_call_target="tpu_custom_call" | custom-call | flops 1342177280 | bytes 1179648 | tf_op jit(solution)/shard_map/route/pallas_call | solution.py:176
  17.0 1.8 %collective-permute-start.15 = (bf16[2,128,384]{2,1,0:T(8,128)(2,1)S(1)}, bf16[2,128,384]{2,1,0:T(8,128)(2,1)S(1)}, u32[]{:S(2)}, u32[]{:S(2)}) collective-permute-start(bf16[2,128,384]{2,1,0:T(8,128)(2,1)S(1)} %pad_maximum_fusion.2.rest_1_), channel_id=1, source_target_pairs={{0,2},{2,0},{1,3},{3,1},{4,6},{6,4},{5,7},{7,5},{8,10},{10,8},{9,1... | collective-permute-start | bytes 589832 | tf_op jit(solution)/shard_map/ppermute | solution.py:686
  20.4 2.6 %collective-permute-start.5 = (bf16[2,72,1024]{2,1,0:T(8,128)(2,1)S(1)}, bf16[2,72,1024]{2,1,0:T(8,128)(2,1)S(1)}, u32[]{:S(2)}, u32[]{:S(2)}) collective-permute-start(bf16[2,72,1024]{2,1,0:T(8,128)(2,1)S(1)} %get-tuple-element.60), channel_id=1, source_target_pairs={{0,8},{4,12},{8,0},{12,4},{1,9},{5,13},{9,1},{13,5},{2,10},{6,14},... | collective-permute-start | bytes 884744 | tf_op jit(solution)/shard_map/ppermute | solution.py:690
  26.4 7.2 %collective-permute-done.3.rest_0_ = bf16[2,72,1024]{2,1,0:T(8,128)(2,1)S(1)} collective-permute-done((bf16[2,72,1024]{2,1,0:T(8,128)(2,1)S(1)}, bf16[2,72,1024]{2,1,0:T(8,128)(2,1)S(1)}, u32[]{:S(2)}, u32[]{:S(2)}) %collective-permute-start.3) | collective-permute-done | bytes 294944 | tf_op jit(solution)/shard_map/ppermute | solution.py:690
  33.7 10.1 %collective-permute-done.5.rest_2_ = bf16[2,72,1024]{2,1,0:T(8,128)(2,1)S(1)} collective-permute-done((bf16[2,72,1024]{2,1,0:T(8,128)(2,1)S(1)}, bf16[2,72,1024]{2,1,0:T(8,128)(2,1)S(1)}, u32[]{:S(2)}, u32[]{:S(2)}) %collective-permute-start.5) | collective-permute-done | bytes 294944 | tf_op jit(solution)/shard_map/ppermute | solution.py:690
  44.5 2.5 %grid_part.3.rest_2_ = f32[528,384]{1,0:T(8,128)S(1)} custom-call(bf16[2,72,1024]{2,1,0:T(8,128)(2,1)S(1)} %collective-permute-done.3.rest_0_, bf16[1,72,1024]{2,1,0:T(8,128)(2,1)S(1)} %collective-permute-done.4.rest_1_, bf16[2,72,1024]{2,1,0:T(8,128)(2,1)S(1)} %collective-permute-done.5.rest_2_, bf16[2,72,1024]{2,1,0:T(8,128)(2,1)S(1)} %collective-permute-done.6.rest_3_, ...), custom_call_target="tpu_custom_call" | custom-call | flops 1660944384 | bytes 589824 | tf_op jit(solution)/shard_map/grid_part/pallas_call | solution.py:269
  48.3 7.2 %collective-permute-start.10 = (bf16[136,384]{1,0:T(8,128)(2,1)S(1)}, bf16[136,384]{1,0:T(8,128)(2,1)S(1)}, u32[]{:S(2)}, u32[]{:S(2)}) collective-permute-start(bf16[136,384]{1,0:T(8,128)(2,1)S(1)} %get-tuple-element.73), channel_id=1, source_target_pairs={{0,4},{4,8},{8,12},{1,5},{5,9},{9,13},{2,6},{6,10},{10,14},{3,7},{... | collective-permute-start | bytes 313352 | tf_op jit(solution)/shard_map/ppermute | solution.py:796
  58.3 5.2 %collective-permute-done.11 = bf16[136,384]{1,0:T(8,128)(2,1)S(1)} collective-permute-done((bf16[136,384]{1,0:T(8,128)(2,1)S(1)}, bf16[136,384]{1,0:T(8,128)(2,1)S(1)}, u32[]{:S(2)}, u32[]{:S(2)}) %collective-permute-start.11) | collective-permute-done | bytes 104480 | tf_op jit(solution)/shard_map/ppermute | solution.py:797
  64.8 3.7 %back.1.back_ref = f32[128,3072]{1,0:T(8,128)S(1)} custom-call(s32[5]{0:T(128)S(1)} %stack.43.index_ref, bf16[3,128,768]{2,1,0:T(8,128)(2,1)S(1)} %get-tuple-element.76.kernel_ref, bf16[8,128,384]{2,1,0:T(8,128)(2,1)S(1)} %bitcast.27, bf16[2,128,384]{2,1,0:T(8,128)(2,1)S(1)} %pad_maximum_fusion.2.rest_1_, bf16[8,128,384]{2,1,0:T(8,128)(2,1)S(1)} %bitcast.33, ...), custom_call_target="tpu_custom_call" | custom-call | flops 2264924160 | bytes 1966080 | tf_op jit(solution)/shard_map/back/pallas_call | solution.py:321
  68.5 3.5 %collective-permute-done.13.peer_edge_ref = bf16[272,384]{1,0:T(8,128)(2,1)S(1)} collective-permute-done((bf16[272,384]{1,0:T(8,128)(2,1)S(1)}, bf16[272,384]{1,0:T(8,128)(2,1)S(1)}, u32[]{:S(2)}, u32[]{:S(2)}) %collective-permute-start.13) | collective-permute-done | bytes 208928 | tf_op jit(solution)/shard_map/ppermute | solution.py:686
  72.1 1.7 %collective-permute-done.17.side_ref = bf16[1600,128]{1,0:T(8,128)(2,1)S(1)} collective-permute-done((bf16[1600,128]{1,0:T(8,128)(2,1)S(1)}, bf16[1600,128]{1,0:T(8,128)(2,1)S(1)}, u32[]{:S(2)}, u32[]{:S(2)}) %collective-permute-start.17) | collective-permute-done | bytes 409632 | tf_op jit(solution)/shard_map/ppermute | solution.py:682
  73.9 8.2 %grads.1 = (bf16[10,256,512]{2,1,0:T(8,128)(2,1)S(1)}, f32[256,768]{1,0:T(8,128)S(1)}, bf16[256,768]{1,0:T(8,128)(2,1)S(1)}) custom-call(s32[5]{0:T(128)S(1)} %stack.43.index_ref, bf16[3,256,192]{2,1,0:T(8,128)(2,1)S(1)} %get-tuple-element.69.kernel_ref, f32[256,128]{1,0:T(8,128)S(1)} %get-tuple-element.70.gain_ref, ...), custom_call_target="tpu_custom_call" | custom-call | flops 3397386240 | bytes 5898240 | tf_op jit(solution)/shard_map/grads/pallas_call | solution.py:485
  82.3 1.6 %collective-permute-done.18.got_ref = bf16[256,768]{1,0:T(8,128)(2,1)S(1)} collective-permute-done((bf16[256,768]{1,0:T(8,128)(2,1)S(1)}, bf16[256,768]{1,0:T(8,128)(2,1)S(1)}, u32[]{:S(2)}, u32[]{:S(2)}) %collective-permute-start.18) | collective-permute-done | bytes 393248 | tf_op jit(solution)/shard_map/ppermute | solution.py:682
  84.5 1.6 %collective-permute-start.19 = (bf16[64,768]{1,0:T(8,128)(2,1)S(1)}, bf16[64,768]{1,0:T(8,128)(2,1)S(1)}, u32[]{:S(2)}, u32[]{:S(2)}) collective-permute-start(bf16[64,768]{1,0:T(8,128)(2,1)S(1)} %get-tuple-element.86), channel_id=1, source_target_pairs={{0,4},{4,0},{8,12},{12,8},{1,5},{5,1},{9,13},{13,9},{2,6},{6,2},{1... | collective-permute-start | bytes 294920 | tf_op jit(solution)/shard_map/ppermute | solution.py:690
  86.2 2.8 %collective-permute-start.21 = (bf16[64,768]{1,0:T(8,128)(2,1)S(1)}, bf16[64,768]{1,0:T(8,128)(2,1)S(1)}, u32[]{:S(2)}, u32[]{:S(2)}) collective-permute-start(bf16[64,768]{1,0:T(8,128)(2,1)S(1)} %get-tuple-element.88), channel_id=1, source_target_pairs={{0,12},{4,8},{8,4},{12,0},{1,13},{5,9},{9,5},{13,1},{2,14},{6,10},... | collective-permute-start | bytes 294920 | tf_op jit(solution)/shard_map/ppermute | solution.py:690
  89.0 3.3 %encode.1 = bf16[8,128,384]{2,1,0:T(8,128)(2,1)S(1)} custom-call(bf16[3,128,768]{2,1,0:T(8,128)(2,1)S(1)} %get-tuple-element.89.kernel_ref, bf16[10,256,512]{2,1,0:T(8,128)(2,1)S(1)} %get-tuple-element.90.hidden_ref), custom_call_target="tpu_custom_call" | custom-call | flops 2264924160 | bytes 2621440 | tf_op jit(solution)/shard_map/encode/pallas_call | solution.py:525
  92.3 4.0 %collective-permute-done.20 = bf16[64,768]{1,0:T(8,128)(2,1)S(1)} collective-permute-done((bf16[64,768]{1,0:T(8,128)(2,1)S(1)}, bf16[64,768]{1,0:T(8,128)(2,1)S(1)}, u32[]{:S(2)}, u32[]{:S(2)}) %collective-permute-start.20) | collective-permute-done | bytes 98336 | tf_op jit(solution)/shard_map/ppermute | solution.py:690
  97.5 2.5 %collective-permute-start.23 = (bf16[64,768]{1,0:T(8,128)(2,1)S(1)}, bf16[64,768]{1,0:T(8,128)(2,1)S(1)}, u32[]{:S(2)}, u32[]{:S(2)}) collective-permute-start(bf16[64,768]{1,0:T(8,128)(2,1)S(1)} %add_convert_fusion), channel_id=1, source_target_pairs={{0,8},{4,12},{8,0},{12,4},{1,9},{5,13},{9,1},{13,5},{2,10},{6,14},... | collective-permute-start | bytes 294920 | tf_op jit(solution)/shard_map/ppermute | solution.py:690
  100.8 3.0 %collective-permute-done.24 = bf16[64,768]{1,0:T(8,128)(2,1)S(1)} collective-permute-done((bf16[64,768]{1,0:T(8,128)(2,1)S(1)}, bf16[64,768]{1,0:T(8,128)(2,1)S(1)}, u32[]{:S(2)}, u32[]{:S(2)}) %collective-permute-start.24) | collective-permute-done | bytes 98336 | tf_op jit(solution)/shard_map/ppermute | solution.py:690
  103.9 4.4 %collective-permute-done.23 = bf16[64,768]{1,0:T(8,128)(2,1)S(1)} collective-permute-done((bf16[64,768]{1,0:T(8,128)(2,1)S(1)}, bf16[64,768]{1,0:T(8,128)(2,1)S(1)}, u32[]{:S(2)}, u32[]{:S(2)}) %collective-permute-start.23) | collective-permute-done | bytes 98336 | tf_op jit(solution)/shard_map/ppermute | solution.py:690
  110.1 1.8 %finish.1 = (f32[3,3,128,256]{3,2,1,0:T(8,128)}, f32[3,3,64,128]{3,2,1,0:T(8,128)}, f32[1,128]{1,0:T(1,128)}) custom-call(s32[5]{0:T(128)S(1)} %stack.43.index_ref, bf16[4,64,768]{2,1,0:T(8,128)(2,1)S(1)} %pad_maximum_fusion.1.mine_ref, bf16[4,64,768]{2,1,0:T(8,128)(2,1)S(1)} %collective-permute-done.25.other_ref), custom_call_target="tpu_custom_call" | custom-call | flops 196608 | bytes 2359296 | tf_op jit(solution)/shard_map/finish/pallas_call | solution.py:587
  (79 shorter events, 18.5 us)
Async XLA Ops:
  3.3 13.6 %collective-permute-start.2 = (bf16[3,3,200,128]{3,2,1,0:T(8,128)(2,1)S(1)}, bf16[3,3,200,128]{3,2,1,0:T(8,128)(2,1)S(1)}, u32[]{:S(2)}, u32[]{:S(2)}) collective-permute-start(bf16[3,3,200,128]{3,2,1,0:T(8,128)(2,1)S(1)} %offer.1), channel_id=1, source_target_pairs={{0,2},{2,0},{1,3},{3,1},{4,6},{6,4},{5,7},{7,5},{8,10},{10,8},{9,1... | collective-permute-start | bytes 1382408 | tf_op jit(solution)/shard_map/ppermute | solution.py:686
  6.3 10.1 %collective-permute-start = (bf16[128,384]{1,0:T(8,128)(2,1)S(1)}, bf16[128,384]{1,0:T(8,128)(2,1)S(1)}, u32[]{:S(2)}, u32[]{:S(2)}) collective-permute-start(bf16[128,384]{1,0:T(8,128)(2,1)S(1)} %get-tuple-element.56), channel_id=1, source_target_pairs={{0,4},{4,8},{8,12},{1,5},{5,9},{9,13},{2,6},{6,10},{10,14},{3,7},{... | collective-permute-start | bytes 294920 | tf_op jit(solution)/shard_map/ppermute | solution.py:726
  9.8 6.6 %collective-permute-start.1 = (bf16[128,384]{1,0:T(8,128)(2,1)S(1)}, bf16[128,384]{1,0:T(8,128)(2,1)S(1)}, u32[]{:S(2)}, u32[]{:S(2)}) collective-permute-start(bf16[128,384]{1,0:T(8,128)(2,1)S(1)} %get-tuple-element.57), channel_id=1, source_target_pairs={{4,0},{8,4},{12,8},{5,1},{9,5},{13,9},{6,2},{10,6},{14,10},{7,3},{... | collective-permute-start | bytes 294920 | tf_op jit(solution)/shard_map/ppermute | solution.py:727
  16.9 8.1 %collective-permute-start.7 = (bf16[1,72,1024]{2,1,0:T(8,128)(2,1)S(1)}, bf16[1,72,1024]{2,1,0:T(8,128)(2,1)S(1)}, u32[]{:S(2)}, u32[]{:S(2)}) collective-permute-start(bf16[1,72,1024]{2,1,0:T(8,128)(2,1)S(1)} %get-tuple-element.63), channel_id=1, source_target_pairs={{0,1},{1,0},{2,3},{3,2},{4,5},{5,4},{6,7},{7,6},{8,9},{9,8},{10,11... | collective-permute-start | bytes 442376 | tf_op jit(solution)/shard_map/ppermute | solution.py:682
  17.0 16.7 %collective-permute-start.15 = (bf16[2,128,384]{2,1,0:T(8,128)(2,1)S(1)}, bf16[2,128,384]{2,1,0:T(8,128)(2,1)S(1)}, u32[]{:S(2)}, u32[]{:S(2)}) collective-permute-start(bf16[2,128,384]{2,1,0:T(8,128)(2,1)S(1)} %pad_maximum_fusion.2.rest_1_), channel_id=1, source_target_pairs={{0,2},{2,0},{1,3},{3,1},{4,6},{6,4},{5,7},{7,5},{8,10},{10,8},{9,1... | collective-permute-start | bytes 589832 | tf_op jit(solution)/shard_map/ppermute | solution.py:686
  18.8 14.8 %collective-permute-start.3 = (bf16[2,72,1024]{2,1,0:T(8,128)(2,1)S(1)}, bf16[2,72,1024]{2,1,0:T(8,128)(2,1)S(1)}, u32[]{:S(2)}, u32[]{:S(2)}) collective-permute-start(bf16[2,72,1024]{2,1,0:T(8,128)(2,1)S(1)} %get-tuple-element.59), channel_id=1, source_target_pairs={{0,4},{4,0},{8,12},{12,8},{1,5},{5,1},{9,13},{13,9},{2,6},{6,2},{1... | collective-permute-start | bytes 884744 | tf_op jit(solution)/shard_map/ppermute | solution.py:690
  20.4 23.4 %collective-permute-start.5 = (bf16[2,72,1024]{2,1,0:T(8,128)(2,1)S(1)}, bf16[2,72,1024]{2,1,0:T(8,128)(2,1)S(1)}, u32[]{:S(2)}, u32[]{:S(2)}) collective-permute-start(bf16[2,72,1024]{2,1,0:T(8,128)(2,1)S(1)} %get-tuple-element.60), channel_id=1, source_target_pairs={{0,8},{4,12},{8,0},{12,4},{1,9},{5,13},{9,1},{13,5},{2,10},{6,14},... | collective-permute-start | bytes 884744 | tf_op jit(solution)/shard_map/ppermute | solution.py:690
  23.1 32.4 %collective-permute-start.14 = (bf16[128,8,384]{2,0,1:T(8,128)(2,1)S(1)}, bf16[128,8,384]{2,0,1:T(8,128)(2,1)S(1)}, u32[]{:S(2)}, u32[]{:S(2)}) collective-permute-start(bf16[128,8,384]{2,0,1:T(8,128)(2,1)S(1)} %copy.23), channel_id=1, source_target_pairs={{0,2},{2,0},{1,3},{3,1},{4,6},{6,4},{5,7},{7,5},{8,10},{10,8},{9,1... | collective-permute-start | bytes 2359304 | tf_op jit(solution)/shard_map/ppermute | solution.py:686
  25.0 18.9 %collective-permute-start.6 = (bf16[2,72,1024]{2,1,0:T(8,128)(2,1)S(1)}, bf16[2,72,1024]{2,1,0:T(8,128)(2,1)S(1)}, u32[]{:S(2)}, u32[]{:S(2)}) collective-permute-start(bf16[2,72,1024]{2,1,0:T(8,128)(2,1)S(1)} %get-tuple-element.61), channel_id=1, source_target_pairs={{0,12},{4,8},{8,4},{12,0},{1,13},{5,9},{9,5},{13,1},{2,14},{6,10},... | collective-permute-start | bytes 884744 | tf_op jit(solution)/shard_map/ppermute | solution.py:690
  33.6 10.9 %collective-permute-start.4 = (bf16[1,72,1024]{2,1,0:T(8,128)(2,1)S(1)}, bf16[1,72,1024]{2,1,0:T(8,128)(2,1)S(1)}, u32[]{:S(2)}, u32[]{:S(2)}) collective-permute-start(bf16[1,72,1024]{2,1,0:T(8,128)(2,1)S(1)} %slice.106), channel_id=1, source_target_pairs={{0,1},{1,0},{2,3},{3,2},{4,5},{5,4},{6,7},{7,6},{8,9},{9,8},{10,11... | collective-permute-start | bytes 442376 | tf_op jit(solution)/shard_map/ppermute | solution.py:682
  43.8 3.1 %collective-permute-start.8 = (bf16[1,72,1024]{2,1,0:T(8,128)(2,1)S(1)}, bf16[1,72,1024]{2,1,0:T(8,128)(2,1)S(1)}, u32[]{:S(2)}, u32[]{:S(2)}) collective-permute-start(bf16[1,72,1024]{2,1,0:T(8,128)(2,1)S(1)} %slice.107), channel_id=1, source_target_pairs={{0,1},{1,0},{2,3},{3,2},{4,5},{5,4},{6,7},{7,6},{8,9},{9,8},{10,11... | collective-permute-start | bytes 442376 | tf_op jit(solution)/shard_map/ppermute | solution.py:682
  43.9 3.0 %collective-permute-start.9 = (bf16[1,72,1024]{2,1,0:T(8,128)(2,1)S(1)}, bf16[1,72,1024]{2,1,0:T(8,128)(2,1)S(1)}, u32[]{:S(2)}, u32[]{:S(2)}) collective-permute-start(bf16[1,72,1024]{2,1,0:T(8,128)(2,1)S(1)} %slice.108), channel_id=1, source_target_pairs={{0,1},{1,0},{2,3},{3,2},{4,5},{5,4},{6,7},{7,6},{8,9},{9,8},{10,11... | collective-permute-start | bytes 442376 | tf_op jit(solution)/shard_map/ppermute | solution.py:682
  48.3 10.0 %collective-permute-start.10 = (bf16[136,384]{1,0:T(8,128)(2,1)S(1)}, bf16[136,384]{1,0:T(8,128)(2,1)S(1)}, u32[]{:S(2)}, u32[]{:S(2)}) collective-permute-start(bf16[136,384]{1,0:T(8,128)(2,1)S(1)} %get-tuple-element.73), channel_id=1, source_target_pairs={{0,4},{4,8},{8,12},{1,5},{5,9},{9,13},{2,6},{6,10},{10,14},{3,7},{... | collective-permute-start | bytes 313352 | tf_op jit(solution)/shard_map/ppermute | solution.py:796
  55.6 9.2 %collective-permute-start.16 = (bf16[10,256,128]{2,1,0:T(8,128)(2,1)S(1)}, bf16[10,256,128]{2,1,0:T(8,128)(2,1)S(1)}, u32[]{:S(2)}, u32[]{:S(2)}) collective-permute-start(bf16[10,256,128]{2,1,0:T(8,128)(2,1)S(1)} %maximum_maximum_fusion), channel_id=1, source_target_pairs={{0,1},{1,0},{2,3},{3,2},{4,5},{5,4},{6,7},{7,6},{8,9},{9,8},{10,11... | collective-permute-start | bytes 1966088 | tf_op jit(solution)/shard_map/ppermute | solution.py:682
  55.9 16.1 %collective-permute-start.12 = (bf16[528,384]{1,0:T(8,128)(2,1)S(1)}, bf16[528,384]{1,0:T(8,128)(2,1)S(1)}, u32[]{:S(2)}, u32[]{:S(2)}) collective-permute-start(bf16[528,384]{1,0:T(8,128)(2,1)S(1)} %get-tuple-element.75), channel_id=1, source_target_pairs={{0,2},{2,0},{1,3},{3,1},{4,6},{6,4},{5,7},{7,5},{8,10},{10,8},{9,1... | collective-permute-start | bytes 1216520 | tf_op jit(solution)/shard_map/ppermute | solution.py:686
  56.8 6.7 %collective-permute-start.11 = (bf16[136,384]{1,0:T(8,128)(2,1)S(1)}, bf16[136,384]{1,0:T(8,128)(2,1)S(1)}, u32[]{:S(2)}, u32[]{:S(2)}) collective-permute-start(bf16[136,384]{1,0:T(8,128)(2,1)S(1)} %get-tuple-element.74), channel_id=1, source_target_pairs={{4,0},{8,4},{12,8},{5,1},{9,5},{13,9},{6,2},{10,6},{14,10},{7,3},{... | collective-permute-start | bytes 313352 | tf_op jit(solution)/shard_map/ppermute | solution.py:797
  63.6 8.4 %collective-permute-start.13 = (bf16[272,384]{1,0:T(8,128)(2,1)S(1)}, bf16[272,384]{1,0:T(8,128)(2,1)S(1)}, u32[]{:S(2)}, u32[]{:S(2)}) collective-permute-start(bf16[272,384]{1,0:T(8,128)(2,1)S(1)} %constant_dynamic-update-slice_fusion.edge_ref), channel_id=1, source_target_pairs={{0,2},{2,0},{1,3},{3,1},{4,6},{6,4},{5,7},{7,5},{8,10},{10,8},{9,1... | collective-permute-start | bytes 626696 | tf_op jit(solution)/shard_map/ppermute | solution.py:686
  72.1 1.8 %collective-permute-start.17 = (bf16[1600,128]{1,0:T(8,128)(2,1)S(1)}, bf16[1600,128]{1,0:T(8,128)(2,1)S(1)}, u32[]{:S(2)}, u32[]{:S(2)}) collective-permute-start(bf16[1600,128]{1,0:T(8,128)(2,1)S(1)} %pad_maximum_fusion), channel_id=1, source_target_pairs={{0,1},{1,0},{2,3},{3,2},{4,5},{5,4},{6,7},{7,6},{8,9},{9,8},{10,11... | collective-permute-start | bytes 1228808 | tf_op jit(solution)/shard_map/ppermute | solution.py:682
  84.5 7.8 %collective-permute-start.19 = (bf16[64,768]{1,0:T(8,128)(2,1)S(1)}, bf16[64,768]{1,0:T(8,128)(2,1)S(1)}, u32[]{:S(2)}, u32[]{:S(2)}) collective-permute-start(bf16[64,768]{1,0:T(8,128)(2,1)S(1)} %get-tuple-element.86), channel_id=1, source_target_pairs={{0,4},{4,0},{8,12},{12,8},{1,5},{5,1},{9,13},{13,9},{2,6},{6,2},{1... | collective-permute-start | bytes 294920 | tf_op jit(solution)/shard_map/ppermute | solution.py:690
  86.2 10.1 %collective-permute-start.20 = (bf16[64,768]{1,0:T(8,128)(2,1)S(1)}, bf16[64,768]{1,0:T(8,128)(2,1)S(1)}, u32[]{:S(2)}, u32[]{:S(2)}) collective-permute-start(bf16[64,768]{1,0:T(8,128)(2,1)S(1)} %get-tuple-element.87), channel_id=1, source_target_pairs={{0,8},{4,12},{8,0},{12,4},{1,9},{5,13},{9,1},{13,5},{2,10},{6,14},... | collective-permute-start | bytes 294920 | tf_op jit(solution)/shard_map/ppermute | solution.py:690
  86.2 10.1 %collective-permute-start.21 = (bf16[64,768]{1,0:T(8,128)(2,1)S(1)}, bf16[64,768]{1,0:T(8,128)(2,1)S(1)}, u32[]{:S(2)}, u32[]{:S(2)}) collective-permute-start(bf16[64,768]{1,0:T(8,128)(2,1)S(1)} %get-tuple-element.88), channel_id=1, source_target_pairs={{0,12},{4,8},{8,4},{12,0},{1,13},{5,9},{9,5},{13,1},{2,14},{6,10},... | collective-permute-start | bytes 294920 | tf_op jit(solution)/shard_map/ppermute | solution.py:690
  96.4 7.5 %collective-permute-start.24 = (bf16[64,768]{1,0:T(8,128)(2,1)S(1)}, bf16[64,768]{1,0:T(8,128)(2,1)S(1)}, u32[]{:S(2)}, u32[]{:S(2)}) collective-permute-start(bf16[64,768]{1,0:T(8,128)(2,1)S(1)} %add_convert_fusion), channel_id=1, source_target_pairs={{0,12},{4,8},{8,4},{12,0},{1,13},{5,9},{9,5},{13,1},{2,14},{6,10},... | collective-permute-start | bytes 294920 | tf_op jit(solution)/shard_map/ppermute | solution.py:690
  97.5 10.8 %collective-permute-start.23 = (bf16[64,768]{1,0:T(8,128)(2,1)S(1)}, bf16[64,768]{1,0:T(8,128)(2,1)S(1)}, u32[]{:S(2)}, u32[]{:S(2)}) collective-permute-start(bf16[64,768]{1,0:T(8,128)(2,1)S(1)} %add_convert_fusion), channel_id=1, source_target_pairs={{0,8},{4,12},{8,0},{12,4},{1,9},{5,13},{9,1},{13,5},{2,10},{6,14},... | collective-permute-start | bytes 294920 | tf_op jit(solution)/shard_map/ppermute | solution.py:690
  100.0 8.3 %collective-permute-start.22 = (bf16[64,768]{1,0:T(8,128)(2,1)S(1)}, bf16[64,768]{1,0:T(8,128)(2,1)S(1)}, u32[]{:S(2)}, u32[]{:S(2)}) collective-permute-start(bf16[64,768]{1,0:T(8,128)(2,1)S(1)} %add_convert_fusion), channel_id=1, source_target_pairs={{0,4},{4,0},{8,12},{12,8},{1,5},{5,1},{9,13},{13,9},{2,6},{6,2},{1... | collective-permute-start | bytes 294920 | tf_op jit(solution)/shard_map/ppermute | solution.py:690
  (10 other events, 63.2 us)

commit v7 on v6

--- a/solution.py
+++ b/solution.py
@@ -732,10 +732,10 @@
         sent, low, high, theirs = lax.optimization_barrier((sent, low, high, theirs))
     if few:
         far = [swap_tile(sent[k + 1], n_tile, k) for k in (1, 2, 3)]
-        beside = swap_sub(sent[1])
+        near_side = swap_sub(jnp.concatenate([sent[1], far[0][1:]], axis=0))
         steps = [
-            [(sent[0], (0,)), (beside, (0,))],
-            [(far[0], (0,)), (swap_sub(far[0][1:]), (0,)), (far[1], (0,)), (far[2], (0,))],
+            [(sent[0], (0,)), (far[0], (0,)), (near_side, (0, 1))],
+            [(far[1], (0,)), (far[2], (0,))],
             [(swap_sub(far[1][1:]), (0,)), (swap_sub(far[2][1:]), (0,))],
         ]
     else:

time: 112 us -> 112 us (level)
  starting transfers between devices: 35.8 us -> 34.2 us
  waiting for transfers between devices: 41.7 us -> 43 us
    ppermute x1, starting transfers between devices: 7.17 us -> 5.64 us  [body(): low = lax.ppermute(up, 'tile', step_perm(n_tile, 1))]
    ppermute x9, waiting for transfers between devices: 28.7 us -> 30.1 us  [swap_tile(): return lax.ppermute(x, 'tile', [(i, i ^ k) for i in range(n_tile)])]
    ppermute x8 -> x7, waiting for transfers between devices: 3.7 us -> 3.7 us  [swap_sub(): return lax.ppermute(x, 'sub', [(0, 1), (1, 0)])]
  transfers between devices with their start and end apart: 26 -> 25, of which waited for: 11 -> 11; matrix products, arithmetic and copies ran while one was open for 1% -> 2% of each run, Pallas kernels for 16% -> 16%
where the time goes in v7:
time: 112 us
  waiting for transfers between devices  43 us (38%)
  starting transfers between devices  34.2 us (31%)
  Pallas kernels  29.4 us (26%)
  local copies, waits for them, and re-layouts  3.48 us (3%)
    ppermute x9, waiting for transfers between devices, swap_tile(): return lax.ppermute(x, 'tile', [(i, i ^ k) for i in range(n_tile)])  30.1 us
    ppermute x9, starting transfers between devices, swap_tile(): return lax.ppermute(x, 'tile', [(i, i ^ k) for i in range(n_tile)])  13.9 us
    pallas_call x1, Pallas kernels, grads(): call(body, outs, [smem_spec()] + [vmem_spec()] * (2 + len(ins)), [pltpu.V...  8.22 us
    ppermute x5, starting transfers between devices, swap_chan(): return lax.ppermute(x, 'chan', [(0, 1), (1, 0)])  7.1 us
    ppermute x1, starting transfers between devices, body(): low = lax.ppermute(up, 'tile', step_perm(n_tile, 1))  5.64 us
    ppermute x1, waiting for transfers between devices, body(): high = lax.ppermute(down, 'tile', step_perm(n_tile, -1))  5.23 us
    pallas_call x1, Pallas kernels, route(): call(functools.partial(route_kernel, n_tiles, cap, relative), [jax.ShapeD...  5.21 us
    pallas_call x3, Pallas kernels, grid(): call(functools.partial(grid_kernel, n_rows, n_cols, group, takes, before...  5.05 us
  transfers between devices with their start and end apart: 25, of which 11 were waited for; matrix products, arithmetic and copies ran while one was open for 2% of the time, Pallas kernels for 16%

profile of v7, /device:TPU:0, one launch (start us, length us, event | category | flops | bytes accessed | tf_op | source)
XLA Modules:
  0.0 111.6 jit_solution(8972133967933443405)
XLA Ops:
  0.7 1.8 %fusion.1 = (bf16[128,1,384]{2,1,0:T(2,128)(2,1)S(1)}, bf16[128,1,384]{2,1,0:T(2,128)(2,1)S(1)}) fusion(bf16[128,8,384]{2,1,0:T(8,128)(2,1)} %param.15), kind=kLoop, calls=%fused_computation.22 | loop fusion | bytes 393216 | tf_op jit(solution)/shard_map/slice | solution.py:720
  3.3 3.0 %collective-permute-start.2 = (bf16[3,3,200,128]{3,2,1,0:T(8,128)(2,1)S(1)}, bf16[3,3,200,128]{3,2,1,0:T(8,128)(2,1)S(1)}, u32[]{:S(2)}, u32[]{:S(2)}) collective-permute-start(bf16[3,3,200,128]{3,2,1,0:T(8,128)(2,1)S(1)} %offer.1), channel_id=1, source_target_pairs={{0,2},{2,0},{1,3},{3,1},{4,6},{6,4},{5,7},{7,5},{8,10},{10,8},{9,1... | collective-permute-start | bytes 1382408 | tf_op jit(solution)/shard_map/ppermute | solution.py:686
  6.3 3.5 %collective-permute-start = (bf16[128,384]{1,0:T(8,128)(2,1)S(1)}, bf16[128,384]{1,0:T(8,128)(2,1)S(1)}, u32[]{:S(2)}, u32[]{:S(2)}) collective-permute-start(bf16[128,384]{1,0:T(8,128)(2,1)S(1)} %get-tuple-element.56), channel_id=1, source_target_pairs={{0,4},{4,8},{8,12},{1,5},{5,9},{9,13},{2,6},{6,10},{10,14},{3,7},{... | collective-permute-start | bytes 294920 | tf_op jit(solution)/shard_map/ppermute | solution.py:726
  11.1 5.2 %route.1 = (bf16[1,72,1024]{2,1,0:T(8,128)(2,1)S(1)}, bf16[1,72,1024]{2,1,0:T(8,128)(2,1)S(1)}, bf16[2,72,1024]{2,1,0:T(8,128)(2,1)S(1)}, bf16[2,72,1024]{2,1,0:T(8,128)(2,1)S(1)}, bf16[2,72,1024]{2,1,0:T(8,128)(2,1)S(1)}) custom-call(s32[5]{0:T(128)S(1)} %stack.43.index_ref, s32[32,128]{1,0:T(8,128)S(1)} %bitcast.37, bf16[32,128]{1,0:T(8,128)(2,1)S(1)} %bitcast.39, ...), custom_call_target="tpu_custom_call" | custom-call | flops 1342177280 | bytes 1179648 | tf_op jit(solution)/shard_map/route/pallas_call | solution.py:176
  16.9 2.2 %collective-permute-start.5 = (bf16[2,72,1024]{2,1,0:T(8,128)(2,1)S(1)}, bf16[2,72,1024]{2,1,0:T(8,128)(2,1)S(1)}, u32[]{:S(2)}, u32[]{:S(2)}) collective-permute-start(bf16[2,72,1024]{2,1,0:T(8,128)(2,1)S(1)} %get-tuple-element.62), channel_id=1, source_target_pairs={{0,4},{4,0},{8,12},{12,8},{1,5},{5,1},{9,13},{13,9},{2,6},{6,2},{1... | collective-permute-start | bytes 884744 | tf_op jit(solution)/shard_map/ppermute | solution.py:690
  20.3 2.6 %collective-permute-start.3 = (bf16[2,72,1024]{2,1,0:T(8,128)(2,1)S(1)}, bf16[2,72,1024]{2,1,0:T(8,128)(2,1)S(1)}, u32[]{:S(2)}, u32[]{:S(2)}) collective-permute-start(bf16[2,72,1024]{2,1,0:T(8,128)(2,1)S(1)} %get-tuple-element.59), channel_id=1, source_target_pairs={{0,8},{4,12},{8,0},{12,4},{1,9},{5,13},{9,1},{13,5},{2,10},{6,14},... | collective-permute-start | bytes 884744 | tf_op jit(solution)/shard_map/ppermute | solution.py:690
  24.0 5.8 %collective-permute-done.5.rest_1_ = bf16[2,72,1024]{2,1,0:T(8,128)(2,1)S(1)} collective-permute-done((bf16[2,72,1024]{2,1,0:T(8,128)(2,1)S(1)}, bf16[2,72,1024]{2,1,0:T(8,128)(2,1)S(1)}, u32[]{:S(2)}, u32[]{:S(2)}) %collective-permute-start.5) | collective-permute-done | bytes 294944 | tf_op jit(solution)/shard_map/ppermute | solution.py:690
  30.9 12.9 %collective-permute-done.3.rest_0_ = bf16[2,72,1024]{2,1,0:T(8,128)(2,1)S(1)} collective-permute-done((bf16[2,72,1024]{2,1,0:T(8,128)(2,1)S(1)}, bf16[2,72,1024]{2,1,0:T(8,128)(2,1)S(1)}, u32[]{:S(2)}, u32[]{:S(2)}) %collective-permute-start.3) | collective-permute-done | bytes 294944 | tf_op jit(solution)/shard_map/ppermute | solution.py:690
  44.4 2.4 %grid_part.2.rest_2_ = f32[528,384]{1,0:T(8,128)S(1)} custom-call(bf16[1,72,1024]{2,1,0:T(8,128)(2,1)S(1)} %get-tuple-element.61.rest_0_, bf16[2,72,1024]{2,1,0:T(8,128)(2,1)S(1)} %collective-permute-done.5.rest_1_, bf16[2,72,1024]{2,1,0:T(8,128)(2,1)S(1)} %collective-permute-done.6.rest_2_), custom_call_target="tpu_custom_call" | custom-call | flops 1660944384 | bytes 589824 | tf_op jit(solution)/shard_map/grid_part/pallas_call | solution.py:269
  49.5 5.6 %collective-permute-start.9 = (bf16[136,384]{1,0:T(8,128)(2,1)S(1)}, bf16[136,384]{1,0:T(8,128)(2,1)S(1)}, u32[]{:S(2)}, u32[]{:S(2)}) collective-permute-start(bf16[136,384]{1,0:T(8,128)(2,1)S(1)} %get-tuple-element.73), channel_id=1, source_target_pairs={{0,4},{4,8},{8,12},{1,5},{5,9},{9,13},{2,6},{6,10},{10,14},{3,7},{... | collective-permute-start | bytes 313352 | tf_op jit(solution)/shard_map/ppermute | solution.py:796
  58.1 5.2 %collective-permute-done.10 = bf16[136,384]{1,0:T(8,128)(2,1)S(1)} collective-permute-done((bf16[136,384]{1,0:T(8,128)(2,1)S(1)}, bf16[136,384]{1,0:T(8,128)(2,1)S(1)}, u32[]{:S(2)}, u32[]{:S(2)}) %collective-permute-start.10) | collective-permute-done | bytes 104480 | tf_op jit(solution)/shard_map/ppermute | solution.py:797
  64.5 3.7 %back.1.back_ref = f32[128,3072]{1,0:T(8,128)S(1)} custom-call(s32[5]{0:T(128)S(1)} %stack.43.index_ref, bf16[3,128,768]{2,1,0:T(8,128)(2,1)S(1)} %get-tuple-element.76.kernel_ref, bf16[8,128,384]{2,1,0:T(8,128)(2,1)S(1)} %bitcast.27, bf16[2,128,384]{2,1,0:T(8,128)(2,1)S(1)} %pad_maximum_fusion.3.rest_1_, bf16[8,128,384]{2,1,0:T(8,128)(2,1)S(1)} %bitcast.33, ...), custom_call_target="tpu_custom_call" | custom-call | flops 2264924160 | bytes 1966080 | tf_op jit(solution)/shard_map/back/pallas_call | solution.py:321
  68.2 3.5 %collective-permute-done.12.peer_edge_ref = bf16[272,384]{1,0:T(8,128)(2,1)S(1)} collective-permute-done((bf16[272,384]{1,0:T(8,128)(2,1)S(1)}, bf16[272,384]{1,0:T(8,128)(2,1)S(1)}, u32[]{:S(2)}, u32[]{:S(2)}) %collective-permute-start.12) | collective-permute-done | bytes 208928 | tf_op jit(solution)/shard_map/ppermute | solution.py:686
  71.9 1.7 %collective-permute-done.16.side_ref = bf16[1600,128]{1,0:T(8,128)(2,1)S(1)} collective-permute-done((bf16[1600,128]{1,0:T(8,128)(2,1)S(1)}, bf16[1600,128]{1,0:T(8,128)(2,1)S(1)}, u32[]{:S(2)}, u32[]{:S(2)}) %collective-permute-start.16) | collective-permute-done | bytes 409632 | tf_op jit(solution)/shard_map/ppermute | solution.py:682
  73.6 8.2 %grads.1 = (bf16[10,256,512]{2,1,0:T(8,128)(2,1)S(1)}, f32[256,768]{1,0:T(8,128)S(1)}, bf16[256,768]{1,0:T(8,128)(2,1)S(1)}) custom-call(s32[5]{0:T(128)S(1)} %stack.43.index_ref, bf16[3,256,192]{2,1,0:T(8,128)(2,1)S(1)} %get-tuple-element.69.kernel_ref, f32[256,128]{1,0:T(8,128)S(1)} %get-tuple-element.70.gain_ref, ...), custom_call_target="tpu_custom_call" | custom-call | flops 3397386240 | bytes 5898240 | tf_op jit(solution)/shard_map/grads/pallas_call | solution.py:485
  82.0 1.6 %collective-permute-done.17.got_ref = bf16[256,768]{1,0:T(8,128)(2,1)S(1)} collective-permute-done((bf16[256,768]{1,0:T(8,128)(2,1)S(1)}, bf16[256,768]{1,0:T(8,128)(2,1)S(1)}, u32[]{:S(2)}, u32[]{:S(2)}) %collective-permute-start.17) | collective-permute-done | bytes 393248 | tf_op jit(solution)/shard_map/ppermute | solution.py:682
  84.2 1.6 %collective-permute-start.18 = (bf16[64,768]{1,0:T(8,128)(2,1)S(1)}, bf16[64,768]{1,0:T(8,128)(2,1)S(1)}, u32[]{:S(2)}, u32[]{:S(2)}) collective-permute-start(bf16[64,768]{1,0:T(8,128)(2,1)S(1)} %get-tuple-element.86), channel_id=1, source_target_pairs={{0,4},{4,0},{8,12},{12,8},{1,5},{5,1},{9,13},{13,9},{2,6},{6,2},{1... | collective-permute-start | bytes 294920 | tf_op jit(solution)/shard_map/ppermute | solution.py:690
  85.9 2.8 %collective-permute-start.20 = (bf16[64,768]{1,0:T(8,128)(2,1)S(1)}, bf16[64,768]{1,0:T(8,128)(2,1)S(1)}, u32[]{:S(2)}, u32[]{:S(2)}) collective-permute-start(bf16[64,768]{1,0:T(8,128)(2,1)S(1)} %get-tuple-element.88), channel_id=1, source_target_pairs={{0,12},{4,8},{8,4},{12,0},{1,13},{5,9},{9,5},{13,1},{2,14},{6,10},... | collective-permute-start | bytes 294920 | tf_op jit(solution)/shard_map/ppermute | solution.py:690
  88.7 3.3 %encode.1 = bf16[8,128,384]{2,1,0:T(8,128)(2,1)S(1)} custom-call(bf16[3,128,768]{2,1,0:T(8,128)(2,1)S(1)} %get-tuple-element.89.kernel_ref, bf16[10,256,512]{2,1,0:T(8,128)(2,1)S(1)} %get-tuple-element.90.hidden_ref), custom_call_target="tpu_custom_call" | custom-call | flops 2264924160 | bytes 2621440 | tf_op jit(solution)/shard_map/encode/pallas_call | solution.py:525
  92.0 4.0 %collective-permute-done.19 = bf16[64,768]{1,0:T(8,128)(2,1)S(1)} collective-permute-done((bf16[64,768]{1,0:T(8,128)(2,1)S(1)}, bf16[64,768]{1,0:T(8,128)(2,1)S(1)}, u32[]{:S(2)}, u32[]{:S(2)}) %collective-permute-start.19) | collective-permute-done | bytes 98336 | tf_op jit(solution)/shard_map/ppermute | solution.py:690
  97.2 2.5 %collective-permute-start.22 = (bf16[64,768]{1,0:T(8,128)(2,1)S(1)}, bf16[64,768]{1,0:T(8,128)(2,1)S(1)}, u32[]{:S(2)}, u32[]{:S(2)}) collective-permute-start(bf16[64,768]{1,0:T(8,128)(2,1)S(1)} %add_convert_fusion), channel_id=1, source_target_pairs={{0,8},{4,12},{8,0},{12,4},{1,9},{5,13},{9,1},{13,5},{2,10},{6,14},... | collective-permute-start | bytes 294920 | tf_op jit(solution)/shard_map/ppermute | solution.py:690
  100.5 3.0 %collective-permute-done.23 = bf16[64,768]{1,0:T(8,128)(2,1)S(1)} collective-permute-done((bf16[64,768]{1,0:T(8,128)(2,1)S(1)}, bf16[64,768]{1,0:T(8,128)(2,1)S(1)}, u32[]{:S(2)}, u32[]{:S(2)}) %collective-permute-start.23) | collective-permute-done | bytes 98336 | tf_op jit(solution)/shard_map/ppermute | solution.py:690
  103.6 4.4 %collective-permute-done.22 = bf16[64,768]{1,0:T(8,128)(2,1)S(1)} collective-permute-done((bf16[64,768]{1,0:T(8,128)(2,1)S(1)}, bf16[64,768]{1,0:T(8,128)(2,1)S(1)}, u32[]{:S(2)}, u32[]{:S(2)}) %collective-permute-start.22) | collective-permute-done | bytes 98336 | tf_op jit(solution)/shard_map/ppermute | solution.py:690
  109.8 1.8 %finish.1 = (f32[3,3,128,256]{3,2,1,0:T(8,128)}, f32[3,3,64,128]{3,2,1,0:T(8,128)}, f32[1,128]{1,0:T(1,128)}) custom-call(s32[5]{0:T(128)S(1)} %stack.43.index_ref, bf16[4,64,768]{2,1,0:T(8,128)(2,1)S(1)} %pad_maximum_fusion.1.mine_ref, bf16[4,64,768]{2,1,0:T(8,128)(2,1)S(1)} %collective-permute-done.24.other_ref), custom_call_target="tpu_custom_call" | custom-call | flops 196608 | bytes 2359296 | tf_op jit(solution)/shard_map/finish/pallas_call | solution.py:587
  (78 shorter events, 18.0 us)
Async XLA Ops:
  3.3 13.6 %collective-permute-start.2 = (bf16[3,3,200,128]{3,2,1,0:T(8,128)(2,1)S(1)}, bf16[3,3,200,128]{3,2,1,0:T(8,128)(2,1)S(1)}, u32[]{:S(2)}, u32[]{:S(2)}) collective-permute-start(bf16[3,3,200,128]{3,2,1,0:T(8,128)(2,1)S(1)} %offer.1), channel_id=1, source_target_pairs={{0,2},{2,0},{1,3},{3,1},{4,6},{6,4},{5,7},{7,5},{8,10},{10,8},{9,1... | collective-permute-start | bytes 1382408 | tf_op jit(solution)/shard_map/ppermute | solution.py:686
  6.3 10.1 %collective-permute-start = (bf16[128,384]{1,0:T(8,128)(2,1)S(1)}, bf16[128,384]{1,0:T(8,128)(2,1)S(1)}, u32[]{:S(2)}, u32[]{:S(2)}) collective-permute-start(bf16[128,384]{1,0:T(8,128)(2,1)S(1)} %get-tuple-element.56), channel_id=1, source_target_pairs={{0,4},{4,8},{8,12},{1,5},{5,9},{9,13},{2,6},{6,10},{10,14},{3,7},{... | collective-permute-start | bytes 294920 | tf_op jit(solution)/shard_map/ppermute | solution.py:726
  9.8 6.6 %collective-permute-start.1 = (bf16[128,384]{1,0:T(8,128)(2,1)S(1)}, bf16[128,384]{1,0:T(8,128)(2,1)S(1)}, u32[]{:S(2)}, u32[]{:S(2)}) collective-permute-start(bf16[128,384]{1,0:T(8,128)(2,1)S(1)} %get-tuple-element.57), channel_id=1, source_target_pairs={{4,0},{8,4},{12,8},{5,1},{9,5},{13,9},{6,2},{10,6},{14,10},{7,3},{... | collective-permute-start | bytes 294920 | tf_op jit(solution)/shard_map/ppermute | solution.py:727
  16.9 12.9 %collective-permute-start.5 = (bf16[2,72,1024]{2,1,0:T(8,128)(2,1)S(1)}, bf16[2,72,1024]{2,1,0:T(8,128)(2,1)S(1)}, u32[]{:S(2)}, u32[]{:S(2)}) collective-permute-start(bf16[2,72,1024]{2,1,0:T(8,128)(2,1)S(1)} %get-tuple-element.62), channel_id=1, source_target_pairs={{0,4},{4,0},{8,12},{12,8},{1,5},{5,1},{9,13},{13,9},{2,6},{6,2},{1... | collective-permute-start | bytes 884744 | tf_op jit(solution)/shard_map/ppermute | solution.py:690
  19.1 11.7 %collective-permute-start.14 = (bf16[2,128,384]{2,1,0:T(8,128)(2,1)S(1)}, bf16[2,128,384]{2,1,0:T(8,128)(2,1)S(1)}, u32[]{:S(2)}, u32[]{:S(2)}) collective-permute-start(bf16[2,128,384]{2,1,0:T(8,128)(2,1)S(1)} %pad_maximum_fusion.3.rest_1_), channel_id=1, source_target_pairs={{0,2},{2,0},{1,3},{3,1},{4,6},{6,4},{5,7},{7,5},{8,10},{10,8},{9,1... | collective-permute-start | bytes 589832 | tf_op jit(solution)/shard_map/ppermute | solution.py:686
  20.3 23.5 %collective-permute-start.3 = (bf16[2,72,1024]{2,1,0:T(8,128)(2,1)S(1)}, bf16[2,72,1024]{2,1,0:T(8,128)(2,1)S(1)}, u32[]{:S(2)}, u32[]{:S(2)}) collective-permute-start(bf16[2,72,1024]{2,1,0:T(8,128)(2,1)S(1)} %get-tuple-element.59), channel_id=1, source_target_pairs={{0,8},{4,12},{8,0},{12,4},{1,9},{5,13},{9,1},{13,5},{2,10},{6,14},... | collective-permute-start | bytes 884744 | tf_op jit(solution)/shard_map/ppermute | solution.py:690
  22.9 21.0 %collective-permute-start.4 = (bf16[2,72,1024]{2,1,0:T(8,128)(2,1)S(1)}, bf16[2,72,1024]{2,1,0:T(8,128)(2,1)S(1)}, u32[]{:S(2)}, u32[]{:S(2)}) collective-permute-start(bf16[2,72,1024]{2,1,0:T(8,128)(2,1)S(1)} %get-tuple-element.60), channel_id=1, source_target_pairs={{0,12},{4,8},{8,4},{12,0},{1,13},{5,9},{9,5},{13,1},{2,14},{6,10},... | collective-permute-start | bytes 884744 | tf_op jit(solution)/shard_map/ppermute | solution.py:690
  23.2 32.0 %collective-permute-start.13 = (bf16[128,8,384]{2,0,1:T(8,128)(2,1)S(1)}, bf16[128,8,384]{2,0,1:T(8,128)(2,1)S(1)}, u32[]{:S(2)}, u32[]{:S(2)}) collective-permute-start(bf16[128,8,384]{2,0,1:T(8,128)(2,1)S(1)} %copy.23), channel_id=1, source_target_pairs={{0,2},{2,0},{1,3},{3,1},{4,6},{6,4},{5,7},{7,5},{8,10},{10,8},{9,1... | collective-permute-start | bytes 2359304 | tf_op jit(solution)/shard_map/ppermute | solution.py:686
  29.8 14.6 %collective-permute-start.6 = (bf16[2,72,1024]{2,1,0:T(8,128)(2,1)S(1)}, bf16[2,72,1024]{2,1,0:T(8,128)(2,1)S(1)}, u32[]{:S(2)}, u32[]{:S(2)}) collective-permute-start(bf16[2,72,1024]{2,1,0:T(8,128)(2,1)S(1)} %pad_maximum_fusion.2), channel_id=1, source_target_pairs={{0,1},{1,0},{2,3},{3,2},{4,5},{5,4},{6,7},{7,6},{8,9},{9,8},{10,11... | collective-permute-start | bytes 884744 | tf_op jit(solution)/shard_map/ppermute | solution.py:682
  43.8 4.4 %collective-permute-start.7 = (bf16[1,72,1024]{2,1,0:T(8,128)(2,1)S(1)}, bf16[1,72,1024]{2,1,0:T(8,128)(2,1)S(1)}, u32[]{:S(2)}, u32[]{:S(2)}) collective-permute-start(bf16[1,72,1024]{2,1,0:T(8,128)(2,1)S(1)} %slice.107), channel_id=1, source_target_pairs={{0,1},{1,0},{2,3},{3,2},{4,5},{5,4},{6,7},{7,6},{8,9},{9,8},{10,11... | collective-permute-start | bytes 442376 | tf_op jit(solution)/shard_map/ppermute | solution.py:682
  43.9 4.3 %collective-permute-start.8 = (bf16[1,72,1024]{2,1,0:T(8,128)(2,1)S(1)}, bf16[1,72,1024]{2,1,0:T(8,128)(2,1)S(1)}, u32[]{:S(2)}, u32[]{:S(2)}) collective-permute-start(bf16[1,72,1024]{2,1,0:T(8,128)(2,1)S(1)} %slice.108), channel_id=1, source_target_pairs={{0,1},{1,0},{2,3},{3,2},{4,5},{5,4},{6,7},{7,6},{8,9},{9,8},{10,11... | collective-permute-start | bytes 442376 | tf_op jit(solution)/shard_map/ppermute | solution.py:682
  49.5 8.6 %collective-permute-start.9 = (bf16[136,384]{1,0:T(8,128)(2,1)S(1)}, bf16[136,384]{1,0:T(8,128)(2,1)S(1)}, u32[]{:S(2)}, u32[]{:S(2)}) collective-permute-start(bf16[136,384]{1,0:T(8,128)(2,1)S(1)} %get-tuple-element.73), channel_id=1, source_target_pairs={{0,4},{4,8},{8,12},{1,5},{5,9},{9,13},{2,6},{6,10},{10,14},{3,7},{... | collective-permute-start | bytes 313352 | tf_op jit(solution)/shard_map/ppermute | solution.py:796
  55.3 9.2 %collective-permute-start.15 = (bf16[10,256,128]{2,1,0:T(8,128)(2,1)S(1)}, bf16[10,256,128]{2,1,0:T(8,128)(2,1)S(1)}, u32[]{:S(2)}, u32[]{:S(2)}) collective-permute-start(bf16[10,256,128]{2,1,0:T(8,128)(2,1)S(1)} %maximum_maximum_fusion), channel_id=1, source_target_pairs={{0,1},{1,0},{2,3},{3,2},{4,5},{5,4},{6,7},{7,6},{8,9},{9,8},{10,11... | collective-permute-start | bytes 1966088 | tf_op jit(solution)/shard_map/ppermute | solution.py:682
  55.6 16.1 %collective-permute-start.11 = (bf16[528,384]{1,0:T(8,128)(2,1)S(1)}, bf16[528,384]{1,0:T(8,128)(2,1)S(1)}, u32[]{:S(2)}, u32[]{:S(2)}) collective-permute-start(bf16[528,384]{1,0:T(8,128)(2,1)S(1)} %get-tuple-element.75), channel_id=1, source_target_pairs={{0,2},{2,0},{1,3},{3,1},{4,6},{6,4},{5,7},{7,5},{8,10},{10,8},{9,1... | collective-permute-start | bytes 1216520 | tf_op jit(solution)/shard_map/ppermute | solution.py:686
  56.6 6.7 %collective-permute-start.10 = (bf16[136,384]{1,0:T(8,128)(2,1)S(1)}, bf16[136,384]{1,0:T(8,128)(2,1)S(1)}, u32[]{:S(2)}, u32[]{:S(2)}) collective-permute-start(bf16[136,384]{1,0:T(8,128)(2,1)S(1)} %get-tuple-element.74), channel_id=1, source_target_pairs={{4,0},{8,4},{12,8},{5,1},{9,5},{13,9},{6,2},{10,6},{14,10},{7,3},{... | collective-permute-start | bytes 313352 | tf_op jit(solution)/shard_map/ppermute | solution.py:797
  63.4 8.3 %collective-permute-start.12 = (bf16[272,384]{1,0:T(8,128)(2,1)S(1)}, bf16[272,384]{1,0:T(8,128)(2,1)S(1)}, u32[]{:S(2)}, u32[]{:S(2)}) collective-permute-start(bf16[272,384]{1,0:T(8,128)(2,1)S(1)} %constant_dynamic-update-slice_fusion.edge_ref), channel_id=1, source_target_pairs={{0,2},{2,0},{1,3},{3,1},{4,6},{6,4},{5,7},{7,5},{8,10},{10,8},{9,1... | collective-permute-start | bytes 626696 | tf_op jit(solution)/shard_map/ppermute | solution.py:686
  71.8 1.8 %collective-permute-start.16 = (bf16[1600,128]{1,0:T(8,128)(2,1)S(1)}, bf16[1600,128]{1,0:T(8,128)(2,1)S(1)}, u32[]{:S(2)}, u32[]{:S(2)}) collective-permute-start(bf16[1600,128]{1,0:T(8,128)(2,1)S(1)} %pad_maximum_fusion), channel_id=1, source_target_pairs={{0,1},{1,0},{2,3},{3,2},{4,5},{5,4},{6,7},{7,6},{8,9},{9,8},{10,11... | collective-permute-start | bytes 1228808 | tf_op jit(solution)/shard_map/ppermute | solution.py:682
  81.8 1.8 %collective-permute-start.17 = (bf16[256,768]{1,0:T(8,128)(2,1)S(1)}, bf16[256,768]{1,0:T(8,128)(2,1)S(1)}, u32[]{:S(2)}, u32[]{:S(2)}) collective-permute-start(bf16[256,768]{1,0:T(8,128)(2,1)S(1)} %get-tuple-element.84), channel_id=1, source_target_pairs={{0,1},{1,0},{2,3},{3,2},{4,5},{5,4},{6,7},{7,6},{8,9},{9,8},{10,11... | collective-permute-start | bytes 1179656 | tf_op jit(solution)/shard_map/ppermute | solution.py:682
  84.2 7.8 %collective-permute-start.18 = (bf16[64,768]{1,0:T(8,128)(2,1)S(1)}, bf16[64,768]{1,0:T(8,128)(2,1)S(1)}, u32[]{:S(2)}, u32[]{:S(2)}) collective-permute-start(bf16[64,768]{1,0:T(8,128)(2,1)S(1)} %get-tuple-element.86), channel_id=1, source_target_pairs={{0,4},{4,0},{8,12},{12,8},{1,5},{5,1},{9,13},{13,9},{2,6},{6,2},{1... | collective-permute-start | bytes 294920 | tf_op jit(solution)/shard_map/ppermute | solution.py:690
  85.9 10.2 %collective-permute-start.19 = (bf16[64,768]{1,0:T(8,128)(2,1)S(1)}, bf16[64,768]{1,0:T(8,128)(2,1)S(1)}, u32[]{:S(2)}, u32[]{:S(2)}) collective-permute-start(bf16[64,768]{1,0:T(8,128)(2,1)S(1)} %get-tuple-element.87), channel_id=1, source_target_pairs={{0,8},{4,12},{8,0},{12,4},{1,9},{5,13},{9,1},{13,5},{2,10},{6,14},... | collective-permute-start | bytes 294920 | tf_op jit(solution)/shard_map/ppermute | solution.py:690
  85.9 10.2 %collective-permute-start.20 = (bf16[64,768]{1,0:T(8,128)(2,1)S(1)}, bf16[64,768]{1,0:T(8,128)(2,1)S(1)}, u32[]{:S(2)}, u32[]{:S(2)}) collective-permute-start(bf16[64,768]{1,0:T(8,128)(2,1)S(1)} %get-tuple-element.88), channel_id=1, source_target_pairs={{0,12},{4,8},{8,4},{12,0},{1,13},{5,9},{9,5},{13,1},{2,14},{6,10},... | collective-permute-start | bytes 294920 | tf_op jit(solution)/shard_map/ppermute | solution.py:690
  96.1 7.5 %collective-permute-start.23 = (bf16[64,768]{1,0:T(8,128)(2,1)S(1)}, bf16[64,768]{1,0:T(8,128)(2,1)S(1)}, u32[]{:S(2)}, u32[]{:S(2)}) collective-permute-start(bf16[64,768]{1,0:T(8,128)(2,1)S(1)} %add_convert_fusion), channel_id=1, source_target_pairs={{0,12},{4,8},{8,4},{12,0},{1,13},{5,9},{9,5},{13,1},{2,14},{6,10},... | collective-permute-start | bytes 294920 | tf_op jit(solution)/shard_map/ppermute | solution.py:690
  97.2 10.8 %collective-permute-start.22 = (bf16[64,768]{1,0:T(8,128)(2,1)S(1)}, bf16[64,768]{1,0:T(8,128)(2,1)S(1)}, u32[]{:S(2)}, u32[]{:S(2)}) collective-permute-start(bf16[64,768]{1,0:T(8,128)(2,1)S(1)} %add_convert_fusion), channel_id=1, source_target_pairs={{0,8},{4,12},{8,0},{12,4},{1,9},{5,13},{9,1},{13,5},{2,10},{6,14},... | collective-permute-start | bytes 294920 | tf_op jit(solution)/shard_map/ppermute | solution.py:690
  99.7 8.2 %collective-permute-start.21 = (bf16[64,768]{1,0:T(8,128)(2,1)S(1)}, bf16[64,768]{1,0:T(8,128)(2,1)S(1)}, u32[]{:S(2)}, u32[]{:S(2)}) collective-permute-start(bf16[64,768]{1,0:T(8,128)(2,1)S(1)} %add_convert_fusion), channel_id=1, source_target_pairs={{0,4},{4,0},{8,12},{12,8},{1,5},{5,1},{9,13},{13,9},{2,6},{6,2},{1... | collective-permute-start | bytes 294920 | tf_op jit(solution)/shard_map/ppermute | solution.py:690
  (9 other events, 61.5 us)

commit v8 on v7

--- a/solution.py
+++ b/solution.py
@@ -142,11 +142,11 @@
             add(t, wide, tile, slot, info_smem[0, t * n_lines + 2 * b] + skip)
 
     def first_some(i, carry):
-        for j in range(8):
-            place_block(8 * i + j, 0)
+        for j in range(n_blocks):
+            place_block(n_blocks * i + j, 0)
         return carry
 
-    lax.fori_loop(0, n_blocks // 8, first_some, 0)
+    lax.fori_loop(0, 1, first_some, 0)
 
     @pl.when(info_smem[1, 0] > 0)
     def _():

time: 112 us -> 112 us (level)
  no operation moved by 1% of the time
where the time goes in v8:
time: 112 us
  waiting for transfers between devices  42.9 us (38%)
  starting transfers between devices  34.3 us (31%)
  Pallas kernels  29.5 us (26%)
  local copies, waits for them, and re-layouts  3.48 us (3%)
    ppermute x9, waiting for transfers between devices, swap_tile(): return lax.ppermute(x, 'tile', [(i, i ^ k) for i in range(n_tile)])  30 us
    ppermute x9, starting transfers between devices, swap_tile(): return lax.ppermute(x, 'tile', [(i, i ^ k) for i in range(n_tile)])  14 us
    pallas_call x1, Pallas kernels, grads(): call(body, outs, [smem_spec()] + [vmem_spec()] * (2 + len(ins)), [pltpu.V...  8.22 us
    ppermute x5, starting transfers between devices, swap_chan(): return lax.ppermute(x, 'chan', [(0, 1), (1, 0)])  7.1 us
    ppermute x1, starting transfers between devices, body(): low = lax.ppermute(up, 'tile', step_perm(n_tile, 1))  5.63 us
    pallas_call x1, Pallas kernels, route(): call(functools.partial(route_kernel, n_tiles, cap, relative), [jax.ShapeD...  5.27 us
    ppermute x1, waiting for transfers between devices, body(): high = lax.ppermute(down, 'tile', step_perm(n_tile, -1))  5.23 us
    pallas_call x3, Pallas kernels, grid(): call(functools.partial(grid_kernel, n_rows, n_cols, group, takes, before...  5.05 us
  transfers between devices with their start and end apart: 25, of which 11 were waited for; matrix products, arithmetic and copies ran while one was open for 2% of the time, Pallas kernels for 16%

profile of v8, /device:TPU:0, one launch (start us, length us, event | category | flops | bytes accessed | tf_op | source)
XLA Modules:
  0.0 111.6 jit_solution(4086565232389746407)
XLA Ops:
  0.7 1.8 %fusion.1 = (bf16[128,1,384]{2,1,0:T(2,128)(2,1)S(1)}, bf16[128,1,384]{2,1,0:T(2,128)(2,1)S(1)}) fusion(bf16[128,8,384]{2,1,0:T(8,128)(2,1)} %param.15), kind=kLoop, calls=%fused_computation.22 | loop fusion | bytes 393216 | tf_op jit(solution)/shard_map/slice | solution.py:720
  3.3 3.0 %collective-permute-start.2 = (bf16[3,3,200,128]{3,2,1,0:T(8,128)(2,1)S(1)}, bf16[3,3,200,128]{3,2,1,0:T(8,128)(2,1)S(1)}, u32[]{:S(2)}, u32[]{:S(2)}) collective-permute-start(bf16[3,3,200,128]{3,2,1,0:T(8,128)(2,1)S(1)} %offer.1), channel_id=1, source_target_pairs={{0,2},{2,0},{1,3},{3,1},{4,6},{6,4},{5,7},{7,5},{8,10},{10,8},{9,1... | collective-permute-start | bytes 1382408 | tf_op jit(solution)/shard_map/ppermute | solution.py:686
  6.3 3.5 %collective-permute-start = (bf16[128,384]{1,0:T(8,128)(2,1)S(1)}, bf16[128,384]{1,0:T(8,128)(2,1)S(1)}, u32[]{:S(2)}, u32[]{:S(2)}) collective-permute-start(bf16[128,384]{1,0:T(8,128)(2,1)S(1)} %get-tuple-element.56), channel_id=1, source_target_pairs={{0,4},{4,8},{8,12},{1,5},{5,9},{9,13},{2,6},{6,10},{10,14},{3,7},{... | collective-permute-start | bytes 294920 | tf_op jit(solution)/shard_map/ppermute | solution.py:726
  11.1 5.3 %route.1 = (bf16[1,72,1024]{2,1,0:T(8,128)(2,1)S(1)}, bf16[1,72,1024]{2,1,0:T(8,128)(2,1)S(1)}, bf16[2,72,1024]{2,1,0:T(8,128)(2,1)S(1)}, bf16[2,72,1024]{2,1,0:T(8,128)(2,1)S(1)}, bf16[2,72,1024]{2,1,0:T(8,128)(2,1)S(1)}) custom-call(s32[5]{0:T(128)S(1)} %stack.43.index_ref, s32[32,128]{1,0:T(8,128)S(1)} %bitcast.37, bf16[32,128]{1,0:T(8,128)(2,1)S(1)} %bitcast.39, ...), custom_call_target="tpu_custom_call" | custom-call | flops 1342177280 | bytes 1179648 | tf_op jit(solution)/shard_map/route/pallas_call | solution.py:176
  16.9 2.3 %collective-permute-start.5 = (bf16[2,72,1024]{2,1,0:T(8,128)(2,1)S(1)}, bf16[2,72,1024]{2,1,0:T(8,128)(2,1)S(1)}, u32[]{:S(2)}, u32[]{:S(2)}) collective-permute-start(bf16[2,72,1024]{2,1,0:T(8,128)(2,1)S(1)} %get-tuple-element.62), channel_id=1, source_target_pairs={{0,4},{4,0},{8,12},{12,8},{1,5},{5,1},{9,13},{13,9},{2,6},{6,2},{1... | collective-permute-start | bytes 884744 | tf_op jit(solution)/shard_map/ppermute | solution.py:690
  20.3 2.6 %collective-permute-start.3 = (bf16[2,72,1024]{2,1,0:T(8,128)(2,1)S(1)}, bf16[2,72,1024]{2,1,0:T(8,128)(2,1)S(1)}, u32[]{:S(2)}, u32[]{:S(2)}) collective-permute-start(bf16[2,72,1024]{2,1,0:T(8,128)(2,1)S(1)} %get-tuple-element.59), channel_id=1, source_target_pairs={{0,8},{4,12},{8,0},{12,4},{1,9},{5,13},{9,1},{13,5},{2,10},{6,14},... | collective-permute-start | bytes 884744 | tf_op jit(solution)/shard_map/ppermute | solution.py:690
  24.1 5.8 %collective-permute-done.5.rest_1_ = bf16[2,72,1024]{2,1,0:T(8,128)(2,1)S(1)} collective-permute-done((bf16[2,72,1024]{2,1,0:T(8,128)(2,1)S(1)}, bf16[2,72,1024]{2,1,0:T(8,128)(2,1)S(1)}, u32[]{:S(2)}, u32[]{:S(2)}) %collective-permute-start.5) | collective-permute-done | bytes 294944 | tf_op jit(solution)/shard_map/ppermute | solution.py:690
  31.0 12.8 %collective-permute-done.3.rest_0_ = bf16[2,72,1024]{2,1,0:T(8,128)(2,1)S(1)} collective-permute-done((bf16[2,72,1024]{2,1,0:T(8,128)(2,1)S(1)}, bf16[2,72,1024]{2,1,0:T(8,128)(2,1)S(1)}, u32[]{:S(2)}, u32[]{:S(2)}) %collective-permute-start.3) | collective-permute-done | bytes 294944 | tf_op jit(solution)/shard_map/ppermute | solution.py:690
  44.4 2.4 %grid_part.2.rest_2_ = f32[528,384]{1,0:T(8,128)S(1)} custom-call(bf16[1,72,1024]{2,1,0:T(8,128)(2,1)S(1)} %get-tuple-element.61.rest_0_, bf16[2,72,1024]{2,1,0:T(8,128)(2,1)S(1)} %collective-permute-done.5.rest_1_, bf16[2,72,1024]{2,1,0:T(8,128)(2,1)S(1)} %collective-permute-done.6.rest_2_), custom_call_target="tpu_custom_call" | custom-call | flops 1660944384 | bytes 589824 | tf_op jit(solution)/shard_map/grid_part/pallas_call | solution.py:269
  49.5 5.6 %collective-permute-start.9 = (bf16[136,384]{1,0:T(8,128)(2,1)S(1)}, bf16[136,384]{1,0:T(8,128)(2,1)S(1)}, u32[]{:S(2)}, u32[]{:S(2)}) collective-permute-start(bf16[136,384]{1,0:T(8,128)(2,1)S(1)} %get-tuple-element.73), channel_id=1, source_target_pairs={{0,4},{4,8},{8,12},{1,5},{5,9},{9,13},{2,6},{6,10},{10,14},{3,7},{... | collective-permute-start | bytes 313352 | tf_op jit(solution)/shard_map/ppermute | solution.py:796
  58.2 5.2 %collective-permute-done.10 = bf16[136,384]{1,0:T(8,128)(2,1)S(1)} collective-permute-done((bf16[136,384]{1,0:T(8,128)(2,1)S(1)}, bf16[136,384]{1,0:T(8,128)(2,1)S(1)}, u32[]{:S(2)}, u32[]{:S(2)}) %collective-permute-start.10) | collective-permute-done | bytes 104480 | tf_op jit(solution)/shard_map/ppermute | solution.py:797
  64.5 3.7 %back.1.back_ref = f32[128,3072]{1,0:T(8,128)S(1)} custom-call(s32[5]{0:T(128)S(1)} %stack.43.index_ref, bf16[3,128,768]{2,1,0:T(8,128)(2,1)S(1)} %get-tuple-element.76.kernel_ref, bf16[8,128,384]{2,1,0:T(8,128)(2,1)S(1)} %bitcast.27, bf16[2,128,384]{2,1,0:T(8,128)(2,1)S(1)} %pad_maximum_fusion.3.rest_1_, bf16[8,128,384]{2,1,0:T(8,128)(2,1)S(1)} %bitcast.33, ...), custom_call_target="tpu_custom_call" | custom-call | flops 2264924160 | bytes 1966080 | tf_op jit(solution)/shard_map/back/pallas_call | solution.py:321
  68.2 3.5 %collective-permute-done.12.peer_edge_ref = bf16[272,384]{1,0:T(8,128)(2,1)S(1)} collective-permute-done((bf16[272,384]{1,0:T(8,128)(2,1)S(1)}, bf16[272,384]{1,0:T(8,128)(2,1)S(1)}, u32[]{:S(2)}, u32[]{:S(2)}) %collective-permute-start.12) | collective-permute-done | bytes 208928 | tf_op jit(solution)/shard_map/ppermute | solution.py:686
  71.9 1.7 %collective-permute-done.16.side_ref = bf16[1600,128]{1,0:T(8,128)(2,1)S(1)} collective-permute-done((bf16[1600,128]{1,0:T(8,128)(2,1)S(1)}, bf16[1600,128]{1,0:T(8,128)(2,1)S(1)}, u32[]{:S(2)}, u32[]{:S(2)}) %collective-permute-start.16) | collective-permute-done | bytes 409632 | tf_op jit(solution)/shard_map/ppermute | solution.py:682
  73.6 8.2 %grads.1 = (bf16[10,256,512]{2,1,0:T(8,128)(2,1)S(1)}, f32[256,768]{1,0:T(8,128)S(1)}, bf16[256,768]{1,0:T(8,128)(2,1)S(1)}) custom-call(s32[5]{0:T(128)S(1)} %stack.43.index_ref, bf16[3,256,192]{2,1,0:T(8,128)(2,1)S(1)} %get-tuple-element.69.kernel_ref, f32[256,128]{1,0:T(8,128)S(1)} %get-tuple-element.70.gain_ref, ...), custom_call_target="tpu_custom_call" | custom-call | flops 3397386240 | bytes 5898240 | tf_op jit(solution)/shard_map/grads/pallas_call | solution.py:485
  82.0 1.6 %collective-permute-done.17.got_ref = bf16[256,768]{1,0:T(8,128)(2,1)S(1)} collective-permute-done((bf16[256,768]{1,0:T(8,128)(2,1)S(1)}, bf16[256,768]{1,0:T(8,128)(2,1)S(1)}, u32[]{:S(2)}, u32[]{:S(2)}) %collective-permute-start.17) | collective-permute-done | bytes 393248 | tf_op jit(solution)/shard_map/ppermute | solution.py:682
  84.2 1.6 %collective-permute-start.18 = (bf16[64,768]{1,0:T(8,128)(2,1)S(1)}, bf16[64,768]{1,0:T(8,128)(2,1)S(1)}, u32[]{:S(2)}, u32[]{:S(2)}) collective-permute-start(bf16[64,768]{1,0:T(8,128)(2,1)S(1)} %get-tuple-element.86), channel_id=1, source_target_pairs={{0,4},{4,0},{8,12},{12,8},{1,5},{5,1},{9,13},{13,9},{2,6},{6,2},{1... | collective-permute-start | bytes 294920 | tf_op jit(solution)/shard_map/ppermute | solution.py:690
  85.9 2.8 %collective-permute-start.20 = (bf16[64,768]{1,0:T(8,128)(2,1)S(1)}, bf16[64,768]{1,0:T(8,128)(2,1)S(1)}, u32[]{:S(2)}, u32[]{:S(2)}) collective-permute-start(bf16[64,768]{1,0:T(8,128)(2,1)S(1)} %get-tuple-element.88), channel_id=1, source_target_pairs={{0,12},{4,8},{8,4},{12,0},{1,13},{5,9},{9,5},{13,1},{2,14},{6,10},... | collective-permute-start | bytes 294920 | tf_op jit(solution)/shard_map/ppermute | solution.py:690
  88.7 3.3 %encode.1 = bf16[8,128,384]{2,1,0:T(8,128)(2,1)S(1)} custom-call(bf16[3,128,768]{2,1,0:T(8,128)(2,1)S(1)} %get-tuple-element.89.kernel_ref, bf16[10,256,512]{2,1,0:T(8,128)(2,1)S(1)} %get-tuple-element.90.hidden_ref), custom_call_target="tpu_custom_call" | custom-call | flops 2264924160 | bytes 2621440 | tf_op jit(solution)/shard_map/encode/pallas_call | solution.py:525
  92.0 4.0 %collective-permute-done.19 = bf16[64,768]{1,0:T(8,128)(2,1)S(1)} collective-permute-done((bf16[64,768]{1,0:T(8,128)(2,1)S(1)}, bf16[64,768]{1,0:T(8,128)(2,1)S(1)}, u32[]{:S(2)}, u32[]{:S(2)}) %collective-permute-start.19) | collective-permute-done | bytes 98336 | tf_op jit(solution)/shard_map/ppermute | solution.py:690
  97.2 2.5 %collective-permute-start.22 = (bf16[64,768]{1,0:T(8,128)(2,1)S(1)}, bf16[64,768]{1,0:T(8,128)(2,1)S(1)}, u32[]{:S(2)}, u32[]{:S(2)}) collective-permute-start(bf16[64,768]{1,0:T(8,128)(2,1)S(1)} %add_convert_fusion), channel_id=1, source_target_pairs={{0,8},{4,12},{8,0},{12,4},{1,9},{5,13},{9,1},{13,5},{2,10},{6,14},... | collective-permute-start | bytes 294920 | tf_op jit(solution)/shard_map/ppermute | solution.py:690
  100.5 3.0 %collective-permute-done.23 = bf16[64,768]{1,0:T(8,128)(2,1)S(1)} collective-permute-done((bf16[64,768]{1,0:T(8,128)(2,1)S(1)}, bf16[64,768]{1,0:T(8,128)(2,1)S(1)}, u32[]{:S(2)}, u32[]{:S(2)}) %collective-permute-start.23) | collective-permute-done | bytes 98336 | tf_op jit(solution)/shard_map/ppermute | solution.py:690
  103.6 4.4 %collective-permute-done.22 = bf16[64,768]{1,0:T(8,128)(2,1)S(1)} collective-permute-done((bf16[64,768]{1,0:T(8,128)(2,1)S(1)}, bf16[64,768]{1,0:T(8,128)(2,1)S(1)}, u32[]{:S(2)}, u32[]{:S(2)}) %collective-permute-start.22) | collective-permute-done | bytes 98336 | tf_op jit(solution)/shard_map/ppermute | solution.py:690
  109.8 1.8 %finish.1 = (f32[3,3,128,256]{3,2,1,0:T(8,128)}, f32[3,3,64,128]{3,2,1,0:T(8,128)}, f32[1,128]{1,0:T(1,128)}) custom-call(s32[5]{0:T(128)S(1)} %stack.43.index_ref, bf16[4,64,768]{2,1,0:T(8,128)(2,1)S(1)} %pad_maximum_fusion.1.mine_ref, bf16[4,64,768]{2,1,0:T(8,128)(2,1)S(1)} %collective-permute-done.24.other_ref), custom_call_target="tpu_custom_call" | custom-call | flops 196608 | bytes 2359296 | tf_op jit(solution)/shard_map/finish/pallas_call | solution.py:587
  (78 shorter events, 18.0 us)
Async XLA Ops:
  3.3 13.6 %collective-permute-start.2 = (bf16[3,3,200,128]{3,2,1,0:T(8,128)(2,1)S(1)}, bf16[3,3,200,128]{3,2,1,0:T(8,128)(2,1)S(1)}, u32[]{:S(2)}, u32[]{:S(2)}) collective-permute-start(bf16[3,3,200,128]{3,2,1,0:T(8,128)(2,1)S(1)} %offer.1), channel_id=1, source_target_pairs={{0,2},{2,0},{1,3},{3,1},{4,6},{6,4},{5,7},{7,5},{8,10},{10,8},{9,1... | collective-permute-start | bytes 1382408 | tf_op jit(solution)/shard_map/ppermute | solution.py:686
  6.3 10.1 %collective-permute-start = (bf16[128,384]{1,0:T(8,128)(2,1)S(1)}, bf16[128,384]{1,0:T(8,128)(2,1)S(1)}, u32[]{:S(2)}, u32[]{:S(2)}) collective-permute-start(bf16[128,384]{1,0:T(8,128)(2,1)S(1)} %get-tuple-element.56), channel_id=1, source_target_pairs={{0,4},{4,8},{8,12},{1,5},{5,9},{9,13},{2,6},{6,10},{10,14},{3,7},{... | collective-permute-start | bytes 294920 | tf_op jit(solution)/shard_map/ppermute | solution.py:726
  9.8 6.6 %collective-permute-start.1 = (bf16[128,384]{1,0:T(8,128)(2,1)S(1)}, bf16[128,384]{1,0:T(8,128)(2,1)S(1)}, u32[]{:S(2)}, u32[]{:S(2)}) collective-permute-start(bf16[128,384]{1,0:T(8,128)(2,1)S(1)} %get-tuple-element.57), channel_id=1, source_target_pairs={{4,0},{8,4},{12,8},{5,1},{9,5},{13,9},{6,2},{10,6},{14,10},{7,3},{... | collective-permute-start | bytes 294920 | tf_op jit(solution)/shard_map/ppermute | solution.py:727
  16.9 13.0 %collective-permute-start.5 = (bf16[2,72,1024]{2,1,0:T(8,128)(2,1)S(1)}, bf16[2,72,1024]{2,1,0:T(8,128)(2,1)S(1)}, u32[]{:S(2)}, u32[]{:S(2)}) collective-permute-start(bf16[2,72,1024]{2,1,0:T(8,128)(2,1)S(1)} %get-tuple-element.62), channel_id=1, source_target_pairs={{0,4},{4,0},{8,12},{12,8},{1,5},{5,1},{9,13},{13,9},{2,6},{6,2},{1... | collective-permute-start | bytes 884744 | tf_op jit(solution)/shard_map/ppermute | solution.py:690
  19.2 11.8 %collective-permute-start.14 = (bf16[2,128,384]{2,1,0:T(8,128)(2,1)S(1)}, bf16[2,128,384]{2,1,0:T(8,128)(2,1)S(1)}, u32[]{:S(2)}, u32[]{:S(2)}) collective-permute-start(bf16[2,128,384]{2,1,0:T(8,128)(2,1)S(1)} %pad_maximum_fusion.3.rest_1_), channel_id=1, source_target_pairs={{0,2},{2,0},{1,3},{3,1},{4,6},{6,4},{5,7},{7,5},{8,10},{10,8},{9,1... | collective-permute-start | bytes 589832 | tf_op jit(solution)/shard_map/ppermute | solution.py:686
  20.3 23.5 %collective-permute-start.3 = (bf16[2,72,1024]{2,1,0:T(8,128)(2,1)S(1)}, bf16[2,72,1024]{2,1,0:T(8,128)(2,1)S(1)}, u32[]{:S(2)}, u32[]{:S(2)}) collective-permute-start(bf16[2,72,1024]{2,1,0:T(8,128)(2,1)S(1)} %get-tuple-element.59), channel_id=1, source_target_pairs={{0,8},{4,12},{8,0},{12,4},{1,9},{5,13},{9,1},{13,5},{2,10},{6,14},... | collective-permute-start | bytes 884744 | tf_op jit(solution)/shard_map/ppermute | solution.py:690
  22.9 21.0 %collective-permute-start.4 = (bf16[2,72,1024]{2,1,0:T(8,128)(2,1)S(1)}, bf16[2,72,1024]{2,1,0:T(8,128)(2,1)S(1)}, u32[]{:S(2)}, u32[]{:S(2)}) collective-permute-start(bf16[2,72,1024]{2,1,0:T(8,128)(2,1)S(1)} %get-tuple-element.60), channel_id=1, source_target_pairs={{0,12},{4,8},{8,4},{12,0},{1,13},{5,9},{9,5},{13,1},{2,14},{6,10},... | collective-permute-start | bytes 884744 | tf_op jit(solution)/shard_map/ppermute | solution.py:690
  23.2 32.0 %collective-permute-start.13 = (bf16[128,8,384]{2,0,1:T(8,128)(2,1)S(1)}, bf16[128,8,384]{2,0,1:T(8,128)(2,1)S(1)}, u32[]{:S(2)}, u32[]{:S(2)}) collective-permute-start(bf16[128,8,384]{2,0,1:T(8,128)(2,1)S(1)} %copy.23), channel_id=1, source_target_pairs={{0,2},{2,0},{1,3},{3,1},{4,6},{6,4},{5,7},{7,5},{8,10},{10,8},{9,1... | collective-permute-start | bytes 2359304 | tf_op jit(solution)/shard_map/ppermute | solution.py:686
  29.9 14.5 %collective-permute-start.6 = (bf16[2,72,1024]{2,1,0:T(8,128)(2,1)S(1)}, bf16[2,72,1024]{2,1,0:T(8,128)(2,1)S(1)}, u32[]{:S(2)}, u32[]{:S(2)}) collective-permute-start(bf16[2,72,1024]{2,1,0:T(8,128)(2,1)S(1)} %pad_maximum_fusion.2), channel_id=1, source_target_pairs={{0,1},{1,0},{2,3},{3,2},{4,5},{5,4},{6,7},{7,6},{8,9},{9,8},{10,11... | collective-permute-start | bytes 884744 | tf_op jit(solution)/shard_map/ppermute | solution.py:682
  43.8 4.4 %collective-permute-start.7 = (bf16[1,72,1024]{2,1,0:T(8,128)(2,1)S(1)}, bf16[1,72,1024]{2,1,0:T(8,128)(2,1)S(1)}, u32[]{:S(2)}, u32[]{:S(2)}) collective-permute-start(bf16[1,72,1024]{2,1,0:T(8,128)(2,1)S(1)} %slice.107), channel_id=1, source_target_pairs={{0,1},{1,0},{2,3},{3,2},{4,5},{5,4},{6,7},{7,6},{8,9},{9,8},{10,11... | collective-permute-start | bytes 442376 | tf_op jit(solution)/shard_map/ppermute | solution.py:682
  43.9 4.3 %collective-permute-start.8 = (bf16[1,72,1024]{2,1,0:T(8,128)(2,1)S(1)}, bf16[1,72,1024]{2,1,0:T(8,128)(2,1)S(1)}, u32[]{:S(2)}, u32[]{:S(2)}) collective-permute-start(bf16[1,72,1024]{2,1,0:T(8,128)(2,1)S(1)} %slice.108), channel_id=1, source_target_pairs={{0,1},{1,0},{2,3},{3,2},{4,5},{5,4},{6,7},{7,6},{8,9},{9,8},{10,11... | collective-permute-start | bytes 442376 | tf_op jit(solution)/shard_map/ppermute | solution.py:682
  49.5 8.6 %collective-permute-start.9 = (bf16[136,384]{1,0:T(8,128)(2,1)S(1)}, bf16[136,384]{1,0:T(8,128)(2,1)S(1)}, u32[]{:S(2)}, u32[]{:S(2)}) collective-permute-start(bf16[136,384]{1,0:T(8,128)(2,1)S(1)} %get-tuple-element.73), channel_id=1, source_target_pairs={{0,4},{4,8},{8,12},{1,5},{5,9},{9,13},{2,6},{6,10},{10,14},{3,7},{... | collective-permute-start | bytes 313352 | tf_op jit(solution)/shard_map/ppermute | solution.py:796
  55.3 9.2 %collective-permute-start.15 = (bf16[10,256,128]{2,1,0:T(8,128)(2,1)S(1)}, bf16[10,256,128]{2,1,0:T(8,128)(2,1)S(1)}, u32[]{:S(2)}, u32[]{:S(2)}) collective-permute-start(bf16[10,256,128]{2,1,0:T(8,128)(2,1)S(1)} %maximum_maximum_fusion), channel_id=1, source_target_pairs={{0,1},{1,0},{2,3},{3,2},{4,5},{5,4},{6,7},{7,6},{8,9},{9,8},{10,11... | collective-permute-start | bytes 1966088 | tf_op jit(solution)/shard_map/ppermute | solution.py:682
  55.6 16.1 %collective-permute-start.11 = (bf16[528,384]{1,0:T(8,128)(2,1)S(1)}, bf16[528,384]{1,0:T(8,128)(2,1)S(1)}, u32[]{:S(2)}, u32[]{:S(2)}) collective-permute-start(bf16[528,384]{1,0:T(8,128)(2,1)S(1)} %get-tuple-element.75), channel_id=1, source_target_pairs={{0,2},{2,0},{1,3},{3,1},{4,6},{6,4},{5,7},{7,5},{8,10},{10,8},{9,1... | collective-permute-start | bytes 1216520 | tf_op jit(solution)/shard_map/ppermute | solution.py:686
  56.7 6.7 %collective-permute-start.10 = (bf16[136,384]{1,0:T(8,128)(2,1)S(1)}, bf16[136,384]{1,0:T(8,128)(2,1)S(1)}, u32[]{:S(2)}, u32[]{:S(2)}) collective-permute-start(bf16[136,384]{1,0:T(8,128)(2,1)S(1)} %get-tuple-element.74), channel_id=1, source_target_pairs={{4,0},{8,4},{12,8},{5,1},{9,5},{13,9},{6,2},{10,6},{14,10},{7,3},{... | collective-permute-start | bytes 313352 | tf_op jit(solution)/shard_map/ppermute | solution.py:797
  63.4 8.3 %collective-permute-start.12 = (bf16[272,384]{1,0:T(8,128)(2,1)S(1)}, bf16[272,384]{1,0:T(8,128)(2,1)S(1)}, u32[]{:S(2)}, u32[]{:S(2)}) collective-permute-start(bf16[272,384]{1,0:T(8,128)(2,1)S(1)} %constant_dynamic-update-slice_fusion.edge_ref), channel_id=1, source_target_pairs={{0,2},{2,0},{1,3},{3,1},{4,6},{6,4},{5,7},{7,5},{8,10},{10,8},{9,1... | collective-permute-start | bytes 626696 | tf_op jit(solution)/shard_map/ppermute | solution.py:686
  71.8 1.8 %collective-permute-start.16 = (bf16[1600,128]{1,0:T(8,128)(2,1)S(1)}, bf16[1600,128]{1,0:T(8,128)(2,1)S(1)}, u32[]{:S(2)}, u32[]{:S(2)}) collective-permute-start(bf16[1600,128]{1,0:T(8,128)(2,1)S(1)} %pad_maximum_fusion), channel_id=1, source_target_pairs={{0,1},{1,0},{2,3},{3,2},{4,5},{5,4},{6,7},{7,6},{8,9},{9,8},{10,11... | collective-permute-start | bytes 1228808 | tf_op jit(solution)/shard_map/ppermute | solution.py:682
  81.8 1.8 %collective-permute-start.17 = (bf16[256,768]{1,0:T(8,128)(2,1)S(1)}, bf16[256,768]{1,0:T(8,128)(2,1)S(1)}, u32[]{:S(2)}, u32[]{:S(2)}) collective-permute-start(bf16[256,768]{1,0:T(8,128)(2,1)S(1)} %get-tuple-element.84), channel_id=1, source_target_pairs={{0,1},{1,0},{2,3},{3,2},{4,5},{5,4},{6,7},{7,6},{8,9},{9,8},{10,11... | collective-permute-start | bytes 1179656 | tf_op jit(solution)/shard_map/ppermute | solution.py:682
  84.2 7.8 %collective-permute-start.18 = (bf16[64,768]{1,0:T(8,128)(2,1)S(1)}, bf16[64,768]{1,0:T(8,128)(2,1)S(1)}, u32[]{:S(2)}, u32[]{:S(2)}) collective-permute-start(bf16[64,768]{1,0:T(8,128)(2,1)S(1)} %get-tuple-element.86), channel_id=1, source_target_pairs={{0,4},{4,0},{8,12},{12,8},{1,5},{5,1},{9,13},{13,9},{2,6},{6,2},{1... | collective-permute-start | bytes 294920 | tf_op jit(solution)/shard_map/ppermute | solution.py:690
  85.9 10.1 %collective-permute-start.19 = (bf16[64,768]{1,0:T(8,128)(2,1)S(1)}, bf16[64,768]{1,0:T(8,128)(2,1)S(1)}, u32[]{:S(2)}, u32[]{:S(2)}) collective-permute-start(bf16[64,768]{1,0:T(8,128)(2,1)S(1)} %get-tuple-element.87), channel_id=1, source_target_pairs={{0,8},{4,12},{8,0},{12,4},{1,9},{5,13},{9,1},{13,5},{2,10},{6,14},... | collective-permute-start | bytes 294920 | tf_op jit(solution)/shard_map/ppermute | solution.py:690
  85.9 10.1 %collective-permute-start.20 = (bf16[64,768]{1,0:T(8,128)(2,1)S(1)}, bf16[64,768]{1,0:T(8,128)(2,1)S(1)}, u32[]{:S(2)}, u32[]{:S(2)}) collective-permute-start(bf16[64,768]{1,0:T(8,128)(2,1)S(1)} %get-tuple-element.88), channel_id=1, source_target_pairs={{0,12},{4,8},{8,4},{12,0},{1,13},{5,9},{9,5},{13,1},{2,14},{6,10},... | collective-permute-start | bytes 294920 | tf_op jit(solution)/shard_map/ppermute | solution.py:690
  96.1 7.5 %collective-permute-start.23 = (bf16[64,768]{1,0:T(8,128)(2,1)S(1)}, bf16[64,768]{1,0:T(8,128)(2,1)S(1)}, u32[]{:S(2)}, u32[]{:S(2)}) collective-permute-start(bf16[64,768]{1,0:T(8,128)(2,1)S(1)} %add_convert_fusion), channel_id=1, source_target_pairs={{0,12},{4,8},{8,4},{12,0},{1,13},{5,9},{9,5},{13,1},{2,14},{6,10},... | collective-permute-start | bytes 294920 | tf_op jit(solution)/shard_map/ppermute | solution.py:690
  97.2 10.8 %collective-permute-start.22 = (bf16[64,768]{1,0:T(8,128)(2,1)S(1)}, bf16[64,768]{1,0:T(8,128)(2,1)S(1)}, u32[]{:S(2)}, u32[]{:S(2)}) collective-permute-start(bf16[64,768]{1,0:T(8,128)(2,1)S(1)} %add_convert_fusion), channel_id=1, source_target_pairs={{0,8},{4,12},{8,0},{12,4},{1,9},{5,13},{9,1},{13,5},{2,10},{6,14},... | collective-permute-start | bytes 294920 | tf_op jit(solution)/shard_map/ppermute | solution.py:690
  99.7 8.3 %collective-permute-start.21 = (bf16[64,768]{1,0:T(8,128)(2,1)S(1)}, bf16[64,768]{1,0:T(8,128)(2,1)S(1)}, u32[]{:S(2)}, u32[]{:S(2)}) collective-permute-start(bf16[64,768]{1,0:T(8,128)(2,1)S(1)} %add_convert_fusion), channel_id=1, source_target_pairs={{0,4},{4,0},{8,12},{12,8},{1,5},{5,1},{9,13},{13,9},{2,6},{6,2},{1... | collective-permute-start | bytes 294920 | tf_op jit(solution)/shard_map/ppermute | solution.py:690
  (9 other events, 61.5 us)
